TPU v7x, 256 devices: a whole 4x4x8 slice. The times are simulated.
256 devices in a mesh: dp: 128 (over x, z, y_hi, core), shard: 2 (over y_lo).
Axes of the slice: x: 4, y: 4 (y_hi: 2, y_lo: 2; y = y_hi * 2 + y_lo), z: 8, core: 2. Of those that a mesh axis runs over, the one named last changes fastest.
Arguments:
- clips: bfloat16 [512, 5, 256, 512], P(('dp', 'shard')), may hold values from -16 to 16
- code_grad: bfloat16 [512, 5, 256, 18], P(('dp', 'shard')), may hold values from -6 to 6
- conv_weight: bfloat16 [1536, 512], replicated, may hold values from -0.15625 to 0.15625
- norm_gain: float32 [512], replicated, may hold values from 0.5 to 1.5
- proj_weight: bfloat16 [512, 18], replicated, may hold values from -0.25 to 0.25
- code_bias: float32 [18], replicated, may hold values from -1 to 1
- rotation: float32 [18, 18], replicated, may hold values from -1.5 to 1.5
- first_moment: float32 [1536, 512], P('shard'), may hold values from -4 to 4
- second_moment: float32 [1536, 512], P('shard'), may hold values from 0.01 to 0.3
Outputs:
- new_weight: bfloat16 [1536, 512], replicated
- first_moment_out: float32 [1536, 512], P('shard')
- second_moment_out: float32 [1536, 512], P('shard')
- input_grad: bfloat16 [512, 5, 256, 512], P(('dp', 'shard'))
- loss: float32 [], replicated
All inputs are finite; a program needn't handle non-finite values.
Results may differ from a plain program's by a relative error of at most 0.014.
Values may be sent and summed in bfloat16 or wider, within the bound.
No kernel may reach another device: no remote copies, remote signals or barrier semaphores. Data moves between devices by JAX's collectives and lax.ppermute only.
A program may use at most 128 MiB of HBM per device.

v0:
```python
import jax
import jax.numpy as jnp
from jax import lax
from jax.sharding import Mesh
from jax.sharding import PartitionSpec as P

DP = ("dp_0", "dp_1", "dp_2", "dp_3")
DP_SHARD = ("dp_0", "dp_1", "dp_2", "dp_3", "shard")


def one_axis_at_a_time(shard, axes):
    for axis in axes:
        shard = lax.psum(shard, axis)
    return shard


def split_up(shard, dim, count):
    before, after = (shard.shape[:dim], shard.shape[dim + 1 :])
    return jnp.moveaxis(shard.reshape(*before, count, -1, *after), dim, 0)


def sum_at_owner(shard, axis, dim):
    count = lax.axis_size(axis)
    tiles = lax.all_to_all(split_up(shard, dim, count), axis, 0, 0, tiled=True)
    return jnp.sum(tiles.astype(jnp.float32), axis=0)


def sum_at_owner_2(shard, axis, dim):
    count = lax.axis_size(axis)
    tiles = lax.all_to_all(split_up(shard, dim, count), axis, 0, 0, tiled=True)
    return jnp.sum(tiles, axis=0)


def sum_by_axis(shard, axes, dim):
    far, near = axes
    tiles = split_up(shard, dim, lax.axis_size(far))
    nearer = sum_at_owner_2(tiles, near, dim + 1)
    arrived = lax.all_to_all(nearer, far, split_axis=0, concat_axis=0, tiled=True)
    return arrived.sum(axis=0)


def filled_up(lines, count):
    spare = -len(lines) % count
    return jnp.pad(lines, [(0, spare)] + [(0, 0)] * (lines.ndim - 1))


def copy_for_each(shard, axis):
    copies = jnp.broadcast_to(shard, (lax.axis_size(axis), *shard.shape))
    return lax.all_to_all(copies, axis, split_axis=0, concat_axis=0, tiled=True)


def joined_along(tiles, dim):
    shape = list(tiles.shape[1:])
    shape[dim] *= tiles.shape[0]
    return jnp.moveaxis(tiles, 0, dim).reshape(shape)


def gathered_by_axis(shard, axes, dim):
    far, near = axes
    tiles = copy_for_each(copy_for_each(shard, far), near)
    return joined_along(tiles.swapaxes(0, 1).reshape(-1, *shard.shape), dim)


def total_of(shard, axes):
    lines = shard.reshape(-1, shard.shape[-1])
    own = sum_by_axis(filled_up(lines, lax.axis_size(axes[0]) * lax.axis_size(axes[1])), axes, 0)
    whole = gathered_by_axis(own, axes, 0)
    return whole[: len(lines)].reshape(shard.shape)


def collect(shard, axis, dim):
    tiles = copy_for_each(shard, axis)
    return joined_along(tiles, dim)


def stacked_taps(block):
    batch, frames, sites, width = block.shape
    padded = jnp.pad(block, ((0, 0), (2, 0), (0, 0), (0, 0)))
    taps = [padded[:, 2 - k : 2 - k + frames] for k in range(3)]
    return jnp.concatenate(taps, axis=3).reshape(batch * frames * sites, 3 * width)


def forward(block, conv_weight, norm_gain, proj_weight, code_bias, rotation):
    width = block.shape[3]
    stacked = stacked_taps(block)
    hidden = block.reshape(-1, width).astype(jnp.float32) + jnp.dot(
        stacked, conv_weight, preferred_element_type=jnp.float32
    )
    inverse = lax.rsqrt(jnp.mean(hidden * hidden, axis=1, keepdims=True) + 1e-06)
    unit = hidden * inverse
    normed = (unit * norm_gain).astype(jnp.bfloat16)
    latent = jnp.dot(normed, proj_weight, preferred_element_type=jnp.float32) + code_bias
    rotated = jnp.dot(latent, rotation, precision=lax.Precision.HIGHEST)
    codes = jnp.tanh(rotated)
    return (stacked, inverse, unit, rotated, codes)


def token_terms(rotated, codes, cotangent):
    probs = (1.0 + codes) / 2.0
    logit = 2.0 * rotated
    entropy = jax.nn.softplus(logit) - logit * probs
    token_loss = cotangent * codes + 0.25 * (rotated - codes) ** 2 + 0.1 * entropy
    return (probs, logit, jnp.sum(token_loss))


def backward(
    block, cotangent, conv_weight, norm_gain, proj_weight, rotation, saved, lean, clip_count
):
    stacked, inverse, unit, rotated, codes = saved
    probs = (1.0 + codes) / 2.0
    logit = 2.0 * rotated
    slope = 1.0 - codes * codes
    d_rot = (
        cotangent * slope
        + 0.5 * (rotated - codes) * (1.0 - slope)
        - 0.2 * logit * probs * (1.0 - probs)
        - 0.05 * slope * lean
    ) / clip_count
    d_lat = jnp.dot(d_rot, rotation.T, precision=lax.Precision.HIGHEST)
    d_norm = jnp.dot(d_lat, proj_weight.astype(jnp.float32).T, precision=lax.Precision.HIGHEST)
    scaled = d_norm * norm_gain
    d_hidden = inverse * (scaled - unit * jnp.mean(scaled * unit, axis=1, keepdims=True))
    d_conv = d_hidden.astype(jnp.bfloat16)
    batch, frames, sites, width = block.shape
    d_taps = lax.dot_general(
        d_conv, conv_weight, (((1,), (1,)), ((), ())), preferred_element_type=jnp.float32
    )
    d_taps = d_taps.reshape(batch, frames, sites, 3, width)
    padded = jnp.pad(d_taps, ((0, 0), (0, 2), (0, 0), (0, 0), (0, 0)))
    back = (
        padded[:, 0:frames, :, 0, :]
        + padded[:, 1 : frames + 1, :, 1, :]
        + padded[:, 2 : frames + 2, :, 2, :]
    )
    input_grad = (d_hidden.reshape(batch, frames, sites, width) + back).astype(jnp.bfloat16)
    return (stacked, d_conv, input_grad)


def on_device(
    clips,
    code_grad,
    conv_weight,
    norm_gain,
    proj_weight,
    code_bias,
    rotation,
    first_moment,
    second_moment,
):
    bit_count = code_grad.shape[3]
    devices = lax.axis_size(DP) * lax.axis_size("shard")
    clip_count = clips.shape[0] * devices
    token_count = clips.shape[0] * clips.shape[1] * clips.shape[2] * devices
    cotangent = code_grad.reshape(-1, bit_count).astype(jnp.float32)
    saved = forward(clips, conv_weight, norm_gain, proj_weight, code_bias, rotation)
    probs, logit, loss_part = token_terms(saved[3], saved[4], cotangent)
    bit_total, loss_total = (
        one_axis_at_a_time(jnp.sum(probs, axis=0), DP_SHARD),
        one_axis_at_a_time(loss_part, DP_SHARD),
    )
    bit_mean = bit_total / token_count
    code_entropy = jnp.sum(
        -bit_mean * jnp.log(bit_mean) - (1.0 - bit_mean) * jnp.log(1.0 - bit_mean)
    )
    loss = loss_total / token_count - 0.1 * code_entropy
    lean = jnp.log((1.0 - bit_mean) / bit_mean)
    stacked, d_conv, input_grad = backward(
        clips, cotangent, conv_weight, norm_gain, proj_weight, rotation, saved, lean, clip_count
    )
    owned_rows = first_moment.shape[0]
    group_part = sum_at_owner(
        lax.dot_general(
            stacked, d_conv, (((0,), (0,)), ((), ())), preferred_element_type=jnp.float32
        ).astype(jnp.bfloat16),
        "shard",
        0,
    )
    grad_owned = total_of(group_part, (("dp_0", "dp_1", "dp_2"), "dp_3"))
    first_out = 0.9 * first_moment + 0.1 * grad_owned
    second_out = 0.99 * second_moment + 0.01 * grad_owned * grad_owned
    owner = lax.axis_index("shard")
    own_weight = lax.dynamic_slice_in_dim(conv_weight, owner * owned_rows, owned_rows, 0).astype(
        jnp.float32
    )
    stepped = (own_weight - 0.001 * first_out / (jnp.sqrt(second_out) + 1e-08)).astype(jnp.bfloat16)
    new_weight = collect(stepped, "shard", 0)
    return (new_weight, first_out, second_out, input_grad, loss)


def solution(mesh):
    finer = Mesh(
        mesh.devices.reshape(4, 8, 2, 2, mesh.shape["shard"]),
        ("dp_0", "dp_1", "dp_2", "dp_3", "shard"),
    )
    in_specs = (
        P(DP_SHARD, None, None, None),
        P(DP_SHARD, None, None, None),
        P(),
        P(),
        P(),
        P(),
        P(),
        P("shard", None),
        P("shard", None),
    )
    out_specs = (P(), P("shard", None), P("shard", None), P(DP_SHARD, None, None, None), P())
    return jax.shard_map(
        on_device, mesh=finer, in_specs=in_specs, out_specs=out_specs, check_vma=False
    )
```

profile of v0, /device:TPU:1, one launch (start us, length us, event | category | flops | bytes accessed | tf_op | source)
XLA Modules:
  0.0 238.2 jit_solution(2002389347079798934)
XLA Ops:
  0.6 0.0 copy-start
  0.6 0.9 copy.25
  1.6 0.1 reshape.54
  1.6 0.0 copy-start.4
  1.7 2.7 %pad_slice_fusion.3 = (bf16[2,5,256,512]{3,2,1,0:T(8,128)(2,1)S(1)}, bf16[2,5,256,512]{3,2,1,0:T(8,128)(2,1)S(1)}) fusion(bf16[2,5,256,512]{3,2,1,0:T(8,128)(2,1)} %param.9), kind=kLoop, calls=%fused_computation.14 | loop fusion | bytes 7864320 | tf_op jit(solution)/shard_map/slice | solution.py:79
  4.3 0.2 copy-done.4
  4.5 0.8 pad_maximum_fusion
  5.4 0.5 copy-done.6
  5.9 4.6 %multiply_reduce_fusion.1 = (f32[2560]{0:T(1024)S(1)}, f32[2560,512]{1,0:T(8,128)S(1)}) fusion(bf16[2560,1536]{1,0:T(8,128)(2,1)S(1)} %bitcast.29, bf16[1536,512]{1,0:T(8,128)(2,1)S(1)} %copy-done.6, bf16[2560,512]{1,0:T(8,128)(2,1)S(1)} %bitcast.27), kind=kOutput, calls=%fused_computation.11 | convolution fusion | flops 4031772160 | bytes 17311744 | tf_op jit(solution)/shard_map/dot_general | solution.py:86
  10.6 0.0 copy-start.10
  10.6 1.0 convolution_add_fusion
  11.6 1.2 copy-done.3
  12.9 1.3 fusion.13
  14.1 9.9 %all-reduce.3 = (f32[18]{0:T(128)S(1)}, f32[]{:T(128)}) all-reduce(f32[18]{0:T(128)S(1)} %get-tuple-element.6, f32[]{:T(128)} %get-tuple-element.5), channel_id=1, replica_groups=mesh['dp_0'=4,'dp_1'=8,'dp_2'=2,'dp_3'=2,'shard'=2] {'dp_0'}, use_global_device_ids=true, to_apply=%region_2.3 | all-reduce | flops 19 | bytes 152 | tf_op jit(solution)/shard_map/psum | solution.py:13
  24.0 16.9 %all-reduce.2 = (f32[18]{0:T(128)S(1)}, f32[]{:T(128)}) all-reduce(f32[18]{0:T(128)S(1)} %get-tuple-element.9, f32[]{:T(128)} %get-tuple-element.10), channel_id=1, replica_groups=mesh['dp_0'=4,'dp_1'=8,'dp_2'=2,'dp_3'=2,'shard'=2] {'dp_1'}, use_global_device_ids=true, to_apply=%region_3.4 | all-reduce | flops 19 | bytes 152 | tf_op jit(solution)/shard_map/psum | solution.py:13
  40.9 5.9 %all-reduce.6 = (f32[18]{0:T(128)S(1)}, f32[]{:T(128)}) all-reduce(f32[18]{0:T(128)S(1)} %get-tuple-element.7, f32[]{:T(128)} %get-tuple-element.8), channel_id=1, replica_groups=mesh['dp_0'=4,'dp_1'=8,'dp_2'=2,'dp_3'=2,'shard'=2] {'dp_2'}, use_global_device_ids=true, to_apply=%region_4.5 | all-reduce | flops 19 | bytes 152 | tf_op jit(solution)/shard_map/psum | solution.py:13
  46.8 10.3 %all-reduce.5 = (f32[18]{0:T(128)S(1)}, f32[]{:T(128)}) all-reduce(f32[18]{0:T(128)S(1)} %get-tuple-element.15, f32[]{:T(128)} %get-tuple-element.16), channel_id=1, replica_groups=mesh['dp_0'=4,'dp_1'=8,'dp_2'=2,'dp_3'=2,'shard'=2] {'dp_3'}, use_global_device_ids=true, to_apply=%region_5.6 | all-reduce | flops 19 | bytes 152 | tf_op jit(solution)/shard_map/psum | solution.py:13
  57.1 4.6 %all-reduce.4 = (f32[18]{0:T(128)S(1)}, f32[]{:T(128)}) all-reduce(f32[18]{0:T(128)S(1)} %get-tuple-element.13, f32[]{:T(128)} %get-tuple-element.14), channel_id=1, replica_groups=mesh['dp_0'=4,'dp_1'=8,'dp_2'=2,'dp_3'=2,'shard'=2] {'shard'}, use_global_device_ids=true, to_apply=%region_6.7 | all-reduce | flops 19 | bytes 152 | tf_op jit(solution)/shard_map/psum | solution.py:13
  61.7 0.6 fusion.46
  62.3 0.5 fusion.20
  62.9 5.8 %multiply_reduce_fusion = (f32[2560]{0:T(1024)S(1)}, f32[2560,512]{1,0:T(8,128)S(1)}) fusion(f32[2560,512]{1,0:T(8,128)} %copy-done.3, f32[2560]{0:T(1024)S(1)} %add_rsqrt_fusion, f32[512]{0:T(512)S(1)} %copy-done.8, f32[2560,18]{0,1:T(8,128)S(1)} %fusion.20, bf16[512,18]{0,1:T(8,128)(2,1)S(1)} %copy-done), kind=kOutput, calls=%fused_computation.9 | convolution fusion | flops 288355840 | bytes 10711040 | tf_op jit(solution)/shard_map/dot_general | solution.py:120
  68.7 1.6 subtract_multiply_fusion
  70.3 0.4 slice-done.3
  70.8 4.3 %convolution_convert_fusion = bf16[1536,512]{1,0:T(8,128)(2,1)S(1)} fusion(bf16[2560,1536]{1,0:T(8,128)(2,1)S(1)} %bitcast.32, f32[2560,512]{1,0:T(8,128)S(1)} %subtract_multiply_fusion), kind=kOutput, calls=%fused_computation.17 | convolution fusion | flops 4028628992 | bytes 14680064 | tf_op jit(solution)/shard_map/dot_general | solution.py:172
  75.1 20.2 %all_to_all.30 = bf16[2,768,512]{2,1,0:T(8,128)(2,1)S(1)} all-to-all(bf16[2,768,512]{2,1,0:T(8,128)(2,1)S(1)} %bitcast.35), channel_id=1, replica_groups=mesh['dp_0'=4,'dp_1'=8,'dp_2'=2,'dp_3'=2,'shard'=2] {'shard'}, dimensions={0} | all-to-all | bytes 3145728 | tf_op jit(solution)/shard_map/all_to_all | solution.py:24
  95.2 1.5 convert_reduce_fusion
  96.7 1.5 reshape_reshape.6
  98.2 0.9 copy.26
  99.1 7.1 %all_to_all.31 = f32[2,64,6,512]{3,1,2,0:T(8,128)S(1)} all-to-all(f32[2,64,6,512]{3,1,2,0:T(8,128)S(1)} %copy.26), channel_id=1, replica_groups=mesh['dp_0'=4,'dp_1'=8,'dp_2'=2,'dp_3'=2,'shard'=2] {'dp_3'}, dimensions={0} | all-to-all | bytes 3145728 | tf_op jit(solution)/shard_map/all_to_all | solution.py:30
  106.2 0.2 reduce_sum.76
  106.4 0.5 copy.27
  106.9 36.2 %all_to_all.32 = f32[64,6,512]{2,1,0:T(8,128)S(1)} all-to-all(f32[64,6,512]{2,1,0:T(8,128)S(1)} %copy.27), channel_id=1, replica_groups=mesh['dp_0'=4,'dp_1'=8,'dp_2'=2,'dp_3'=2,'shard'=2] {'dp_0','dp_1','dp_2'}, dimensions={0} | all-to-all | bytes 1572864 | tf_op jit(solution)/shard_map/all_to_all | solution.py:38
  143.1 0.1 reduce_sum.77
  143.2 1.1 broadcast_in_dim.6
  144.3 6.9 %all-to-all-start.3 = ((f32[64,6,512]{2,1,0:T(8,128)}), f32[64,6,512]{2,1,0:T(8,128)S(1)}, u32[]{:S(2)}, u32[]{:S(2)}) async-start(f32[64,6,512]{2,1,0:T(8,128)} %broadcast_in_dim.6), calls=%async_computation.3 | async-start | bytes 2097152 | tf_op jit(solution)/shard_map/all_to_all | solution.py:49
  151.3 10.3 %fusion.6 = f32[2560,1536]{1,0:T(8,128)} fusion(bf16[1536,512]{1,0:T(8,128)(2,1)S(1)} %copy-done.7, f32[2560,512]{1,0:T(8,128)} %copy-done.2), kind=kOutput, calls=%fused_computation.24 | convolution fusion | flops 4027842560 | bytes 22544384 | tf_op jit(solution)/shard_map/dot_general | solution.py:125
  161.5 26.1 %reshape.52 = f32[2,5,256,3,512]{4,3,2,1,0:T(4,128)} reshape(f32[2560,1536]{1,0:T(8,128)} %fusion.6) | data formatting | bytes 31457280 | tf_op jit(solution)/shard_map/reshape | solution.py:128
  187.6 0.5 copy.28
  188.1 0.2 broadcast_in_dim.7
  188.3 6.0 %all_to_all.33 = f32[2,64,6,512]{3,1,2,0:T(8,128)S(1)} all-to-all(f32[2,64,6,512]{3,1,2,0:T(8,128)S(1)} %broadcast_in_dim.7), channel_id=1, replica_groups=mesh['dp_0'=4,'dp_1'=8,'dp_2'=2,'dp_3'=2,'shard'=2] {'dp_3'}, dimensions={0} | all-to-all | bytes 3145728 | tf_op jit(solution)/shard_map/all_to_all | solution.py:49
  194.2 0.9 copy.29
  195.2 1.4 reshape_reshape.7
  196.6 5.3 %subtract_convert_fusion = (bf16[768,512]{1,0:T(8,128)(2,1)S(1)}, f32[768,512]{1,0:T(8,128)}, f32[768,512]{1,0:T(8,128)}) fusion(bf16[1536,512]{1,0:T(8,128)(2,1)} %param.11, s32[]{:T(128)S(6)} %select_n.7, f32[768,512]{1,0:T(8,128)} %reshape_reshape.7, f32[768,512]{1,0:T(8,128)} %param.16, f32[768,512]{1,0:T(8,128)} %param.17), kind=kLoop, calls=%fused_computation.22 | loop fusion | flops 5111808 | bytes 9437188 | tf_op jit(solution)/shard_map/convert_element_type | solution.py:185
  201.9 1.2 broadcast_in_dim.8
  203.1 3.7 %all-to-all-start.5 = ((bf16[2,768,512]{2,1,0:T(8,128)(2,1)}), bf16[2,768,512]{2,1,0:T(8,128)(2,1)S(1)}, u32[]{:S(2)}, u32[]{:S(2)}) async-start(bf16[2,768,512]{2,1,0:T(8,128)(2,1)} %broadcast_in_dim.8), calls=%async_computation.5 | async-start | bytes 3145728 | tf_op jit(solution)/shard_map/all_to_all | solution.py:49
  206.8 21.4 %fusion.1 = f32[2,5,256,1,512]{4,3,2,1,0:T(1,128)} fusion(f32[2,5,256,3,512]{4,3,2,1,0:T(4,128)} %reshape.52), kind=kLoop, calls=%fused_computation.4 | loop fusion | flops 2621440 | bytes 31457280 | tf_op jit(solution)/shard_map/add | solution.py:131
  229.5 6.5 %fusion.2 = bf16[2,5,256,512]{3,2,1,0:T(8,128)(2,1)} fusion(f32[2,5,256,512]{3,2,1,0:T(8,128)} %bitcast.24, f32[2,5,256,1,512]{4,3,2,1,0:T(1,128)} %fusion.1), kind=kLoop, calls=%fused_computation.6 | loop fusion | flops 2621440 | bytes 13107200 | tf_op jit(solution)/shard_map/convert_element_type | solution.py:135
  235.9 1.1 copy.33
  (29 shorter events, 0.1 us)
Async XLA Ops:
  0.6 10.0 %copy-start = (bf16[512,18]{0,1:T(8,128)(2,1)S(1)}, bf16[512,18]{0,1:T(8,128)(2,1)}, u32[]{:S(2)}) copy-start(bf16[512,18]{0,1:T(8,128)(2,1)} %param.13) | copy-start | bytes 55300
  1.6 2.8 %copy-start.4 = (bf16[2,5,256,512]{3,2,1,0:T(8,128)(2,1)S(1)}, bf16[2,5,256,512]{3,2,1,0:T(8,128)(2,1)}, u32[]{:S(2)}) copy-start(bf16[2,5,256,512]{3,2,1,0:T(8,128)(2,1)} %param.9) | copy-start | bytes 7864324
  4.5 1.4 copy-start.6
  5.4 5.2 %copy-start.5 = (bf16[2,5,256,1536]{3,2,1,0:T(8,128)(2,1)}, bf16[2,5,256,1536]{3,2,1,0:T(8,128)(2,1)S(1)}, u32[]{:S(2)}) copy-start(bf16[2,5,256,1536]{3,2,1,0:T(8,128)(2,1)S(1)} %pad_maximum_fusion) | copy-start | bytes 23592964
  5.9 4.7 %copy-start.8 = (f32[512]{0:T(512)S(1)}, f32[512]{0:T(512)}, u32[]{:S(2)}) copy-start(f32[512]{0:T(512)} %param.12) | copy-start | bytes 6148
  5.9 4.7 %copy-start.9 = (f32[18]{0:T(128)S(1)}, f32[18]{0:T(128)}, u32[]{:S(2)}) copy-start(f32[18]{0:T(128)} %param.14) | copy-start | bytes 220
  10.6 2.3 copy-start.3
  10.6 2.3 copy-start.10
  62.3 6.4 %slice-start = ((s8[5242880]{0:T(1024)(128)(4,1)}), s8[4194304]{0:T(1024)(128)(4,1)S(1)}, s32[]{:S(2)}) async-start(s8[5242880]{0:T(1024)(128)(4,1)} %bitcast.25), calls=%async_computation.6 | async-start | bytes 8388608
  62.8 5.9 %slice-start.1 = ((s8[5242880]{0:T(1024)(128)(4,1)}), s8[1048576]{0:T(1024)(128)(4,1)S(1)}, s32[]{:S(2)}) async-start(s8[5242880]{0:T(1024)(128)(4,1)} %bitcast.25), calls=%async_computation.7 | async-start | bytes 2097152
  62.9 7.5 %slice-start.2 = ((s8[7864320]{0:T(1024)(128)(4,1)}), s8[4194304]{0:T(1024)(128)(4,1)S(1)}, s32[]{:S(2)}) async-start(s8[7864320]{0:T(1024)(128)(4,1)} %bitcast.30), calls=%async_computation.8 | async-start | bytes 8388608
  68.7 2.0 slice-start.3
  70.8 4.3 %copy-start.2 = (f32[2560,512]{1,0:T(8,128)}, f32[2560,512]{1,0:T(8,128)S(1)}, u32[]{:S(2)}) copy-start(f32[2560,512]{1,0:T(8,128)S(1)} %subtract_multiply_fusion) | copy-start | bytes 15728644
  143.1 8.1 %copy-start.7 = (bf16[1536,512]{1,0:T(8,128)(2,1)S(1)}, bf16[1536,512]{1,0:T(8,128)(2,1)}, u32[]{:S(2)}) copy-start(bf16[1536,512]{1,0:T(8,128)(2,1)} %param.11) | copy-start | bytes 4718596
  144.3 43.3 %all-to-all-start.3 = ((f32[64,6,512]{2,1,0:T(8,128)}), f32[64,6,512]{2,1,0:T(8,128)S(1)}, u32[]{:S(2)}, u32[]{:S(2)}) async-start(f32[64,6,512]{2,1,0:T(8,128)} %broadcast_in_dim.6), calls=%async_computation.3 | async-start | bytes 2097152 | tf_op jit(solution)/shard_map/all_to_all | solution.py:49
  203.1 32.8 %all-to-all-start.5 = ((bf16[2,768,512]{2,1,0:T(8,128)(2,1)}), bf16[2,768,512]{2,1,0:T(8,128)(2,1)S(1)}, u32[]{:S(2)}, u32[]{:S(2)}) async-start(bf16[2,768,512]{2,1,0:T(8,128)(2,1)} %broadcast_in_dim.8), calls=%async_computation.5 | async-start | bytes 3145728 | tf_op jit(solution)/shard_map/all_to_all | solution.py:49
  229.5 7.6 %copy-start.1 = (bf16[512,18]{0,1:T(8,128)(2,1)S(1)}, bf16[512,18]{0,1:T(8,128)(2,1)}, u32[]{:S(2)}) copy-start(bf16[512,18]{0,1:T(8,128)(2,1)} %param.13) | copy-start | bytes 55300
where the time goes:
time: 240 us; the launch traced here: 238 us
  blocking collectives  117 us (49%)
  local copies, waits for them, and re-layouts  41.5 us (17%)
  other arithmetic  38 us (16%)
  matrix products  27.8 us (12%)
  starting transfers between devices  10.6 us (4%)
  between operations  3.36 us (1%)
    psum x5, blocking collectives, one_axis_at_a_time(): shard = lax.psum(shard, axis)  47.5 us
    all_to_all x1, blocking collectives, sum_by_axis(): lax.all_to_all(nearer, far, split_axis=0, concat_axis=0, tiled=True)  36.2 us
    reshape x1, local copies, waits for them, and re-layouts, backward(): d_taps = d_taps.reshape(batch, frames, sites, 3, width)  26.1 us
    add x1, other arithmetic, backward(): padded[:, 0:frames, :, 0, :] + padded[:, 1:frames + 1, :, 1, :]  21.4 us
    all_to_all x1, blocking collectives, sum_at_owner(): tiles = lax.all_to_all(split_up(shard, dim, count), axis, 0, 0, tiled=True)  20.2 us
    all_to_all x2, starting transfers between devices, copy_for_each(): return lax.all_to_all(copies, axis, split_axis=0, concat_axis=0, tiled=True)  10.6 us
    dot_general x1, matrix products, backward(): lax.dot_general(d_conv, conv_weight, (((1,), (1,)), ((), ())), preferred_...  10.3 us
    all_to_all x1, blocking collectives, sum_at_owner_2(): tiles = lax.all_to_all(split_up(shard, dim, count), axis, 0, 0, tiled=True)  7.14 us
  transfers between devices with their start and end apart: 2, of which 0 were waited for; matrix products, arithmetic and copies ran while one was open for 27% of the time, Pallas kernels for 0%

commit v1 on v0

v1 whole, which is shorter than its diff:
```python
import functools

import jax
import jax.numpy as jnp
from jax import lax
from jax.experimental import pallas as pl
from jax.experimental.pallas import tpu as pltpu
from jax.sharding import Mesh
from jax.sharding import PartitionSpec as P

ALL = ("x", "z", "yh", "core", "yl")
PLANE = ("x", "yh", "yl")
ROWS = 24
LANES = 128
F32 = jnp.float32
BF16 = jnp.bfloat16
NT = (((1,), (1,)), ((), ()))
TN = (((0,), (0,)), ((), ()))
EXACT = lax.Precision.HIGHEST


def hi_lo(value):
    high = value.astype(BF16)
    return high, (value - high.astype(F32)).astype(BF16)


def diagonal(row, count):
    grid = jnp.broadcast_to(row, (count, row.shape[1]))
    at = lax.broadcasted_iota(jnp.int32, grid.shape, 0)
    to = lax.broadcasted_iota(jnp.int32, grid.shape, 1)
    return jnp.sum(jnp.where(at == to, grid, 0.0), axis=1, keepdims=True)


def lane_groups(value):
    part = value[:, :LANES]
    for g in range(1, value.shape[1] // LANES):
        part = part + value[:, g * LANES : (g + 1) * LANES]
    return part


def forward_kernel(
    x_ref, w_ref, proj_ref, gain_ref, code_bias_ref, rotation_ref, cg_ref,
    h_ref, xt_ref, base_ref, slope_ref, q_ref, ag_out, stat_ref,
    map_ref, bias_ref, ag_ref, sum_ref,
):
    clip = pl.program_id(0)
    frames, sites, width = x_ref.shape[1:]
    bits = rotation_ref.shape[0]

    @pl.when(clip == 0)
    def _():
        map_ref[...] = jnp.zeros_like(map_ref)
        bias_ref[...] = jnp.zeros_like(bias_ref)
        map_ref[:bits, :] = (
            lax.dot_general(
                rotation_ref[...], proj_ref[...].astype(F32), TN, precision=EXACT, preferred_element_type=F32
            )
            * gain_ref[...]
        )
        row = jnp.dot(code_bias_ref[...], rotation_ref[...], precision=EXACT, preferred_element_type=F32)
        bias_ref[:bits, :] = jnp.broadcast_to(diagonal(row, bits), (bits, LANES))
        high, low = hi_lo(map_ref[...])
        ag_ref[...] = jnp.concatenate([high, low], axis=0)
        ag_out[...] = ag_ref[...]
        sum_ref[...] = jnp.zeros_like(sum_ref)

    ones = jnp.ones((8, LANES), F32)
    bias = bias_ref[:, :1]
    total_p = jnp.zeros((ROWS, LANES), F32)
    total_l = jnp.zeros((ROWS, LANES), F32)
    for f in range(frames):
        taps = min(f, 2) + 1
        block = x_ref[0, f]
        stacked = jnp.concatenate([x_ref[0, f - k] for k in range(taps)], axis=1)
        hidden = block.astype(F32) + jnp.dot(
            stacked, w_ref[: taps * width, :], preferred_element_type=F32
        )
        rounded = hidden.astype(BF16)
        h_ref[0, f] = rounded
        xt_ref[0, :, f * sites : (f + 1) * sites] = block.T
        mean = (
            lax.dot_general(ones, lane_groups(hidden * hidden), NT, preferred_element_type=F32)[:1] / width
        )
        inv = lax.rsqrt(mean + 1e-06)
        both = lax.dot_general(ag_ref[...], rounded, NT, preferred_element_type=F32)
        raw = both[:ROWS] + both[ROWS:]
        rotated = raw * inv + bias
        cotangent = cg_ref[0, f].astype(F32)
        small = jnp.exp(-2.0 * jnp.abs(rotated))
        size = (1.0 - small) / (1.0 + small)
        codes = jnp.where(rotated < 0.0, -size, size)
        probs = 0.5 + 0.5 * codes
        logit = 2.0 * rotated
        gap = rotated - codes
        entropy = jnp.maximum(logit, 0.0) + jnp.log(1.0 + small) - logit * probs
        total_p = total_p + lane_groups(probs)
        total_l = total_l + lane_groups(cotangent * codes + 0.25 * gap * gap + 0.1 * entropy)
        slope = 1.0 - codes * codes
        base = cotangent * slope + 0.5 * gap * (1.0 - slope) - 0.1 * rotated * slope
        base_ref[0, f] = base * inv
        slope_ref[0, f] = slope * inv
        q_ref[0, f] = raw * (inv * inv) / width
    sum_ref[:ROWS] += total_p
    sum_ref[ROWS:] += total_l

    @pl.when(clip == pl.num_programs(0) - 1)
    def _():
        ones = jnp.ones((8, LANES), F32)
        probs = sum_ref[:ROWS]
        at = lax.broadcasted_iota(jnp.int32, probs.shape, 0)
        losses = jnp.sum(jnp.where(at < bits, sum_ref[ROWS:], 0.0), axis=0, keepdims=True)
        table = jnp.where(at < bits, probs, jnp.where(at == bits, losses, 0.0))
        filled = jnp.concatenate([table, jnp.zeros((LANES - ROWS, LANES), F32)], axis=0)
        row = lax.dot_general(ones, filled, NT, precision=EXACT, preferred_element_type=F32)
        stat_ref[...] = row[:1]


def backward_kernel(
    bits, clip_count, token_count, core_ref,
    h_ref, xt_ref, base_ref, slope_ref, q_ref, ag_ref, part_ref,
    d_ref, mine_ref, theirs_ref, loss_ref,
    acc_ref, lean_ref, right_ref,
):
    clip = pl.program_id(0)
    frames, sites, width = h_ref.shape[1:]

    @pl.when(clip == 0)
    def _():
        total = jnp.sum(part_ref[...], axis=0, keepdims=True)
        lane = lax.broadcasted_iota(jnp.int32, total.shape, 1)
        mean = jnp.where(lane < bits, total / token_count, 0.5)
        lean = jnp.log((1.0 - mean) / mean)
        entropy = -mean * jnp.log(mean) - (1.0 - mean) * jnp.log(1.0 - mean)
        term = jnp.where(
            lane < bits, -0.1 * entropy, jnp.where(lane == bits, total / token_count, 0.0)
        )
        loss_ref[...] = jnp.sum(term, axis=1, keepdims=True)
        lean_ref[...] = jnp.broadcast_to(diagonal(lean, ROWS) * 0.05, (ROWS, LANES))
        high = ag_ref[:ROWS]
        low = ag_ref[ROWS:]
        right_ref[:, :width] = jnp.concatenate(
            [high, high, low, jnp.zeros((LANES - 3 * ROWS, width), BF16)], axis=0
        )
        at = lax.broadcasted_iota(jnp.int32, (LANES, LANES), 0)
        right_ref[:, width:] = jnp.where((at >= 3 * ROWS) & (at < 5 * ROWS), 1.0, 0.0).astype(BF16)

    lean = lean_ref[:, :1]
    for f in range(frames):
        u = (base_ref[0, f] - slope_ref[0, f] * lean) * (1.0 / clip_count)
        u_hi, u_lo = hi_lo(u)
        q_hi, q_lo = hi_lo(u * q_ref[0, f])
        spare = jnp.zeros((LANES - 5 * ROWS, sites), BF16)
        left = jnp.concatenate([u_hi, u_lo, u_hi, q_hi, q_lo, spare], axis=0)
        out = lax.dot_general(left, right_ref[...], TN, preferred_element_type=F32)
        centre = jnp.concatenate([out[:, width:]] * (width // LANES), axis=1)
        d_hidden = out[:, :width] - centre * h_ref[0, f].astype(F32)
        d_ref[0, f] = d_hidden.astype(BF16)

    def store(target, column, k, total):
        block = target.shape[1]
        for piece in range(3 * width // block):
            start = piece * block - k * width
            low, high = max(start, 0), min(start + block, width)
            if low >= high:
                continue
            half, quarter = divmod(piece, 4)
            slot = column * 8 + quarter * 2 + half
            target[slot, low - start : high - start, :] = total[low:high]

    for k in range(3):
        count = (frames - k) * sites
        d_part = d_ref[0, k:].reshape(count, width)
        part = jnp.dot(xt_ref[0, :, :count], d_part, preferred_element_type=F32)
        rows = pl.ds(k * width, width)

        @pl.when(clip == 0)
        def _():
            acc_ref[rows, :] = part

        @pl.when(clip != 0)
        def _():
            total = (acc_ref[rows, :] + part).astype(BF16)
            pieces = [total[:, g * LANES : (g + 1) * LANES] for g in range(width // LANES)]

            @pl.when(core_ref[0] == 0)
            def _():
                for c in range(2):
                    store(mine_ref, c, k, pieces[c])
                    store(theirs_ref, c, k, pieces[2 + c])

            @pl.when(core_ref[0] != 0)
            def _():
                for c in range(2):
                    store(mine_ref, c, k, pieces[2 + c])
                    store(theirs_ref, c, k, pieces[c])


def input_kernel(d_ref, w_ref, out_ref):
    frames, sites, width = d_ref.shape[1:]
    for f in range(frames):
        total = d_ref[0, f].astype(F32)
        for k in range(min(3, frames - f)):
            total = total + lax.dot_general(
                d_ref[0, f + k], w_ref[k * width : (k + 1) * width, :], NT, preferred_element_type=F32
            )
        out_ref[0, f] = total.astype(BF16)


def updated(weight, first, second, grad):
    first_out = 0.9 * first + 0.1 * grad
    second_out = 0.99 * second + 0.01 * grad * grad
    new = (weight - 0.001 * first_out / (jnp.sqrt(second_out) + 1e-08)).astype(BF16)
    return new, first_out, second_out


def block_kernel(place_ref, parts_ref, w_ref, m_ref, v_ref, send_ref):
    grad = jnp.sum(parts_ref[...].astype(F32), axis=0).astype(BF16)
    new, _, _ = updated(w_ref[...].astype(F32), m_ref[...], v_ref[...], grad.astype(F32))
    for half in range(2):

        @pl.when(place_ref[0] == half)
        def _():
            for d in range(send_ref.shape[0]):
                send_ref[d] = grad if d % 2 == half else new


def final_kernel(place_ref, near_ref, far_ref, w_ref, m_ref, v_ref, new_ref, first_ref, second_ref):
    step = pl.program_id(0)
    rows = m_ref.shape[0]
    block = near_ref.shape[1]

    def write(source, half):
        for quarter in range(rows // block):
            part = pl.ds(quarter * block, block)
            here = pl.ds(half * rows + quarter * block, block)
            there = pl.ds((1 - half) * rows + quarter * block, block)
            grad = source[quarter * 2 + half].astype(F32)
            new, first_out, second_out = updated(w_ref[here, :].astype(F32), m_ref[part, :], v_ref[part, :], grad)
            new_ref[here, :] = new
            first_ref[part, :] = first_out
            second_ref[part, :] = second_out
            new_ref[there, :] = source[quarter * 2 + 1 - half]

    near = (step // 2) == place_ref[1]
    for half in range(2):

        @pl.when((place_ref[0] == half) & near)
        def _():
            write(near_ref, half)

        @pl.when((place_ref[0] == half) & jnp.logical_not(near))
        def _():
            write(far_ref, half)


def per_clip(shape):
    return pl.BlockSpec((1, *shape[1:]), lambda c, *_: (c,) + (0,) * (len(shape) - 1))


def whole(shape):
    return pl.BlockSpec(shape, lambda *_: (0,) * len(shape))


def shaped(outs):
    return [jax.ShapeDtypeStruct(s, t) for s, t in outs]


def run_forward(clips, weight, proj, gain, code_bias, rotation, cotangent):
    batch, frames, sites, width = clips.shape
    rows = (batch, frames, ROWS, sites)
    outs = [
        (clips.shape, BF16), ((batch, width, frames * sites), BF16),
        (rows, F32), (rows, F32), (rows, F32), ((2 * ROWS, width), BF16), ((1, LANES), F32),
    ]
    shared = (weight, proj, gain, code_bias, rotation)
    return pl.pallas_call(
        forward_kernel,
        grid=(batch,),
        in_specs=[per_clip(clips.shape)] + [whole(a.shape) for a in shared] + [per_clip(cotangent.shape)],
        out_specs=[per_clip(s) for s, _ in outs[:5]] + [whole(s) for s, _ in outs[5:]],
        out_shape=shaped(outs),
        scratch_shapes=[
            pltpu.VMEM((ROWS, width), F32), pltpu.VMEM((ROWS, LANES), F32),
            pltpu.VMEM((2 * ROWS, width), BF16), pltpu.VMEM((2 * ROWS, LANES), F32),
        ],
        name="forward",
    )(clips, *shared, cotangent)


def run_backward(bits, clip_count, token_count, core, saved, ag, parts, row_count):
    hidden = saved[0]
    batch, frames, sites, width = hidden.shape
    block = (16, row_count // 8, LANES)
    outs = [(hidden.shape, BF16), (block, BF16), (block, BF16), ((1, 1), F32)]
    return pl.pallas_call(
        functools.partial(backward_kernel, bits, clip_count, token_count),
        grid_spec=pltpu.PrefetchScalarGridSpec(
            num_scalar_prefetch=1,
            grid=(batch,),
            in_specs=[per_clip(a.shape) for a in saved] + [whole(ag.shape), whole(parts.shape)],
            out_specs=[per_clip(hidden.shape)] + [whole(s) for s, _ in outs[1:]],
            scratch_shapes=[
                pltpu.VMEM((row_count, width), F32), pltpu.VMEM((ROWS, LANES), F32),
                pltpu.VMEM((LANES, width + LANES), BF16),
            ],
        ),
        out_shape=shaped(outs),
        name="backward",
    )(core, *saved, ag, parts)


def run_input(d_conv, weight):
    return pl.pallas_call(
        input_kernel,
        grid=(d_conv.shape[0],),
        in_specs=[per_clip(d_conv.shape), whole(weight.shape)],
        out_specs=per_clip(d_conv.shape),
        out_shape=jax.ShapeDtypeStruct(d_conv.shape, BF16),
        name="input_grad",
    )(d_conv, weight)


def run_block(place, parts, weight, first, second):
    block = parts.shape[1:]
    send = (16, *block)
    return pl.pallas_call(
        block_kernel,
        grid_spec=pltpu.PrefetchScalarGridSpec(
            num_scalar_prefetch=1,
            grid=(1,),
            in_specs=[
                whole(parts.shape),
                pl.BlockSpec(block, lambda i, p: (p[0] * 4 + p[2], p[3])),
                pl.BlockSpec(block, lambda i, p: (p[2], p[3])),
                pl.BlockSpec(block, lambda i, p: (p[2], p[3])),
            ],
            out_specs=whole(send),
        ),
        out_shape=jax.ShapeDtypeStruct(send, BF16),
        name="owner_step",
    )(place, parts, weight, first, second)


def run_final(place, near, far, weight, first, second):
    total, width = weight.shape
    owned = first.shape[0]
    side = near.shape[0] // 2
    column = lambda rows: pl.BlockSpec((rows, LANES), lambda i, p: (0, i))
    part = pl.BlockSpec((side, *near.shape[1:]), lambda i, p: (i % 2, 0, 0))
    return pl.pallas_call(
        final_kernel,
        grid_spec=pltpu.PrefetchScalarGridSpec(
            num_scalar_prefetch=1,
            grid=(width // LANES,),
            in_specs=[part, part, column(total), column(owned), column(owned)],
            out_specs=[column(total), column(owned), column(owned)],
        ),
        out_shape=shaped([((total, width), BF16), ((owned, width), F32), ((owned, width), F32)]),
        name="final_step",
    )(place, near, far, weight, first, second)


def spread(value, axes):
    return lax.all_to_all(value, axes, 0, 0, tiled=True)


def swapped(value):
    return lax.ppermute(value, "core", [(0, 1), (1, 0)])


def on_device(clips, code_grad, conv_weight, norm_gain, proj_weight, code_bias, rotation, first_moment, second_moment):
    bits = code_grad.shape[3]
    devices = lax.axis_size(ALL)
    batch, frames, sites, width = clips.shape
    clip_count = batch * devices
    token_count = clip_count * frames * sites
    half, core = lax.axis_index("yl"), lax.axis_index("core")
    x_at, y_at = lax.axis_index("x"), lax.axis_index("yh")
    place = jnp.stack([half, core, (x_at % 2) * 2 + y_at, core * 2 + x_at // 2]).astype(jnp.int32)
    cotangent = jnp.pad(code_grad.transpose(0, 1, 3, 2), ((0, 0), (0, 0), (0, ROWS - bits), (0, 0)))
    *saved, ag, stats = run_forward(
        clips, conv_weight, proj_weight.T, norm_gain[None, :], code_bias[None, :], rotation, cotangent
    )
    parts = spread(jnp.broadcast_to(stats, (devices, LANES)), ALL)
    d_conv, mine, theirs, loss = run_backward(
        bits, clip_count, token_count, place[1:2], saved, ag, parts, conv_weight.shape[0]
    )
    chip = (mine.astype(F32) + swapped(theirs).astype(F32)).astype(BF16)
    plane = spread(chip, PLANE)
    input_grad = run_input(d_conv, conv_weight)
    column = jnp.sum(plane.astype(F32), axis=0).astype(BF16)
    tower = spread(jnp.broadcast_to(column, (lax.axis_size("z"), *column.shape)), "z")
    near = spread(run_block(place, tower, conv_weight, first_moment, second_moment), PLANE)
    far = swapped(near)
    new_weight, first_out, second_out = run_final(place, near, far, conv_weight, first_moment, second_moment)
    return new_weight, first_out, second_out, input_grad, loss[0, 0]


def solution(mesh):
    finer = Mesh(mesh.devices.reshape(4, 8, 2, 2, mesh.shape["shard"]), ALL)
    split = P(ALL, None, None, None)
    in_specs = (split, split, P(), P(), P(), P(), P(), P("yl", None), P("yl", None))
    out_specs = (P(), P("yl", None), P("yl", None), split, P())
    return jax.shard_map(on_device, mesh=finer, in_specs=in_specs, out_specs=out_specs, check_vma=False)
```

time: 240 us -> 128 us (0.53)
  blocking collectives: 117 us -> 31.1 us
  Pallas kernels: 0 us -> 36.5 us
  other arithmetic: 38 us -> 2.05 us
  local copies, waits for them, and re-layouts: 41.5 us -> 6.03 us
  matrix products: 27.8 us -> 0 us
  waiting for transfers between devices: 0.01 us -> 26.8 us
  starting transfers between devices: 10.6 us -> 24.1 us
  between operations: 3.36 us -> 0.71 us
    psum x5 -> x0, blocking collectives: 47.5 us -> none  [one_axis_at_a_time(): shard = lax.psum(shard, axis)]
    all_to_all x4 -> x2, blocking collectives: 69.4 us -> 31.1 us  [spread(): return lax.all_to_all(value, axes, 0, 0, tiled=True)]
    pallas_call x0 -> x5, Pallas kernels: none -> 36.5 us  [the longest x1 10.3 us: run_forward(): pl.pallas_call(forward_kernel, grid=(batch,), in_specs=[per_clip(clips.sh...]
    dot_general x7 -> x0, matrix products: 27.8 us -> none  [the longest x1 10.3 us: backward(): lax.dot_general(d_conv, conv_weight, (((1,), (1,)), ((), ())), preferred_...]
    reshape x1 -> x0, local copies, waits for them, and re-layouts: 26.1 us -> none  [backward(): d_taps = d_taps.reshape(batch, frames, sites, 3, width)]
    all_to_all x2, waiting for transfers between devices: 0.01 us -> 24.7 us  [spread(): return lax.all_to_all(value, axes, 0, 0, tiled=True)]
    add x1 -> x0, other arithmetic: 21.4 us -> none  [backward(): padded[:, 0:frames, :, 0, :] + padded[:, 1:frames + 1, :, 1, :]]
    convert_element_type x2 -> x1, other arithmetic: 11.8 us -> 1.34 us  [on_device(): chip = (mine.astype(F32) + swapped(theirs).astype(F32)).astype(BF16)]
  transfers between devices with their start and end apart: 2 -> 4, of which waited for: 0 -> 3; matrix products, arithmetic and copies ran while one was open for 27% -> 0% of each run, Pallas kernels for 0% -> 5%
where the time goes in v1:
time: 128 us; the launch traced here: 127 us
  Pallas kernels  36.5 us (29%)
  blocking collectives  31.1 us (24%)
  waiting for transfers between devices  26.8 us (21%)
  starting transfers between devices  24.1 us (19%)
  local copies, waits for them, and re-layouts  6.03 us (5%)
  other arithmetic  2.05 us (2%)
    all_to_all x2, blocking collectives, spread(): return lax.all_to_all(value, axes, 0, 0, tiled=True)  31.1 us
    all_to_all x2, waiting for transfers between devices, spread(): return lax.all_to_all(value, axes, 0, 0, tiled=True)  24.7 us
    all_to_all x2, starting transfers between devices, spread(): return lax.all_to_all(value, axes, 0, 0, tiled=True)  19.1 us
    pallas_call x1, Pallas kernels, run_forward(): pl.pallas_call(forward_kernel, grid=(batch,), in_specs=[per_clip(clips.sh...  10.3 us
    pallas_call x1, Pallas kernels, run_backward(): pl.pallas_call(functools.partial(backward_kernel, bits, clip_count, token...  10.1 us
    pallas_call x1, Pallas kernels, run_final(): pl.pallas_call(final_kernel, grid_spec=pltpu.PrefetchScalarGridSpec(num_s...  6.81 us
    pallas_call x1, Pallas kernels, run_input(): pl.pallas_call(input_kernel, grid=(d_conv.shape[0],), in_specs=[per_clip(...  6.53 us
    ppermute x2, starting transfers between devices, swapped(): return lax.ppermute(value, 'core', [(0, 1), (1, 0)])  5.03 us
  transfers between devices with their start and end apart: 4, of which 3 were waited for; matrix products, arithmetic and copies ran while one was open for 0% of the time, Pallas kernels for 5%

profile of v1, /device:TPU:1, one launch (start us, length us, event | category | flops | bytes accessed | tf_op | source)
XLA Modules:
  0.0 127.4 jit_solution(17113656132567187834)
XLA Ops:
  0.6 0.9 copy.17
  1.5 0.7 pad.4.cg_ref
  2.2 10.3 %forward.1 = (bf16[2,5,256,512]{3,2,1,0:T(8,128)(2,1)}, bf16[2,512,1280]{2,1,0:T(8,128)(2,1)}, f32[2,5,24,256]{3,2,1,0:T(8,128)}, f32[2,5,24,256]{3,2,1,0:T(8,12...) custom-call(bf16[2,5,256,512]{3,2,1,0:T(8,128)(2,1)} %x_ref.1, bf16[1536,512]{1,0:T(8,128)(2,1)} %w_ref.7, ...), custom_call_target="tpu_custom_call" | custom-call | tf_op jit(solution)/shard_map/forward/pallas_call | solution.py:276
  12.5 1.4 %broadcast_in_dim.16 = f32[256,1,128]{2,1,0:T(1,128)} broadcast(f32[128]{0:T(128)} %bitcast.18), dimensions={2} | broadcast | bytes 131584 | tf_op jit(solution)/shard_map/broadcast_in_dim | solution.py:384
  13.9 15.6 %all-to-all-start = ((f32[256,1,128]{2,1,0:T(1,128)}), f32[256,1,128]{2,1,0:T(1,128)S(1)}, u32[]{:S(2)}, u32[]{:S(2)}) async-start(f32[256,1,128]{2,1,0:T(1,128)} %broadcast_in_dim.16), calls=%async_computation | async-start | bytes 262144 | tf_op jit(solution)/shard_map/all_to_all | solution.py:364
  29.5 13.0 %all-to-all-done = f32[256,1,128]{2,1,0:T(1,128)S(1)} async-done(((f32[256,1,128]{2,1,0:T(1,128)}), f32[256,1,128]{2,1,0:T(1,128)S(1)}, u32[]{:S(2)}, u32[]{:S(2)}) %all-to-all-start) | async-done | bytes 131104 | tf_op jit(solution)/shard_map/all_to_all | solution.py:364
  42.5 0.0 copy-start.3
  42.5 0.7 copy-done.3
  43.2 10.1 %backward.1 = (bf16[2,5,256,512]{3,2,1,0:T(8,128)(2,1)}, bf16[16,192,128]{2,1,0:T(8,128)(2,1)}, bf16[16,192,128]{2,1,0:T(8,128)(2,1)}, f32[1,1]{1,0:T(1,128)}) custom-call(s32[1]{0:T(128)} %bitcast.1.core_ref, bf16[2,5,256,512]{3,2,1,0:T(8,128)(2,1)} %get-tuple-element.19.h_ref, bf16[2,512,1280]{2,1,0:T(8,128)(2,1)} %get-tuple-element.20.xt_ref, ...), custom_call_target="tpu_custom_call" | custom-call | tf_op jit(solution)/shard_map/backward/pallas_call | solution.py:295
  53.3 0.6 collective-permute-start
  53.9 2.1 %collective-permute-done = bf16[16,192,128]{2,1,0:T(8,128)(2,1)S(1)} collective-permute-done((bf16[16,192,128]{2,1,0:T(8,128)(2,1)}, bf16[16,192,128]{2,1,0:T(8,128)(2,1)S(1)}, u32[]{:S(2)}, u32[]{:S(2)}) %collective-permute-start) | collective-permute-done | bytes 786464 | tf_op jit(solution)/shard_map/ppermute | solution.py:368
  56.0 1.3 %add_convert_fusion = bf16[16,192,128]{2,1,0:T(8,128)(2,1)S(1)} fusion(bf16[16,192,128]{2,1,0:T(8,128)(2,1)S(1)} %collective-permute-done, bf16[16,192,128]{2,1,0:T(8,128)(2,1)} %get-tuple-element.26), kind=kLoop, calls=%fused_computation | loop fusion | flops 1572864 | bytes 2359296 | tf_op jit(solution)/shard_map/convert_element_type | solution.py:388
  57.4 16.4 %all_to_all.23 = bf16[16,192,128]{2,1,0:T(8,128)(2,1)S(1)} all-to-all(bf16[16,192,128]{2,1,0:T(8,128)(2,1)S(1)} %add_convert_fusion), channel_id=1, replica_groups=mesh['x'=4,'z'=8,'yh'=2,'core'=2,'yl'=2] {'x','yh','yl'}, dimensions={0} | all-to-all | bytes 1572864 | tf_op jit(solution)/shard_map/all_to_all | solution.py:364
  73.7 0.1 reduce_sum.12
  73.9 0.8 broadcast_in_dim.17
  74.7 3.5 %all-to-all-start.2 = ((bf16[8,192,128]{2,1,0:T(8,128)(2,1)}), bf16[8,192,128]{2,1,0:T(8,128)(2,1)S(1)}, u32[]{:S(2)}, u32[]{:S(2)}) async-start(bf16[8,192,128]{2,1,0:T(8,128)(2,1)} %broadcast_in_dim.17), calls=%async_computation.2 | async-start | bytes 786432 | tf_op jit(solution)/shard_map/all_to_all | solution.py:364
  78.1 0.6 pad_add_fusion.place_ref
  78.7 11.7 %all-to-all-done.2.parts_ref = bf16[8,192,128]{2,1,0:T(8,128)(2,1)S(1)} async-done(((bf16[8,192,128]{2,1,0:T(8,128)(2,1)}), bf16[8,192,128]{2,1,0:T(8,128)(2,1)S(1)}, u32[]{:S(2)}, u32[]{:S(2)}) %all-to-all-start.2) | async-done | bytes 393248 | tf_op jit(solution)/shard_map/all_to_all | solution.py:364
  90.5 0.0 copy-start.1
  90.5 0.7 copy-done.1
  91.2 2.8 %owner_step.1 = bf16[16,192,128]{2,1,0:T(8,128)(2,1)} custom-call(s32[4]{0:T(128)} %pad_add_fusion.place_ref, bf16[8,192,128]{2,1,0:T(8,128)(2,1)} %copy-done.1, bf16[1536,512]{1,0:T(8,128)(2,1)} %w_ref.7, f32[768,512]{1,0:T(8,128)} %m_ref.3, f32[768,512]{1,0:T(8,128)} %v_ref.3), custom_call_target="tpu_custom_call" | custom-call | tf_op jit(solution)/shard_map/owner_step/pallas_call | solution.py:326
  94.0 14.7 %all_to_all.24.near_ref = bf16[16,192,128]{2,1,0:T(8,128)(2,1)S(1)} all-to-all(bf16[16,192,128]{2,1,0:T(8,128)(2,1)} %owner_step.1), channel_id=1, replica_groups=mesh['x'=4,'z'=8,'yh'=2,'core'=2,'yl'=2] {'x','yh','yl'}, dimensions={0} | all-to-all | bytes 1572864 | tf_op jit(solution)/shard_map/all_to_all | solution.py:364
  108.7 0.0 copy-start
  108.7 4.4 %collective-permute-start.1 = (bf16[16,192,128]{2,1,0:T(8,128)(2,1)S(1)}, bf16[16,192,128]{2,1,0:T(8,128)(2,1)S(1)}, u32[]{:S(2)}, u32[]{:S(2)}) collective-permute-start(bf16[16,192,128]{2,1,0:T(8,128)(2,1)S(1)} %all_to_all.24.near_ref), channel_id=1, source_target_pairs={{0,2},{2,0},{1,3},{3,1},{4,6},{6,4},{5,7},{7,5},{8,10},{10,8},{9,1... | collective-permute-start | bytes 2359304 | tf_op jit(solution)/shard_map/ppermute | solution.py:368
  113.1 6.5 %input_grad.1 = bf16[2,5,256,512]{3,2,1,0:T(8,128)(2,1)} custom-call(bf16[2,5,256,512]{3,2,1,0:T(8,128)(2,1)} %get-tuple-element.31.d_ref, bf16[1536,512]{1,0:T(8,128)(2,1)} %w_ref.7), custom_call_target="tpu_custom_call" | custom-call | tf_op jit(solution)/shard_map/input_grad/pallas_call | solution.py:313
  119.7 0.0 copy-done
  119.7 0.0 collective-permute-done.1.far_ref
  119.7 0.0 copy-start.2
  119.7 0.9 copy-done.2
  120.5 6.8 %final_step.1 = (bf16[1536,512]{1,0:T(8,128)(2,1)}, f32[768,512]{1,0:T(8,128)}, f32[768,512]{1,0:T(8,128)}) custom-call(s32[4]{0:T(128)} %pad_add_fusion.place_ref, bf16[16,192,128]{2,1,0:T(8,128)(2,1)} %copy-done, bf16[16,192,128]{2,1,0:T(8,128)(2,1)} %copy-done.2, bf16[1536,512]{1,0:T(8,128)(2,1)} %w_ref.7, f32[768,512]{1,0:T(8,128)} %m_ref.3, ...), custom_call_target="tpu_custom_call" | custom-call | tf_op jit(solution)/shard_map/final_step/pallas_call | solution.py:350
Async XLA Ops:
  13.9 28.6 %all-to-all-start = ((f32[256,1,128]{2,1,0:T(1,128)}), f32[256,1,128]{2,1,0:T(1,128)S(1)}, u32[]{:S(2)}, u32[]{:S(2)}) async-start(f32[256,1,128]{2,1,0:T(1,128)} %broadcast_in_dim.16), calls=%async_computation | async-start | bytes 262144 | tf_op jit(solution)/shard_map/all_to_all | solution.py:364
  42.5 0.7 copy-start.3
  53.3 2.7 %collective-permute-start = (bf16[16,192,128]{2,1,0:T(8,128)(2,1)}, bf16[16,192,128]{2,1,0:T(8,128)(2,1)S(1)}, u32[]{:S(2)}, u32[]{:S(2)}) collective-permute-start(bf16[16,192,128]{2,1,0:T(8,128)(2,1)} %get-tuple-element.27), channel_id=1, source_target_pairs={{0,2},{2,0},{1,3},{3,1},{4,6},{6,4},{5,7},{7,5},{8,10},{10,8},{9,1... | collective-permute-start | bytes 2359304 | tf_op jit(solution)/shard_map/ppermute | solution.py:368
  74.7 15.8 %all-to-all-start.2 = ((bf16[8,192,128]{2,1,0:T(8,128)(2,1)}), bf16[8,192,128]{2,1,0:T(8,128)(2,1)S(1)}, u32[]{:S(2)}, u32[]{:S(2)}) async-start(bf16[8,192,128]{2,1,0:T(8,128)(2,1)} %broadcast_in_dim.17), calls=%async_computation.2 | async-start | bytes 786432 | tf_op jit(solution)/shard_map/all_to_all | solution.py:364
  90.5 0.7 copy-start.1
  108.7 10.9 %copy-start = (bf16[16,192,128]{2,1,0:T(8,128)(2,1)}, bf16[16,192,128]{2,1,0:T(8,128)(2,1)S(1)}, u32[]{:S(2)}) copy-start(bf16[16,192,128]{2,1,0:T(8,128)(2,1)S(1)} %all_to_all.24.near_ref) | copy-start | bytes 2359300
  108.7 10.9 %collective-permute-start.1 = (bf16[16,192,128]{2,1,0:T(8,128)(2,1)S(1)}, bf16[16,192,128]{2,1,0:T(8,128)(2,1)S(1)}, u32[]{:S(2)}, u32[]{:S(2)}) collective-permute-start(bf16[16,192,128]{2,1,0:T(8,128)(2,1)S(1)} %all_to_all.24.near_ref), channel_id=1, source_target_pairs={{0,2},{2,0},{1,3},{3,1},{4,6},{6,4},{5,7},{7,5},{8,10},{10,8},{9,1... | collective-permute-start | bytes 2359304 | tf_op jit(solution)/shard_map/ppermute | solution.py:368
  119.7 0.9 copy-start.2

commit v2 on v1

v2 whole, which is shorter than its diff:
```python
import functools

import jax
import jax.numpy as jnp
from jax import lax
from jax.experimental import pallas as pl
from jax.experimental.pallas import tpu as pltpu
from jax.sharding import Mesh
from jax.sharding import PartitionSpec as P

ALL = ("x", "z", "yh", "core", "yl")
PLANE = ("x", "yh", "yl")
ROWS = 24
ROW_STEP = 512
COL_STEP = 512
GRAD_STEP = 512
LANES = 128
F32 = jnp.float32
BF16 = jnp.bfloat16
NT = (((1,), (1,)), ((), ()))
TN = (((0,), (0,)), ((), ()))
EXACT = lax.Precision.HIGHEST


def hi_lo(value):
    high = value.astype(BF16)
    return high, (value - high.astype(F32)).astype(BF16)


def diagonal(row, count):
    grid = jnp.broadcast_to(row, (count, row.shape[1]))
    at = lax.broadcasted_iota(jnp.int32, grid.shape, 0)
    to = lax.broadcasted_iota(jnp.int32, grid.shape, 1)
    return jnp.sum(jnp.where(at == to, grid, 0.0), axis=1, keepdims=True)


def lane_groups(value):
    part = value[:, :LANES]
    for g in range(1, value.shape[1] // LANES):
        part = part + value[:, g * LANES : (g + 1) * LANES]
    return part


def copy(source, target, sem):
    return pltpu.make_async_copy(source, target, sem)


def forward_kernel(
    _, x_hbm, w_hbm, proj_hbm, gain_hbm, code_bias_hbm, rotation_hbm, cg_hbm,
    h_ref, xt_hbm, base_ref, slope_ref, q_ref, ag_ref, stat_ref,
    x_ref, w_ref, map_ref, cot_ref, xt_ref, proj_ref, gain_ref, code_bias_ref, rotation_ref, cg_ref,
    x_sem, w_sem, xt_sem, small_sem,
):
    batch, frames, sites, width = x_hbm.shape
    bits = rotation_ref.shape[0]
    tokens = batch * sites
    pairs = [
        (proj_hbm, proj_ref), (gain_hbm, gain_ref), (code_bias_hbm, code_bias_ref),
        (rotation_hbm, rotation_ref), (cg_hbm, cg_ref),
    ]
    small_copies = [copy(a, b, small_sem.at[i]) for i, (a, b) in enumerate(pairs)]
    for one in small_copies:
        one.start()
    x_copies = [
        [copy(x_hbm.at[c, f], x_ref.at[f, pl.ds(c * sites, sites)], x_sem.at[f, c]) for c in range(batch)]
        for f in range(frames)
    ]
    w_copies = [
        copy(w_hbm.at[pl.ds(k * width, width)], w_ref.at[pl.ds(k * width, width)], w_sem.at[k]) for k in range(3)
    ]
    for f in range(frames):
        for one in x_copies[f]:
            one.start()
        if f < 3:
            w_copies[f].start()
    map_ref[...] = jnp.zeros_like(map_ref)
    cot_ref[...] = jnp.zeros_like(cot_ref)
    for one in small_copies:
        one.wait()
    map_ref[:bits, :] = (
        lax.dot_general(
            rotation_ref[...], proj_ref[...].astype(F32), TN, precision=EXACT, preferred_element_type=F32
        )
        * gain_ref[...]
    )
    row = jnp.dot(code_bias_ref[...], rotation_ref[...], precision=EXACT, preferred_element_type=F32)
    bias = diagonal(jnp.concatenate([row, jnp.zeros((1, LANES - bits), F32)], axis=1), ROWS)
    high, low = hi_lo(map_ref[...])
    ag_ref[...] = jnp.concatenate([high, low], axis=0)
    ones = jnp.ones((8, LANES), F32)
    total_p = jnp.zeros((ROWS, LANES), F32)
    total_l = jnp.zeros((ROWS, LANES), F32)
    def multiply(f):
        means = []
        for start in range(0, tokens, ROW_STEP):
            rows = slice(start, start + ROW_STEP)
            part = jnp.zeros((ROW_STEP, LANES), F32)
            for first in range(0, width, COL_STEP):
                cols = slice(first, first + COL_STEP)
                hidden = x_ref[f, rows, cols].astype(F32)
                for k in range(min(f, 2) + 1):
                    hidden = hidden + jnp.dot(
                        x_ref[f - k, rows, :], w_ref[k * width : (k + 1) * width, cols], preferred_element_type=F32
                    )
                h_ref[f, rows, cols] = hidden.astype(BF16)
                part = part + lane_groups(hidden * hidden)
            means.append(lax.dot_general(ones, part, NT, preferred_element_type=F32)[:1] / width)
        both = lax.dot_general(ag_ref[...], h_ref[f], NT, preferred_element_type=F32)
        return jnp.concatenate(means, axis=1), both[:ROWS] + both[ROWS:]

    def decide(f, mean, raw):
        inv = lax.rsqrt(mean + 1e-06)
        rotated = raw * inv + bias
        cot_ref[f, :bits, :sites] = cg_ref[f, :, 0, :].astype(F32)
        cot_ref[f, :bits, sites:] = cg_ref[f, :, 1, :].astype(F32)
        cotangent = cot_ref[f]
        small = jnp.exp(-2.0 * jnp.abs(rotated))
        size = (1.0 - small) / (1.0 + small)
        codes = jnp.where(rotated < 0.0, -size, size)
        probs = 0.5 + 0.5 * codes
        logit = 2.0 * rotated
        gap = rotated - codes
        entropy = jnp.maximum(logit, 0.0) + jnp.log(1.0 + small) - logit * probs
        slope = 1.0 - codes * codes
        base = cotangent * slope + 0.5 * gap * (1.0 - slope) - 0.1 * rotated * slope
        base_ref[f] = base * inv
        slope_ref[f] = slope * inv
        q_ref[f] = raw * (inv * inv) / width
        xt_ref[:, f * tokens : (f + 1) * tokens] = x_ref[f].T
        return lane_groups(probs), lane_groups(cotangent * codes + 0.25 * gap * gap + 0.1 * entropy)

    def arrive(f):
        for one in x_copies[f]:
            one.wait()
        if f < 3:
            w_copies[f].wait()

    waiting = []
    for f in range(frames):
        arrive(f)
        ready = multiply(f)
        for earlier in waiting:
            sums = decide(*earlier)
            total_p = total_p + sums[0]
            total_l = total_l + sums[1]
        waiting = [(f, *ready)]
    span = pl.ds(0, (frames - 1) * tokens)
    first_part = copy(xt_ref.at[:, span], xt_hbm.at[:, span], xt_sem.at[0])
    first_part.start()
    sums = decide(*waiting[0])
    total_p = total_p + sums[0]
    total_l = total_l + sums[1]
    span = pl.ds((frames - 1) * tokens, tokens)
    last_part = copy(xt_ref.at[:, span], xt_hbm.at[:, span], xt_sem.at[1])
    last_part.start()
    at = lax.broadcasted_iota(jnp.int32, total_p.shape, 0)
    losses = jnp.sum(jnp.where(at < bits, total_l, 0.0), axis=0, keepdims=True)
    table = jnp.where(at < bits, total_p, jnp.where(at == bits, losses, 0.0))
    filled = jnp.concatenate([table, jnp.zeros((LANES - ROWS, LANES), F32)], axis=0)
    row = lax.dot_general(ones, filled, NT, precision=EXACT, preferred_element_type=F32)
    stat_ref[...] = jnp.broadcast_to(row[:1], stat_ref.shape)
    first_part.wait()
    last_part.wait()


def backward_kernel(
    bits, clip_count, token_count, me_ref,
    h_ref, xt_hbm, base_ref, slope_ref, q_ref, ag_ref, part_ref,
    d_hbm, mine_ref, theirs_ref, loss_ref,
    right_ref, xt_ref, d_ref, xt_sem, d_sem,
):
    frames, tokens, width = h_ref.shape
    arriving = copy(xt_hbm, xt_ref, xt_sem)
    arriving.start()
    leaving = [copy(d_ref.at[f], d_hbm.at[f], d_sem.at[f]) for f in range(frames)]
    core = (me_ref[0] // 2) % 2
    total = jnp.sum(part_ref[...], axis=0, keepdims=True)
    lane = lax.broadcasted_iota(jnp.int32, total.shape, 1)
    mean = jnp.where(lane < bits, total / token_count, 0.5)
    lean = jnp.log((1.0 - mean) / mean)
    entropy = -mean * jnp.log(mean) - (1.0 - mean) * jnp.log(1.0 - mean)
    term = jnp.where(lane < bits, -0.1 * entropy, jnp.where(lane == bits, total / token_count, 0.0))
    loss_ref[...] = jnp.sum(term, axis=1, keepdims=True)
    lean = diagonal(lean, ROWS) * 0.05
    high = ag_ref[:ROWS]
    low = ag_ref[ROWS:]
    right_ref[:, :width] = jnp.concatenate(
        [high, high, low, jnp.zeros((LANES - 3 * ROWS, width), BF16)], axis=0
    )
    at = lax.broadcasted_iota(jnp.int32, (LANES, LANES), 0)
    right_ref[:, width:] = jnp.where((at >= 3 * ROWS) & (at < 5 * ROWS), 1.0, 0.0).astype(BF16)
    step = 256
    for f in range(frames):
        u = (base_ref[f] - slope_ref[f] * lean) * (1.0 / clip_count)
        u_hi, u_lo = hi_lo(u)
        q_hi, q_lo = hi_lo(u * q_ref[f])
        spare = jnp.zeros((LANES - 5 * ROWS, tokens), BF16)
        left = jnp.concatenate([u_hi, u_lo, u_hi, q_hi, q_lo, spare], axis=0).T
        for start in range(0, tokens, step):
            piece = left[start : start + step]
            rows = slice(start, start + step)
            centre = jnp.dot(piece, right_ref[:, width:], preferred_element_type=F32)
            centre = jnp.concatenate([centre, centre], axis=1)
            for col in range(0, width, 2 * LANES):
                cols = slice(col, col + 2 * LANES)
                out = jnp.dot(piece, right_ref[:, cols], preferred_element_type=F32)
                d_ref[f, rows, cols] = (out - centre * h_ref[f, rows, cols].astype(F32)).astype(BF16)
        leaving[f].start()
    block = mine_ref.shape[1]
    group = 8 * block
    arriving.wait()
    for k in range(3):
        count = (frames - k) * tokens
        d_part = d_ref[k:].reshape(count, width)
        for first in range(0, width, GRAD_STEP):
            part = jnp.dot(xt_ref[first : first + GRAD_STEP, :count], d_part, preferred_element_type=F32).astype(BF16)
            base = k * width + first
            for side in range(2):

                @pl.when(core == side)
                def _():
                    row = base
                    while row < base + GRAD_STEP:
                        stop = min((row // block + 1) * block, base + GRAD_STEP)
                        half, within = divmod(row, 2 * group)
                        owner, inside = divmod(within, group)
                        slot, offset = divmod(inside, block)
                        target = mine_ref if owner == side else theirs_ref
                        target[slot * 2 + half, offset : offset + stop - row, :] = part[row - base : stop - base]
                        row = stop
    for one in leaving:
        one.wait()


def input_kernel(
    me_ref, d_hbm, w_hbm, m_hbm, v_hbm,
    out_hbm, mh_ref, vh_ref,
    w_ref, out_ref, d_ref, w_sem, keep_sem, out_sem, d_sem,
):
    frames, tokens, width = d_hbm.shape
    batch, _, sites, _ = out_hbm.shape
    w_copies = [
        copy(w_hbm.at[pl.ds(k * width, width)], w_ref.at[pl.ds(k * width, width)], w_sem.at[k]) for k in range(3)
    ]
    kept = [
        copy(m_hbm, mh_ref, keep_sem.at[0]),
        copy(v_hbm, vh_ref, keep_sem.at[1]),
    ]
    d_copies = [copy(d_hbm.at[f], d_ref.at[f], d_sem.at[f]) for f in range(frames)]
    for i in range(frames):
        d_copies[frames - 1 - i].start()
        if i < 3:
            w_copies[i].start()
    for one in kept:
        one.start()
    sent = []
    for f in range(frames - 1, -1, -1):
        if frames - 1 - f < 3:
            w_copies[frames - 1 - f].wait()
        d_copies[f].wait()
        total = d_ref[f].astype(F32)
        for k in range(min(3, frames - f)):
            total = total + lax.dot_general(
                d_ref[f + k], w_ref[k * width : (k + 1) * width, :], NT, preferred_element_type=F32
            )
        out_ref[f] = total.astype(BF16)
        for c in range(batch):
            one = copy(out_ref.at[f, pl.ds(c * sites, sites)], out_hbm.at[c, f], out_sem.at[f, c])
            one.start()
            sent.append(one)
    for one in kept + sent:
        one.wait()


def updated(weight, first, second, grad):
    first_out = 0.9 * first + 0.1 * grad
    second_out = 0.99 * second + 0.01 * grad * grad
    new = (weight - 0.001 * first_out / (jnp.sqrt(second_out) + 1e-08)).astype(BF16)
    return new, first_out, second_out


def block_kernel(me_ref, parts_ref, w_hbm, mh_ref, vh_ref, send_ref, w_ref, w_sem):
    me = me_ref[0]
    half = me % 2
    core = (me // 2) % 2
    slot = (me // 64) * 2 + (me // 4) % 2
    block = parts_ref.shape[1]
    start = core * 8 * block + slot * block
    rows = pl.ds(pl.multiple_of(start, block), block)
    arriving = copy(w_hbm.at[pl.ds(pl.multiple_of(half * mh_ref.shape[0] + start, block), block)], w_ref, w_sem)
    arriving.start()
    grad = jnp.sum(parts_ref[...].astype(F32), axis=0).astype(BF16)
    arriving.wait()
    new, _, _ = updated(w_ref[...].astype(F32), mh_ref[rows, :], vh_ref[rows, :], grad.astype(F32))
    for d in range(0, send_ref.shape[0], 2):
        send_ref[d + half] = grad
        send_ref[d + 1 - half] = new


def final_kernel(
    side, me_ref, blocks_ref, w_hbm, mh_ref, vh_ref, *refs
):
    new_hbm, first_hbm, second_hbm, new_ref, other_ref, first_ref, second_ref, w_ref, sem, w_sem = refs[-10:]
    half = me_ref[0] % 2
    core = (me_ref[0] // 2) % 2
    owner = core if side == 0 else 1 - core
    slots, block, width = blocks_ref.shape
    owned = mh_ref.shape[0]
    start = pl.multiple_of(owner * (owned // 2), owned // 2)
    rows = 4 * block
    arriving = copy(w_hbm.at[pl.ds(pl.multiple_of(half * owned + start, rows), 2 * rows)], w_ref, w_sem)
    arriving.start()
    arriving.wait()
    sent = []
    for chunk in range(2):
        for j in range(4):
            slot = chunk * 4 + j
            part = pl.ds(pl.multiple_of(start + slot * block, block), block)
            here = pl.ds(slot * block, block)
            grad = blocks_ref[slot * 2 + half].astype(F32)
            new, first_out, second_out = updated(w_ref[here, :].astype(F32), mh_ref[part, :], vh_ref[part, :], grad)
            new_ref[here, :] = new
            other_ref[here, :] = blocks_ref[slot * 2 + 1 - half]
            first_ref[here, :] = first_out
            second_ref[here, :] = second_out
        local = pl.ds(chunk * rows, rows)
        far = pl.ds(pl.multiple_of(start + chunk * rows, rows), rows)
        mine = pl.ds(pl.multiple_of(half * owned + start + chunk * rows, rows), rows)
        peer = pl.ds(pl.multiple_of((1 - half) * owned + start + chunk * rows, rows), rows)
        for i, (source, target, place) in enumerate(
            [(new_ref, new_hbm, mine), (other_ref, new_hbm, peer), (first_ref, first_hbm, far), (second_ref, second_hbm, far)]
        ):
            one = copy(source.at[local], target.at[place], sem.at[chunk, i])
            one.start()
            sent.append(one)
    for one in sent:
        one.wait()


SCALAR = pl.BlockSpec(memory_space=pltpu.SMEM)
NEAR = pl.BlockSpec(memory_space=pltpu.VMEM)
FAR = pl.BlockSpec(memory_space=pltpu.HBM)
DMA = pltpu.SemaphoreType.DMA
PARAMS = pltpu.CompilerParams(vmem_limit_bytes=32 * 1024 * 1024)


def local(value):
    return pltpu.with_memory_space_constraint(value, pltpu.VMEM)


def remote(value):
    return pltpu.with_memory_space_constraint(value, pltpu.HBM)


def run_forward(me, clips, weight, proj, gain, code_bias, rotation, cotangent, devices):
    batch, frames, sites, width = clips.shape
    tokens = batch * sites
    rows = (frames, ROWS, tokens)
    outs = [
        pltpu.VMEM((frames, tokens, width), BF16), pltpu.HBM((width, frames * tokens), BF16),
        pltpu.VMEM(rows, F32), pltpu.VMEM(rows, F32), pltpu.VMEM(rows, F32),
        pltpu.VMEM((2 * ROWS, width), BF16), pltpu.VMEM((devices, LANES), F32),
    ]
    return pl.pallas_call(
        forward_kernel,
        in_specs=[SCALAR] + [FAR] * 7,
        out_specs=[NEAR, FAR] + [NEAR] * 5,
        out_shape=outs,
        scratch_shapes=[
            pltpu.VMEM((frames, tokens, width), BF16), pltpu.VMEM(weight.shape, BF16),
            pltpu.VMEM((ROWS, width), F32), pltpu.VMEM(rows, F32),
            pltpu.VMEM((width, frames * tokens), BF16),
            *[pltpu.VMEM(a.shape, a.dtype) for a in (proj, gain, code_bias, rotation, cotangent)],
            DMA((frames, batch)), DMA((3,)), DMA((2,)), DMA((5,)),
        ],
        compiler_params=PARAMS,
        name="forward",
    )(me, *[remote(a) for a in (clips, weight, proj, gain, code_bias, rotation, cotangent)])


def run_backward(bits, clip_count, token_count, me, saved, ag, parts, row_count):
    width = saved[0].shape[2]
    block = (16, row_count // 32, width)
    return pl.pallas_call(
        functools.partial(backward_kernel, bits, clip_count, token_count),
        in_specs=[SCALAR, NEAR, FAR] + [NEAR] * 5,
        out_specs=[FAR] + [NEAR] * 3,
        out_shape=[
            pltpu.HBM(saved[0].shape, BF16), pltpu.VMEM(block, BF16), pltpu.VMEM(block, BF16),
            jax.ShapeDtypeStruct((1, 1), F32),
        ],
        scratch_shapes=[
            pltpu.VMEM((LANES, width + LANES), BF16), pltpu.VMEM(saved[1].shape, BF16), pltpu.VMEM(saved[0].shape, BF16),
            DMA(()), DMA((saved[0].shape[0],)),
        ],
        compiler_params=PARAMS,
        name="backward",
    )(me, local(saved[0]), remote(saved[1]), *[local(a) for a in (*saved[2:], ag)], local(parts))


def run_input(me, d_conv, weight, first, second, shape):
    batch, frames = shape[:2]
    owned = first.shape
    return pl.pallas_call(
        input_kernel,
        in_specs=[SCALAR] + [FAR] * 4,
        out_specs=[FAR, NEAR, NEAR],
        out_shape=[
            pltpu.HBM(shape, BF16),
            pltpu.VMEM(owned, F32), pltpu.VMEM(owned, F32),
        ],
        scratch_shapes=[
            pltpu.VMEM(weight.shape, BF16), pltpu.VMEM(d_conv.shape, BF16), pltpu.VMEM(d_conv.shape, BF16),
            DMA((3,)), DMA((2,)), DMA((frames, batch)), DMA((frames,)),
        ],
        compiler_params=PARAMS,
        name="input_grad",
    )(me, *[remote(a) for a in (d_conv, weight, first, second)])


def run_block(me, parts, weight, kept):
    send = (16, *parts.shape[1:])
    return pl.pallas_call(
        block_kernel,
        in_specs=[SCALAR, NEAR, FAR, NEAR, NEAR],
        out_specs=NEAR,
        out_shape=pltpu.VMEM(send, BF16),
        scratch_shapes=[pltpu.VMEM(parts.shape[1:], BF16), DMA(())],
        compiler_params=PARAMS,
        name="owner_step",
    )(me, local(parts), remote(weight), *[local(a) for a in kept])


def run_final(side, me, blocks, weight, kept, carried):
    owned, width = kept[0].shape
    shapes = [((2 * owned, width), BF16), ((owned, width), F32), ((owned, width), F32)]
    half = (owned // 2, width)
    return pl.pallas_call(
        functools.partial(final_kernel, side),
        in_specs=[SCALAR, NEAR, FAR, NEAR, NEAR] + [FAR] * len(carried),
        out_specs=[FAR] * 3,
        out_shape=[pltpu.HBM(s, t) for s, t in shapes],
        scratch_shapes=[
            pltpu.VMEM(half, BF16), pltpu.VMEM(half, BF16), pltpu.VMEM(half, F32), pltpu.VMEM(half, F32),
            pltpu.VMEM(half, BF16), DMA((2, 4)), DMA(()),
        ],
        input_output_aliases={5 + i: i for i in range(len(carried))},
        compiler_params=PARAMS,
        name="final_near" if side == 0 else "final_far",
    )(me, local(blocks), remote(weight), *[local(a) for a in kept], *[remote(a) for a in carried])


def spread(value, axes):
    return lax.all_to_all(value, axes, 0, 0, tiled=True)


def swapped(value):
    return lax.ppermute(value, "core", [(0, 1), (1, 0)])


def on_device(clips, code_grad, conv_weight, norm_gain, proj_weight, code_bias, rotation, first_moment, second_moment):
    bits = code_grad.shape[3]
    devices = lax.axis_size(ALL)
    batch, frames, sites, width = clips.shape
    clip_count = batch * devices
    token_count = clip_count * frames * sites
    me = lax.axis_index(ALL).astype(jnp.int32).reshape(1)
    cotangent = code_grad.transpose(1, 3, 0, 2)
    *saved, ag, stats = run_forward(
        me, clips, conv_weight, proj_weight.T, norm_gain[None, :], code_bias[None, :], rotation, cotangent, devices
    )
    parts = spread(stats, ALL)
    d_conv, mine, theirs, loss = run_backward(
        bits, clip_count, token_count, me, saved, ag, parts, conv_weight.shape[0]
    )
    chip = (mine.astype(F32) + swapped(theirs).astype(F32)).astype(BF16)
    plane = spread(chip, PLANE)
    input_grad, *kept = run_input(me, d_conv, conv_weight, first_moment, second_moment, clips.shape)
    plane, kept = lax.optimization_barrier((plane, kept))
    column = jnp.sum(plane.astype(F32), axis=0).astype(BF16)
    tower = spread(jnp.broadcast_to(column, (lax.axis_size("z"), *column.shape)), "z")
    near = spread(run_block(me, tower, conv_weight, kept), PLANE)
    far = swapped(near)
    carried = run_final(0, me, near, conv_weight, kept, [])
    new_weight, first_out, second_out = run_final(1, me, far, conv_weight, kept, carried)
    return new_weight, first_out, second_out, input_grad, loss[0, 0]


def solution(mesh):
    finer = Mesh(mesh.devices.reshape(4, 8, 2, 2, mesh.shape["shard"]), ALL)
    split = P(ALL, None, None, None)
    in_specs = (split, split, P(), P(), P(), P(), P(), P("yl", None), P("yl", None))
    out_specs = (P(), P("yl", None), P("yl", None), split, P())
    return jax.shard_map(on_device, mesh=finer, in_specs=in_specs, out_specs=out_specs, check_vma=False)
```

time: 128 us -> 111 us (0.87)
  blocking collectives: 31.1 us -> 59.8 us
  waiting for transfers between devices: 26.8 us -> 7.94 us
  starting transfers between devices: 24.1 us -> 9.02 us
  local copies, waits for them, and re-layouts: 6.03 us -> 0.03 us
  Pallas kernels: 36.5 us -> 30.6 us
    all_to_all x2 -> x3, blocking collectives: 31.1 us -> 59.8 us  [spread(): return lax.all_to_all(value, axes, 0, 0, tiled=True)]
    all_to_all x2 -> x1, waiting for transfers between devices: 24.7 us -> 6.03 us  [spread(): return lax.all_to_all(value, axes, 0, 0, tiled=True)]
    all_to_all x2 -> x1, starting transfers between devices: 19.1 us -> 4.47 us  [spread(): return lax.all_to_all(value, axes, 0, 0, tiled=True)]
    pallas_call x4 -> x5, Pallas kernels: 26.4 us -> 22.9 us  [the longest x1 9.9 us: run_forward(): pl.pallas_call(forward_kernel, in_specs=[SCALAR] + [FAR] * 7, out_specs=[...]
    unnamed x9 -> x0, local copies, waits for them, and re-layouts: 3.19 us -> none
    pallas_call x1, Pallas kernels: 10.1 us -> 7.63 us  [run_backward(): pl.pallas_call(functools.partial(backward_kernel, bits, clip_count, token...]
    broadcast_in_dim x1 -> x0, local copies, waits for them, and re-layouts: 1.38 us -> none  [on_device(): parts = spread(jnp.broadcast_to(stats, (devices, LANES)), ALL)]
  transfers between devices with their start and end apart: 4 -> 3, of which waited for: 3 -> 2; matrix products, arithmetic and copies ran while one was open for 0% -> 0% of each run, Pallas kernels for 5% -> 8%
where the time goes in v2:
time: 111 us
  blocking collectives  59.8 us (54%)
  Pallas kernels  30.6 us (28%)
  starting transfers between devices  9.02 us (8%)
  waiting for transfers between devices  7.94 us (7%)
  other arithmetic  2.37 us (2%)
    all_to_all x3, blocking collectives, spread(): return lax.all_to_all(value, axes, 0, 0, tiled=True)  59.8 us
    pallas_call x1, Pallas kernels, run_forward(): pl.pallas_call(forward_kernel, in_specs=[SCALAR] + [FAR] * 7, out_specs=[...  9.9 us
    pallas_call x1, Pallas kernels, run_backward(): pl.pallas_call(functools.partial(backward_kernel, bits, clip_count, token...  7.63 us
    pallas_call x1, Pallas kernels, run_input(): pl.pallas_call(input_kernel, in_specs=[SCALAR] + [FAR] * 4, out_specs=[FA...  6.58 us
    all_to_all x1, waiting for transfers between devices, spread(): return lax.all_to_all(value, axes, 0, 0, tiled=True)  6.03 us
    pallas_call x2, Pallas kernels, run_final(): pl.pallas_call(functools.partial(final_kernel, side), in_specs=[SCALAR, N...  5.53 us
    ppermute x2, starting transfers between devices, swapped(): return lax.ppermute(value, 'core', [(0, 1), (1, 0)])  4.55 us
    all_to_all x1, starting transfers between devices, spread(): return lax.all_to_all(value, axes, 0, 0, tiled=True)  4.47 us
  transfers between devices with their start and end apart: 3, of which 2 were waited for; matrix products, arithmetic and copies ran while one was open for 0% of the time, Pallas kernels for 8%

profile of v2, /device:TPU:1, one launch (start us, length us, event | category | flops | bytes accessed | tf_op | source)
XLA Modules:
  0.0 110.7 jit_solution(10027287992940973622)
XLA Ops:
  0.6 9.9 %forward.1 = (bf16[5,512,512]{2,1,0:T(8,128)(2,1)S(1)}, bf16[512,2560]{1,0:T(8,128)(2,1)}, f32[5,24,512]{2,1,0:T(8,128)S(1)}, f32[5,24,512]{2,1,0:T(8,128)S(1)},...) custom-call(s32[1]{0:T(128)} %bitcast._.me_ref, bf16[2,5,256,512]{3,2,1,0:T(8,128)(2,1)} %x_hbm.1, ...), custom_call_target="tpu_custom_call" | custom-call | tf_op jit(solution)/shard_map/forward/pallas_call | solution.py:364
  10.6 28.5 %all_to_all.26 = f32[256,1,128]{2,1,0:T(1,128)S(1)} all-to-all(f32[256,1,128]{2,1,0:T(1,128)S(1)} %bitcast.11), channel_id=1, replica_groups=mesh['x'=4,'z'=8,'yh'=2,'core'=2,'yl'=2] {'x','z','yh','core','yl'}, dimensions={0} | all-to-all | bytes 262144 | tf_op jit(solution)/shard_map/all_to_all | solution.py:454
  39.1 7.6 %backward.1 = (bf16[5,512,512]{2,1,0:T(8,128)(2,1)}, bf16[16,48,512]{2,1,0:T(8,128)(2,1)S(1)}, bf16[16,48,512]{2,1,0:T(8,128)(2,1)S(1)}, f32[1,1]{1,0:T(1,128)}) custom-call(s32[1]{0:T(128)} %bitcast._.me_ref, bf16[5,512,512]{2,1,0:T(8,128)(2,1)S(1)} %get-tuple-element.28.h_ref, bf16[512,2560]{1,0:T(8,128)(2,1)} %get-tuple-element.29.xt_hbm, ...), custom_call_target="tpu_custom_call" | custom-call | tf_op jit(solution)/shard_map/backward/pallas_call | solution.py:384
  46.7 0.6 collective-permute-start
  47.3 1.9 %collective-permute-done = bf16[16,48,512]{2,1,0:T(8,128)(2,1)S(1)} collective-permute-done((bf16[16,48,512]{2,1,0:T(8,128)(2,1)S(1)}, bf16[16,48,512]{2,1,0:T(8,128)(2,1)S(1)}, u32[]{:S(2)}, u32[]{:S(2)}) %collective-permute-start) | collective-permute-done | bytes 786464 | tf_op jit(solution)/shard_map/ppermute | solution.py:458
  49.2 1.1 %add_convert_fusion = bf16[16,48,512]{2,1,0:T(8,128)(2,1)} fusion(bf16[16,48,512]{2,1,0:T(8,128)(2,1)S(1)} %collective-permute-done, bf16[16,48,512]{2,1,0:T(8,128)(2,1)S(1)} %get-tuple-element.35), kind=kLoop, calls=%fused_computation | loop fusion | flops 1572864 | bytes 2359296 | tf_op jit(solution)/shard_map/convert_element_type | solution.py:476
  50.3 4.5 %all-to-all-start.1 = ((bf16[16,48,512]{2,1,0:T(8,128)(2,1)}), bf16[16,48,512]{2,1,0:T(8,128)(2,1)}, u32[]{:S(2)}, u32[]{:S(2)}) async-start(bf16[16,48,512]{2,1,0:T(8,128)(2,1)} %add_convert_fusion), calls=%async_computation.1 | async-start | bytes 1572864 | tf_op jit(solution)/shard_map/all_to_all | solution.py:454
  54.8 6.6 %input_grad.1 = (bf16[2,5,256,512]{3,2,1,0:T(8,128)(2,1)}, f32[768,512]{1,0:T(8,128)S(1)}, f32[768,512]{1,0:T(8,128)S(1)}) custom-call(s32[1]{0:T(128)} %bitcast._.me_ref, bf16[5,512,512]{2,1,0:T(8,128)(2,1)} %get-tuple-element.37.d_hbm, bf16[1536,512]{1,0:T(8,128)(2,1)} %w_hbm.9, f32[768,512]{1,0:T(8,128)} %m_hbm.1, f32[768,512]{1,0:T(8,128)} %v_hbm.1), custom_call_target="tpu_custom_call" | custom-call | tf_op jit(solution)/shard_map/input_grad/pallas_call | solution.py:404
  61.4 6.0 %all-to-all-done.1 = bf16[16,48,512]{2,1,0:T(8,128)(2,1)} async-done(((bf16[16,48,512]{2,1,0:T(8,128)(2,1)}), bf16[16,48,512]{2,1,0:T(8,128)(2,1)}, u32[]{:S(2)}, u32[]{:S(2)}) %all-to-all-start.1) | async-done | bytes 786464 | tf_op jit(solution)/shard_map/all_to_all | solution.py:454
  67.4 1.2 %reduce_sum.12 = bf16[48,512]{1,0:T(8,128)(2,1)S(1)} reduce(bf16[16,48,512]{2,1,0:T(8,128)(2,1)} %all-to-all-done.1, bf16[]{:T(256)} %constant.29.clone.1), dimensions={0}, to_apply=%region_0.0 | reduce | flops 368640 | bytes 835586 | tf_op jit(solution)/shard_map/reduce_sum | solution.py:480
  68.7 13.8 %all_to_all.27.parts_ref = bf16[8,48,512]{2,1,0:T(8,128)(2,1)S(1)} all-to-all(bf16[8,48,512]{2,1,0:T(8,128)(2,1)S(1)} %broadcast_in_dim.11), channel_id=1, replica_groups=mesh['x'=4,'z'=8,'yh'=2,'core'=2,'yl'=2] {'z'}, dimensions={0} | all-to-all | bytes 786432 | tf_op jit(solution)/shard_map/all_to_all | solution.py:454
  82.5 0.9 owner_step.1
  83.4 17.6 %all_to_all.28.blocks_ref = bf16[16,48,512]{2,1,0:T(8,128)(2,1)S(1)} all-to-all(bf16[16,48,512]{2,1,0:T(8,128)(2,1)S(1)} %owner_step.1), channel_id=1, replica_groups=mesh['x'=4,'z'=8,'yh'=2,'core'=2,'yl'=2] {'x','yh','yl'}, dimensions={0} | all-to-all | bytes 1572864 | tf_op jit(solution)/shard_map/all_to_all | solution.py:454
  101.0 4.0 %collective-permute-start.1 = (bf16[16,48,512]{2,1,0:T(8,128)(2,1)S(1)}, bf16[16,48,512]{2,1,0:T(8,128)(2,1)S(1)}, u32[]{:S(2)}, u32[]{:S(2)}) collective-permute-start(bf16[16,48,512]{2,1,0:T(8,128)(2,1)S(1)} %all_to_all.28.blocks_ref), channel_id=1, source_target_pairs={{0,2},{2,0},{1,3},{3,1},{4,6},{6,4},{5,7},{7,5},{8,10},{10,8},{9,1... | collective-permute-start | bytes 2359304 | tf_op jit(solution)/shard_map/ppermute | solution.py:458
  104.9 2.8 %final_near.1 = (bf16[1536,512]{1,0:T(8,128)(2,1)}, f32[768,512]{1,0:T(8,128)}, f32[768,512]{1,0:T(8,128)}) custom-call(s32[1]{0:T(128)} %bitcast._.me_ref, bf16[16,48,512]{2,1,0:T(8,128)(2,1)S(1)} %all_to_all.28.blocks_ref, bf16[1536,512]{1,0:T(8,128)(2,1)} %w_hbm.9, f32[768,512]{1,0:T(8,128)S(1)} %get-tuple-element.41.mh_ref, ...), custom_call_target="tpu_custom_call" | custom-call | tf_op jit(solution)/shard_map/final_near/pallas_call | solution.py:438
  107.7 0.0 collective-permute-done.1.blocks_ref
  107.7 2.8 %final_far.1 = (bf16[1536,512]{1,0:T(8,128)(2,1)}, f32[768,512]{1,0:T(8,128)}, f32[768,512]{1,0:T(8,128)}) custom-call(s32[1]{0:T(128)} %bitcast._.me_ref, bf16[16,48,512]{2,1,0:T(8,128)(2,1)S(1)} %collective-permute-done.1.blocks_ref, bf16[1536,512]{1,0:T(8,128)(2,1)} %w_hbm.9, ...), custom_call_target="tpu_custom_call", output_to_operand_aliasing={{0}: (5, {}), {1}: (6, {}), {2}: (7, {})} | custom-call | tf_op jit(solution)/shard_map/final_far/pallas_call | solution.py:438
  (1 shorter events, 0.0 us)
Async XLA Ops:
  46.7 2.5 %collective-permute-start = (bf16[16,48,512]{2,1,0:T(8,128)(2,1)S(1)}, bf16[16,48,512]{2,1,0:T(8,128)(2,1)S(1)}, u32[]{:S(2)}, u32[]{:S(2)}) collective-permute-start(bf16[16,48,512]{2,1,0:T(8,128)(2,1)S(1)} %get-tuple-element.36), channel_id=1, source_target_pairs={{0,2},{2,0},{1,3},{3,1},{4,6},{6,4},{5,7},{7,5},{8,10},{10,8},{9,1... | collective-permute-start | bytes 2359304 | tf_op jit(solution)/shard_map/ppermute | solution.py:458
  50.3 17.1 %all-to-all-start.1 = ((bf16[16,48,512]{2,1,0:T(8,128)(2,1)}), bf16[16,48,512]{2,1,0:T(8,128)(2,1)}, u32[]{:S(2)}, u32[]{:S(2)}) async-start(bf16[16,48,512]{2,1,0:T(8,128)(2,1)} %add_convert_fusion), calls=%async_computation.1 | async-start | bytes 1572864 | tf_op jit(solution)/shard_map/all_to_all | solution.py:454
  101.0 6.7 %collective-permute-start.1 = (bf16[16,48,512]{2,1,0:T(8,128)(2,1)S(1)}, bf16[16,48,512]{2,1,0:T(8,128)(2,1)S(1)}, u32[]{:S(2)}, u32[]{:S(2)}) collective-permute-start(bf16[16,48,512]{2,1,0:T(8,128)(2,1)S(1)} %all_to_all.28.blocks_ref), channel_id=1, source_target_pairs={{0,2},{2,0},{1,3},{3,1},{4,6},{6,4},{5,7},{7,5},{8,10},{10,8},{9,1... | collective-permute-start | bytes 2359304 | tf_op jit(solution)/shard_map/ppermute | solution.py:458

commit v3 on v2

--- a/solution.py
+++ b/solution.py
@@ -9,6 +9,7 @@
 from jax.sharding import PartitionSpec as P
 
 ALL = ("x", "z", "yh", "core", "yl")
+CHIPS = ("x", "z", "yh", "yl")
 PLANE = ("x", "yh", "yl")
 ROWS = 24
 ROW_STEP = 512
@@ -47,9 +48,9 @@
 
 def forward_kernel(
     _, x_hbm, w_hbm, proj_hbm, gain_hbm, code_bias_hbm, rotation_hbm, cg_hbm,
-    h_ref, xt_hbm, base_ref, slope_ref, q_ref, ag_ref, stat_ref,
-    x_ref, w_ref, map_ref, cot_ref, xt_ref, proj_ref, gain_ref, code_bias_ref, rotation_ref, cg_ref,
-    x_sem, w_sem, xt_sem, small_sem,
+    h_ref, raw_ref, inv_ref, bias_ref, cot_ref, ag_ref, stat_ref,
+    x_ref, w_ref, map_ref, proj_ref, gain_ref, code_bias_ref, rotation_ref, cg_ref,
+    x_sem, w_sem, small_sem,
 ):
     batch, frames, sites, width = x_hbm.shape
     bits = rotation_ref.shape[0]
@@ -85,6 +86,7 @@
     )
     row = jnp.dot(code_bias_ref[...], rotation_ref[...], precision=EXACT, preferred_element_type=F32)
     bias = diagonal(jnp.concatenate([row, jnp.zeros((1, LANES - bits), F32)], axis=1), ROWS)
+    bias_ref[...] = jnp.broadcast_to(bias, bias_ref.shape)
     high, low = hi_lo(map_ref[...])
     ag_ref[...] = jnp.concatenate([high, low], axis=0)
     ones = jnp.ones((8, LANES), F32)
@@ -121,12 +123,8 @@
         logit = 2.0 * rotated
         gap = rotated - codes
         entropy = jnp.maximum(logit, 0.0) + jnp.log(1.0 + small) - logit * probs
-        slope = 1.0 - codes * codes
-        base = cotangent * slope + 0.5 * gap * (1.0 - slope) - 0.1 * rotated * slope
-        base_ref[f] = base * inv
-        slope_ref[f] = slope * inv
-        q_ref[f] = raw * (inv * inv) / width
-        xt_ref[:, f * tokens : (f + 1) * tokens] = x_ref[f].T
+        raw_ref[f] = raw
+        inv_ref[f] = jnp.broadcast_to(inv, inv_ref.shape[1:])
         return lane_groups(probs), lane_groups(cotangent * codes + 0.25 * gap * gap + 0.1 * entropy)
 
     def arrive(f):
@@ -144,32 +142,72 @@
             total_p = total_p + sums[0]
             total_l = total_l + sums[1]
         waiting = [(f, *ready)]
-    span = pl.ds(0, (frames - 1) * tokens)
-    first_part = copy(xt_ref.at[:, span], xt_hbm.at[:, span], xt_sem.at[0])
-    first_part.start()
     sums = decide(*waiting[0])
     total_p = total_p + sums[0]
     total_l = total_l + sums[1]
-    span = pl.ds((frames - 1) * tokens, tokens)
-    last_part = copy(xt_ref.at[:, span], xt_hbm.at[:, span], xt_sem.at[1])
-    last_part.start()
     at = lax.broadcasted_iota(jnp.int32, total_p.shape, 0)
     losses = jnp.sum(jnp.where(at < bits, total_l, 0.0), axis=0, keepdims=True)
     table = jnp.where(at < bits, total_p, jnp.where(at == bits, losses, 0.0))
     filled = jnp.concatenate([table, jnp.zeros((LANES - ROWS, LANES), F32)], axis=0)
     row = lax.dot_general(ones, filled, NT, precision=EXACT, preferred_element_type=F32)
     stat_ref[...] = jnp.broadcast_to(row[:1], stat_ref.shape)
-    first_part.wait()
-    last_part.wait()
+
+
+def window_kernel(
+    x_hbm, h_ref, raw_ref, inv_ref, bias_ref, cot_ref,
+    h_hbm, xt_hbm, rows_hbm,
+    x_ref, xt_ref, rows_ref, x_sem, xt_sem, h_sem, rows_sem,
+):
+    batch, frames, sites, width = x_hbm.shape
+    tokens = batch * sites
+    arriving = [
+        copy(x_hbm.at[c, f], x_ref.at[f, pl.ds(c * sites, sites)], x_sem.at[f, c])
+        for f in range(frames)
+        for c in range(batch)
+    ]
+    for one in arriving:
+        one.start()
+    moved = copy(h_ref, h_hbm, h_sem)
+    moved.start()
+    bias = bias_ref[:, :1]
+    for f in range(frames):
+        raw = raw_ref[f]
+        inv = inv_ref[f][:1]
+        rotated = raw * inv + bias
+        cotangent = cot_ref[f]
+        small = jnp.exp(-2.0 * jnp.abs(rotated))
+        size = (1.0 - small) / (1.0 + small)
+        codes = jnp.where(rotated < 0.0, -size, size)
+        slope = 1.0 - codes * codes
+        base = cotangent * slope + 0.5 * (rotated - codes) * (1.0 - slope) - 0.1 * rotated * slope
+        rows_ref[f, 0] = base * inv
+        rows_ref[f, 1] = slope * inv
+        rows_ref[f, 2] = raw * (inv * inv) / width
+    gone = copy(rows_ref, rows_hbm, rows_sem)
+    gone.start()
+    for one in arriving:
+        one.wait()
+    for f in range(frames):
+        xt_ref[:, f * tokens : (f + 1) * tokens] = x_ref[f].T
+    leaving = copy(xt_ref, xt_hbm, xt_sem)
+    leaving.start()
+    leaving.wait()
+    moved.wait()
+    gone.wait()
 
 
 def backward_kernel(
     bits, clip_count, token_count, me_ref,
-    h_ref, xt_hbm, base_ref, slope_ref, q_ref, ag_ref, part_ref,
-    d_hbm, mine_ref, theirs_ref, loss_ref,
-    right_ref, xt_ref, d_ref, xt_sem, d_sem,
+    h_hbm, xt_hbm, rows_hbm, ag_ref, part_ref,
+    d_hbm, both_ref, loss_ref,
+    right_ref, xt_ref, d_ref, grad_ref, h_ref, rows_ref, xt_sem, d_sem, h_sem, rows_sem,
 ):
-    frames, tokens, width = h_ref.shape
+    frames, tokens, width = h_hbm.shape
+    h_copies = [copy(h_hbm.at[f], h_ref.at[f], h_sem.at[f]) for f in range(frames)]
+    rows_copies = [copy(rows_hbm.at[f], rows_ref.at[f], rows_sem.at[f]) for f in range(frames)]
+    for f in range(frames):
+        rows_copies[f].start()
+        h_copies[f].start()
     arriving = copy(xt_hbm, xt_ref, xt_sem)
     arriving.start()
     leaving = [copy(d_ref.at[f], d_hbm.at[f], d_sem.at[f]) for f in range(frames)]
@@ -184,50 +222,48 @@
     lean = diagonal(lean, ROWS) * 0.05
     high = ag_ref[:ROWS]
     low = ag_ref[ROWS:]
-    right_ref[:, :width] = jnp.concatenate(
+    right_ref[...] = jnp.concatenate(
         [high, high, low, jnp.zeros((LANES - 3 * ROWS, width), BF16)], axis=0
     )
-    at = lax.broadcasted_iota(jnp.int32, (LANES, LANES), 0)
-    right_ref[:, width:] = jnp.where((at >= 3 * ROWS) & (at < 5 * ROWS), 1.0, 0.0).astype(BF16)
     step = 256
     for f in range(frames):
-        u = (base_ref[f] - slope_ref[f] * lean) * (1.0 / clip_count)
+        for other in {0: [0], 1: range(1, frames)}.get(f, []):
+            rows_copies[other].wait()
+            h_copies[other].wait()
+        u = (rows_ref[f, 0] - rows_ref[f, 1] * lean) * (1.0 / clip_count)
         u_hi, u_lo = hi_lo(u)
-        q_hi, q_lo = hi_lo(u * q_ref[f])
-        spare = jnp.zeros((LANES - 5 * ROWS, tokens), BF16)
-        left = jnp.concatenate([u_hi, u_lo, u_hi, q_hi, q_lo, spare], axis=0).T
+        centres = jnp.sum(u * rows_ref[f, 2], axis=0, keepdims=True)
+        centres = jnp.broadcast_to(centres, (8, tokens)).T
+        spare = jnp.zeros((LANES - 3 * ROWS, tokens), BF16)
+        left = jnp.concatenate([u_hi, u_lo, u_hi, spare], axis=0).T
         for start in range(0, tokens, step):
             piece = left[start : start + step]
             rows = slice(start, start + step)
-            centre = jnp.dot(piece, right_ref[:, width:], preferred_element_type=F32)
-            centre = jnp.concatenate([centre, centre], axis=1)
+            centre = jnp.broadcast_to(centres[rows, :1], (step, 2 * LANES))
             for col in range(0, width, 2 * LANES):
                 cols = slice(col, col + 2 * LANES)
                 out = jnp.dot(piece, right_ref[:, cols], preferred_element_type=F32)
                 d_ref[f, rows, cols] = (out - centre * h_ref[f, rows, cols].astype(F32)).astype(BF16)
         leaving[f].start()
-    block = mine_ref.shape[1]
+    block = both_ref.shape[2]
     group = 8 * block
     arriving.wait()
     for k in range(3):
         count = (frames - k) * tokens
         d_part = d_ref[k:].reshape(count, width)
-        for first in range(0, width, GRAD_STEP):
-            part = jnp.dot(xt_ref[first : first + GRAD_STEP, :count], d_part, preferred_element_type=F32).astype(BF16)
-            base = k * width + first
-            for side in range(2):
-
-                @pl.when(core == side)
-                def _():
-                    row = base
-                    while row < base + GRAD_STEP:
-                        stop = min((row // block + 1) * block, base + GRAD_STEP)
-                        half, within = divmod(row, 2 * group)
-                        owner, inside = divmod(within, group)
-                        slot, offset = divmod(inside, block)
-                        target = mine_ref if owner == side else theirs_ref
-                        target[slot * 2 + half, offset : offset + stop - row, :] = part[row - base : stop - base]
-                        row = stop
+        base = k * width
+        grad_ref[base : base + width, :] = jnp.dot(xt_ref[:, :count], d_part, preferred_element_type=F32).astype(BF16)
+    for k in range(3):
+        base = k * width
+        row = base
+        while row < base + width:
+            stop = min((row // block + 1) * block, base + width)
+            half, within = divmod(row, 2 * group)
+            owner, inside = divmod(within, group)
+            slot, offset = divmod(inside, block)
+            where = core if owner == 0 else 1 - core
+            both_ref[where, slot * 2 + half, offset : offset + stop - row, :] = grad_ref[row:stop, :]
+            row = stop
     for one in leaving:
         one.wait()
 
@@ -297,44 +333,58 @@
         send_ref[d + 1 - half] = new
 
 
-def final_kernel(
-    side, me_ref, blocks_ref, w_hbm, mh_ref, vh_ref, *refs
-):
-    new_hbm, first_hbm, second_hbm, new_ref, other_ref, first_ref, second_ref, w_ref, sem, w_sem = refs[-10:]
+def final_kernel(side, me_ref, blocks_ref, *refs):
     half = me_ref[0] % 2
     core = (me_ref[0] // 2) % 2
     owner = core if side == 0 else 1 - core
     slots, block, width = blocks_ref.shape
+    if side == 0:
+        w_hbm, mh_ref, vh_ref = refs[:3]
+        new_hbm, first_hbm, second_hbm, w_next, new_ref, first_ref, second_ref, w_ref, sem, other_sem, w_sem = refs[3:]
+    else:
+        w_ref, mh_ref, vh_ref = refs[:3]
+        new_hbm, first_hbm, second_hbm, new_ref, first_ref, second_ref, sem, other_sem = refs[6:]
     owned = mh_ref.shape[0]
-    start = pl.multiple_of(owner * (owned // 2), owned // 2)
-    rows = 4 * block
-    arriving = copy(w_hbm.at[pl.ds(pl.multiple_of(half * owned + start, rows), 2 * rows)], w_ref, w_sem)
-    arriving.start()
-    arriving.wait()
+    side_rows = owned // 2
+    start = pl.multiple_of(owner * side_rows, side_rows)
+    if side == 0:
+        next_start = pl.multiple_of(half * owned + (1 - owner) * side_rows, side_rows)
+        near_w = copy(w_hbm.at[pl.ds(pl.multiple_of(half * owned + start, side_rows), side_rows)], w_ref, w_sem.at[0])
+        far_w = copy(w_hbm.at[pl.ds(next_start, side_rows)], w_next, w_sem.at[1])
+        near_w.start()
+        far_w.start()
     sent = []
-    for chunk in range(2):
-        for j in range(4):
-            slot = chunk * 4 + j
+    for slot in range(slots // 2):
+        peer = pl.multiple_of((1 - half) * owned + start + slot * block, block)
+        sent.append(copy(blocks_ref.at[slot * 2 + 1 - half], new_hbm.at[pl.ds(peer, block)], other_sem.at[slot]))
+        sent[-1].start()
+    if side == 0:
+        near_w.wait()
+    per = 2
+    rows = per * block
+    for chunk in range(slots // 2 // per):
+        for j in range(per):
+            slot = chunk * per + j
             part = pl.ds(pl.multiple_of(start + slot * block, block), block)
             here = pl.ds(slot * block, block)
             grad = blocks_ref[slot * 2 + half].astype(F32)
             new, first_out, second_out = updated(w_ref[here, :].astype(F32), mh_ref[part, :], vh_ref[part, :], grad)
             new_ref[here, :] = new
-            other_ref[here, :] = blocks_ref[slot * 2 + 1 - half]
             first_ref[here, :] = first_out
             second_ref[here, :] = second_out
         local = pl.ds(chunk * rows, rows)
         far = pl.ds(pl.multiple_of(start + chunk * rows, rows), rows)
         mine = pl.ds(pl.multiple_of(half * owned + start + chunk * rows, rows), rows)
-        peer = pl.ds(pl.multiple_of((1 - half) * owned + start + chunk * rows, rows), rows)
         for i, (source, target, place) in enumerate(
-            [(new_ref, new_hbm, mine), (other_ref, new_hbm, peer), (first_ref, first_hbm, far), (second_ref, second_hbm, far)]
+            [(new_ref, new_hbm, mine), (first_ref, first_hbm, far), (second_ref, second_hbm, far)]
         ):
             one = copy(source.at[local], target.at[place], sem.at[chunk, i])
             one.start()
             sent.append(one)
     for one in sent:
         one.wait()
+    if side == 0:
+        far_w.wait()
 
 
 SCALAR = pl.BlockSpec(memory_space=pltpu.SMEM)
@@ -357,45 +407,66 @@
     tokens = batch * sites
     rows = (frames, ROWS, tokens)
     outs = [
-        pltpu.VMEM((frames, tokens, width), BF16), pltpu.HBM((width, frames * tokens), BF16),
-        pltpu.VMEM(rows, F32), pltpu.VMEM(rows, F32), pltpu.VMEM(rows, F32),
+        pltpu.VMEM((frames, tokens, width), BF16), pltpu.VMEM(rows, F32), pltpu.VMEM((frames, 8, tokens), F32),
+        pltpu.VMEM((ROWS, LANES), F32), pltpu.VMEM(rows, F32),
         pltpu.VMEM((2 * ROWS, width), BF16), pltpu.VMEM((devices, LANES), F32),
     ]
     return pl.pallas_call(
         forward_kernel,
         in_specs=[SCALAR] + [FAR] * 7,
-        out_specs=[NEAR, FAR] + [NEAR] * 5,
+        out_specs=[NEAR] * 7,
         out_shape=outs,
         scratch_shapes=[
             pltpu.VMEM((frames, tokens, width), BF16), pltpu.VMEM(weight.shape, BF16),
-            pltpu.VMEM((ROWS, width), F32), pltpu.VMEM(rows, F32),
-            pltpu.VMEM((width, frames * tokens), BF16),
+            pltpu.VMEM((ROWS, width), F32),
             *[pltpu.VMEM(a.shape, a.dtype) for a in (proj, gain, code_bias, rotation, cotangent)],
-            DMA((frames, batch)), DMA((3,)), DMA((2,)), DMA((5,)),
+            DMA((frames, batch)), DMA((3,)), DMA((5,)),
         ],
         compiler_params=PARAMS,
         name="forward",
     )(me, *[remote(a) for a in (clips, weight, proj, gain, code_bias, rotation, cotangent)])
 
 
+def run_window(clips, hidden, raw, inv, bias, cot):
+    batch, frames, sites, width = clips.shape
+    tokens = batch * sites
+    return pl.pallas_call(
+        window_kernel,
+        in_specs=[FAR] + [NEAR] * 5,
+        out_specs=[FAR] * 3,
+        out_shape=[
+            pltpu.HBM(hidden.shape, BF16), pltpu.HBM((width, frames * tokens), BF16),
+            pltpu.HBM((frames, 3, *raw.shape[1:]), F32),
+        ],
+        scratch_shapes=[
+            pltpu.VMEM((frames, tokens, width), BF16), pltpu.VMEM((width, frames * tokens), BF16),
+            pltpu.VMEM((frames, 3, *raw.shape[1:]), F32), DMA((frames, batch)), DMA(()), DMA(()), DMA(()),
+        ],
+        compiler_params=PARAMS,
+        name="window",
+    )(remote(clips), *[local(a) for a in (hidden, raw, inv, bias, cot)])
+
+
 def run_backward(bits, clip_count, token_count, me, saved, ag, parts, row_count):
     width = saved[0].shape[2]
-    block = (16, row_count // 32, width)
+    both = (2, 16, row_count // 32, width)
     return pl.pallas_call(
         functools.partial(backward_kernel, bits, clip_count, token_count),
-        in_specs=[SCALAR, NEAR, FAR] + [NEAR] * 5,
-        out_specs=[FAR] + [NEAR] * 3,
+        in_specs=[SCALAR] + [FAR] * 3 + [NEAR] * 2,
+        out_specs=[FAR] + [NEAR] * 2,
         out_shape=[
-            pltpu.HBM(saved[0].shape, BF16), pltpu.VMEM(block, BF16), pltpu.VMEM(block, BF16),
+            pltpu.HBM(saved[0].shape, BF16), pltpu.VMEM(both, BF16),
             jax.ShapeDtypeStruct((1, 1), F32),
         ],
         scratch_shapes=[
-            pltpu.VMEM((LANES, width + LANES), BF16), pltpu.VMEM(saved[1].shape, BF16), pltpu.VMEM(saved[0].shape, BF16),
-            DMA(()), DMA((saved[0].shape[0],)),
+            pltpu.VMEM((LANES, width), BF16), pltpu.VMEM(saved[1].shape, BF16), pltpu.VMEM(saved[0].shape, BF16),
+            pltpu.VMEM((row_count, width), BF16), pltpu.VMEM(saved[0].shape, BF16),
+            pltpu.VMEM(saved[2].shape, F32),
+            DMA(()), *[DMA((saved[0].shape[0],))] * 3,
         ],
         compiler_params=PARAMS,
         name="backward",
-    )(me, local(saved[0]), remote(saved[1]), *[local(a) for a in (*saved[2:], ag)], local(parts))
+    )(me, *[remote(a) for a in saved], local(ag), local(parts))
 
 
 def run_input(me, d_conv, weight, first, second, shape):
@@ -435,19 +506,26 @@
     owned, width = kept[0].shape
     shapes = [((2 * owned, width), BF16), ((owned, width), F32), ((owned, width), F32)]
     half = (owned // 2, width)
+    outs = [pltpu.HBM(s, t) for s, t in shapes]
+    scratch = [pltpu.VMEM(half, BF16), pltpu.VMEM(half, F32), pltpu.VMEM(half, F32)]
+    sems = [DMA((4, 3)), DMA((8,))]
+    if side == 0:
+        outs.append(pltpu.VMEM(half, BF16))
+        scratch.append(pltpu.VMEM(half, BF16))
+        sems.append(DMA((2,)))
     return pl.pallas_call(
         functools.partial(final_kernel, side),
-        in_specs=[SCALAR, NEAR, FAR, NEAR, NEAR] + [FAR] * len(carried),
-        out_specs=[FAR] * 3,
-        out_shape=[pltpu.HBM(s, t) for s, t in shapes],
-        scratch_shapes=[
-            pltpu.VMEM(half, BF16), pltpu.VMEM(half, BF16), pltpu.VMEM(half, F32), pltpu.VMEM(half, F32),
-            pltpu.VMEM(half, BF16), DMA((2, 4)), DMA(()),
-        ],
+        in_specs=[SCALAR, NEAR, FAR if side == 0 else NEAR, NEAR, NEAR] + [FAR] * len(carried),
+        out_specs=[FAR] * 3 + [NEAR] * (1 - side),
+        out_shape=outs,
+        scratch_shapes=scratch + sems,
         input_output_aliases={5 + i: i for i in range(len(carried))},
         compiler_params=PARAMS,
         name="final_near" if side == 0 else "final_far",
-    )(me, local(blocks), remote(weight), *[local(a) for a in kept], *[remote(a) for a in carried])
+    )(
+        me, local(blocks), (remote if side == 0 else local)(weight),
+        *[local(a) for a in kept], *[remote(a) for a in carried],
+    )
 
 
 def spread(value, axes):
@@ -466,14 +544,15 @@
     token_count = clip_count * frames * sites
     me = lax.axis_index(ALL).astype(jnp.int32).reshape(1)
     cotangent = code_grad.transpose(1, 3, 0, 2)
-    *saved, ag, stats = run_forward(
-        me, clips, conv_weight, proj_weight.T, norm_gain[None, :], code_bias[None, :], rotation, cotangent, devices
+    hidden, raw, inv, bias, cot, ag, stats = run_forward(
+        me, clips, conv_weight, proj_weight.T, norm_gain[None, :], code_bias[None, :], rotation, cotangent, lax.axis_size(CHIPS)
     )
-    parts = spread(stats, ALL)
-    d_conv, mine, theirs, loss = run_backward(
+    parts = spread(stats + swapped(stats), CHIPS)
+    saved = run_window(clips, hidden, raw, inv, bias, cot)
+    d_conv, both, loss = run_backward(
         bits, clip_count, token_count, me, saved, ag, parts, conv_weight.shape[0]
     )
-    chip = (mine.astype(F32) + swapped(theirs).astype(F32)).astype(BF16)
+    chip = (both[0].astype(F32) + swapped(both[1]).astype(F32)).astype(BF16)
     plane = spread(chip, PLANE)
     input_grad, *kept = run_input(me, d_conv, conv_weight, first_moment, second_moment, clips.shape)
     plane, kept = lax.optimization_barrier((plane, kept))
@@ -481,8 +560,8 @@
     tower = spread(jnp.broadcast_to(column, (lax.axis_size("z"), *column.shape)), "z")
     near = spread(run_block(me, tower, conv_weight, kept), PLANE)
     far = swapped(near)
-    carried = run_final(0, me, near, conv_weight, kept, [])
-    new_weight, first_out, second_out = run_final(1, me, far, conv_weight, kept, carried)
+    *carried, w_far = run_final(0, me, near, conv_weight, kept, [])
+    new_weight, first_out, second_out = run_final(1, me, far, w_far, kept, carried)
     return new_weight, first_out, second_out, input_grad, loss[0, 0]
 
 

time: 111 us -> 110 us (level)
  blocking collectives: 59.8 us -> 31.3 us
  starting transfers between devices: 9.02 us -> 27.4 us
  waiting for transfers between devices: 7.94 us -> 14.1 us
  Pallas kernels: 30.6 us -> 32.6 us
    all_to_all x3 -> x2, blocking collectives: 59.8 us -> 31.3 us  [spread(): return lax.all_to_all(value, axes, 0, 0, tiled=True)]
    all_to_all x1 -> x2, starting transfers between devices: 4.47 us -> 18.3 us  [spread(): return lax.all_to_all(value, axes, 0, 0, tiled=True)]
    all_to_all x1 -> x2, waiting for transfers between devices: 6.03 us -> 11.3 us  [spread(): return lax.all_to_all(value, axes, 0, 0, tiled=True)]
    pallas_call x0 -> x1, Pallas kernels: none -> 5.24 us  [run_window(): pl.pallas_call(window_kernel, in_specs=[FAR] + [NEAR] * 5, out_specs=[FAR...]
    ppermute x2 -> x3, starting transfers between devices: 4.55 us -> 9.09 us  [swapped(): return lax.ppermute(value, 'core', [(0, 1), (1, 0)])]
    pallas_call x1, Pallas kernels: 9.9 us -> 8.29 us  [run_forward(): pl.pallas_call(forward_kernel, in_specs=[SCALAR] + [FAR] * 7, out_specs=[...]
    pallas_call x2, Pallas kernels: 5.53 us -> 4.34 us  [run_final(): pl.pallas_call(functools.partial(final_kernel, side), in_specs=[SCALAR, N...]
    ppermute x2 -> x3, waiting for transfers between devices: 1.91 us -> 2.82 us  [swapped(): return lax.ppermute(value, 'core', [(0, 1), (1, 0)])]
  transfers between devices with their start and end apart: 3 -> 5, of which waited for: 2 -> 4; matrix products, arithmetic and copies ran while one was open for 0% -> 0% of each run, Pallas kernels for 8% -> 13%
where the time goes in v3:
time: 110 us; the launch traced here: 109 us
  Pallas kernels  32.6 us (30%)
  blocking collectives  31.3 us (28%)
  starting transfers between devices  27.4 us (25%)
  waiting for transfers between devices  14.1 us (13%)
  other arithmetic  3.01 us (3%)
    all_to_all x2, blocking collectives, spread(): return lax.all_to_all(value, axes, 0, 0, tiled=True)  31.3 us
    all_to_all x2, starting transfers between devices, spread(): return lax.all_to_all(value, axes, 0, 0, tiled=True)  18.3 us
    all_to_all x2, waiting for transfers between devices, spread(): return lax.all_to_all(value, axes, 0, 0, tiled=True)  11.3 us
    ppermute x3, starting transfers between devices, swapped(): return lax.ppermute(value, 'core', [(0, 1), (1, 0)])  9.09 us
    pallas_call x1, Pallas kernels, run_forward(): pl.pallas_call(forward_kernel, in_specs=[SCALAR] + [FAR] * 7, out_specs=[...  8.29 us
    pallas_call x1, Pallas kernels, run_backward(): pl.pallas_call(functools.partial(backward_kernel, bits, clip_count, token...  7.22 us
    pallas_call x1, Pallas kernels, run_input(): pl.pallas_call(input_kernel, in_specs=[SCALAR] + [FAR] * 4, out_specs=[FA...  6.58 us
    pallas_call x1, Pallas kernels, run_window(): pl.pallas_call(window_kernel, in_specs=[FAR] + [NEAR] * 5, out_specs=[FAR...  5.24 us
  transfers between devices with their start and end apart: 5, of which 4 were waited for; matrix products, arithmetic and copies ran while one was open for 0% of the time, Pallas kernels for 13%

profile of v3, /device:TPU:1, one launch (start us, length us, event | category | flops | bytes accessed | tf_op | source)
XLA Modules:
  0.0 109.4 jit_solution(16809997187468223061)
XLA Ops:
  0.6 8.3 %forward.1 = (bf16[5,512,512]{2,1,0:T(8,128)(2,1)S(1)}, f32[5,24,512]{2,1,0:T(8,128)S(1)}, f32[5,8,512]{2,1,0:T(8,128)S(1)}, f32[24,128]{1,0:T(8,128)S(1)}, f32[...) custom-call(s32[1]{0:T(128)} %bitcast._.me_ref, bf16[2,5,256,512]{3,2,1,0:T(8,128)(2,1)} %x_hbm.3, ...), custom_call_target="tpu_custom_call" | custom-call | tf_op jit(solution)/shard_map/forward/pallas_call | solution.py:414
  8.9 3.3 %collective-permute-start = (f32[128,128]{1,0:T(8,128)S(1)}, f32[128,128]{1,0:T(8,128)S(1)}, u32[]{:S(2)}, u32[]{:S(2)}) collective-permute-start(f32[128,128]{1,0:T(8,128)S(1)} %get-tuple-element.40), channel_id=1, source_target_pairs={{0,2},{2,0},{1,3},{3,1},{4,6},{6,4},{5,7},{7,5},{8,10},{10,8},{9,1... | collective-permute-start | bytes 196616 | tf_op jit(solution)/shard_map/ppermute | solution.py:536
  12.2 0.9 collective-permute-done
  13.1 0.6 add.22
  13.8 13.8 %all-to-all-start = ((f32[128,1,128]{2,1,0:T(1,128)}), f32[128,1,128]{2,1,0:T(1,128)S(1)}, u32[]{:S(2)}, u32[]{:S(2)}) async-start(f32[128,1,128]{2,1,0:T(1,128)} %bitcast.6), calls=%async_computation | async-start | bytes 131072 | tf_op jit(solution)/shard_map/all_to_all | solution.py:532
  27.6 5.2 %window.1 = (bf16[5,512,512]{2,1,0:T(8,128)(2,1)}, bf16[512,2560]{1,0:T(8,128)(2,1)}, f32[5,3,24,512]{3,2,1,0:T(8,128)}) custom-call(bf16[2,5,256,512]{3,2,1,0:T(8,128)(2,1)} %x_hbm.3, bf16[5,512,512]{2,1,0:T(8,128)(2,1)S(1)} %get-tuple-element.31.h_ref, f32[5,24,512]{2,1,0:T(8,128)S(1)} %get-tuple-element.32.raw_ref, ...), custom_call_target="tpu_custom_call" | custom-call | tf_op jit(solution)/shard_map/window/pallas_call | solution.py:433
  32.8 5.3 %all-to-all-done = f32[128,1,128]{2,1,0:T(1,128)S(1)} async-done(((f32[128,1,128]{2,1,0:T(1,128)}), f32[128,1,128]{2,1,0:T(1,128)S(1)}, u32[]{:S(2)}, u32[]{:S(2)}) %all-to-all-start) | async-done | bytes 65568 | tf_op jit(solution)/shard_map/all_to_all | solution.py:532
  38.1 7.2 %backward.1 = (bf16[5,512,512]{2,1,0:T(8,128)(2,1)}, bf16[2,16,48,512]{3,2,1,0:T(8,128)(2,1)S(1)}, f32[1,1]{1,0:T(1,128)}) custom-call(s32[1]{0:T(128)} %bitcast._.me_ref, bf16[5,512,512]{2,1,0:T(8,128)(2,1)} %get-tuple-element.36.h_hbm, bf16[512,2560]{1,0:T(8,128)(2,1)} %get-tuple-element.37.xt_hbm, f32[5,3,24,512]{3,2,1,0:T(8,128)} %get-tuple-element.38.rows_hbm, ...), custom_call_target="tpu_custom_call" | custom-call | tf_op jit(solution)/shard_map/backward/pallas_call | solution.py:453
  45.3 0.1 slice_bitcast_fusion
  45.4 1.9 %collective-permute-start.1 = (bf16[16,48,512]{2,1,0:T(8,128)(2,1)S(1)}, bf16[16,48,512]{2,1,0:T(8,128)(2,1)S(1)}, u32[]{:S(2)}, u32[]{:S(2)}) collective-permute-start(bf16[16,48,512]{2,1,0:T(8,128)(2,1)S(1)} %slice_bitcast_fusion), channel_id=1, source_target_pairs={{0,2},{2,0},{1,3},{3,1},{4,6},{6,4},{5,7},{7,5},{8,10},{10,8},{9,1... | collective-permute-start | bytes 2359304 | tf_op jit(solution)/shard_map/ppermute | solution.py:536
  47.2 1.9 %collective-permute-done.1 = bf16[16,48,512]{2,1,0:T(8,128)(2,1)S(1)} collective-permute-done((bf16[16,48,512]{2,1,0:T(8,128)(2,1)S(1)}, bf16[16,48,512]{2,1,0:T(8,128)(2,1)S(1)}, u32[]{:S(2)}, u32[]{:S(2)}) %collective-permute-start.1) | collective-permute-done | bytes 786464 | tf_op jit(solution)/shard_map/ppermute | solution.py:536
  49.2 1.1 %fusion = bf16[16,48,512]{2,1,0:T(8,128)(2,1)} fusion(bf16[16,48,512]{2,1,0:T(8,128)(2,1)S(1)} %collective-permute-done.1, bf16[2,16,48,512]{3,2,1,0:T(8,128)(2,1)S(1)} %get-tuple-element.41), kind=kLoop, calls=%fused_computation.1 | loop fusion | flops 1572864 | bytes 2359296 | tf_op jit(solution)/shard_map/convert_element_type | solution.py:555
  50.3 4.5 %all-to-all-start.1 = ((bf16[16,48,512]{2,1,0:T(8,128)(2,1)}), bf16[16,48,512]{2,1,0:T(8,128)(2,1)}, u32[]{:S(2)}, u32[]{:S(2)}) async-start(bf16[16,48,512]{2,1,0:T(8,128)(2,1)} %fusion), calls=%async_computation.1 | async-start | bytes 1572864 | tf_op jit(solution)/shard_map/all_to_all | solution.py:532
  54.8 6.6 %input_grad.1 = (bf16[2,5,256,512]{3,2,1,0:T(8,128)(2,1)}, f32[768,512]{1,0:T(8,128)S(1)}, f32[768,512]{1,0:T(8,128)S(1)}) custom-call(s32[1]{0:T(128)} %bitcast._.me_ref, bf16[5,512,512]{2,1,0:T(8,128)(2,1)} %get-tuple-element.42.d_hbm, bf16[1536,512]{1,0:T(8,128)(2,1)} %refs_0_.1, f32[768,512]{1,0:T(8,128)} %m_hbm.1, f32[768,512]{1,0:T(8,128)} %v_hbm.1), custom_call_target="tpu_custom_call" | custom-call | tf_op jit(solution)/shard_map/input_grad/pallas_call | solution.py:475
  61.3 6.0 %all-to-all-done.1 = bf16[16,48,512]{2,1,0:T(8,128)(2,1)} async-done(((bf16[16,48,512]{2,1,0:T(8,128)(2,1)}), bf16[16,48,512]{2,1,0:T(8,128)(2,1)}, u32[]{:S(2)}, u32[]{:S(2)}) %all-to-all-start.1) | async-done | bytes 786464 | tf_op jit(solution)/shard_map/all_to_all | solution.py:532
  67.4 1.2 %reduce_sum.12 = bf16[48,512]{1,0:T(8,128)(2,1)S(1)} reduce(bf16[16,48,512]{2,1,0:T(8,128)(2,1)} %all-to-all-done.1, bf16[]{:T(256)} %constant.29.clone.1), dimensions={0}, to_apply=%region_0.0 | reduce | flops 368640 | bytes 835586 | tf_op jit(solution)/shard_map/reduce_sum | solution.py:559
  68.7 13.9 %all_to_all.26.parts_ref = bf16[8,48,512]{2,1,0:T(8,128)(2,1)S(1)} all-to-all(bf16[8,48,512]{2,1,0:T(8,128)(2,1)S(1)} %broadcast_in_dim.11), channel_id=1, replica_groups=mesh['x'=4,'z'=8,'yh'=2,'core'=2,'yl'=2] {'z'}, dimensions={0} | all-to-all | bytes 786432 | tf_op jit(solution)/shard_map/all_to_all | solution.py:532
  82.5 0.9 owner_step.1
  83.5 17.5 %all_to_all.27.blocks_ref = bf16[16,48,512]{2,1,0:T(8,128)(2,1)S(1)} all-to-all(bf16[16,48,512]{2,1,0:T(8,128)(2,1)S(1)} %owner_step.1), channel_id=1, replica_groups=mesh['x'=4,'z'=8,'yh'=2,'core'=2,'yl'=2] {'x','yh','yl'}, dimensions={0} | all-to-all | bytes 1572864 | tf_op jit(solution)/shard_map/all_to_all | solution.py:532
  100.9 4.0 %collective-permute-start.2 = (bf16[16,48,512]{2,1,0:T(8,128)(2,1)S(1)}, bf16[16,48,512]{2,1,0:T(8,128)(2,1)S(1)}, u32[]{:S(2)}, u32[]{:S(2)}) collective-permute-start(bf16[16,48,512]{2,1,0:T(8,128)(2,1)S(1)} %all_to_all.27.blocks_ref), channel_id=1, source_target_pairs={{0,2},{2,0},{1,3},{3,1},{4,6},{6,4},{5,7},{7,5},{8,10},{10,8},{9,1... | collective-permute-start | bytes 2359304 | tf_op jit(solution)/shard_map/ppermute | solution.py:536
  104.9 2.7 %final_near.1 = (bf16[1536,512]{1,0:T(8,128)(2,1)}, f32[768,512]{1,0:T(8,128)}, f32[768,512]{1,0:T(8,128)}, bf16[384,512]{1,0:T(8,128)(2,1)S(1)}) custom-call(s32[1]{0:T(128)} %bitcast._.me_ref, bf16[16,48,512]{2,1,0:T(8,128)(2,1)S(1)} %all_to_all.27.blocks_ref, bf16[1536,512]{1,0:T(8,128)(2,1)} %refs_0_.1, f32[768,512]{1,0:T(8,128)S(1)} %get-tuple-element.46.mh_ref.refs_1_, ...), custom_call_target="tpu_custom_call" | custom-call | tf_op jit(solution)/shard_map/final_near/pallas_call | solution.py:516
  107.6 0.0 collective-permute-done.2.blocks_ref
  107.7 1.6 %final_far.1 = (bf16[1536,512]{1,0:T(8,128)(2,1)}, f32[768,512]{1,0:T(8,128)}, f32[768,512]{1,0:T(8,128)}) custom-call(s32[1]{0:T(128)} %bitcast._.me_ref, bf16[16,48,512]{2,1,0:T(8,128)(2,1)S(1)} %collective-permute-done.2.blocks_ref, bf16[384,512]{1,0:T(8,128)(2,1)S(1)} %get-tuple-element.48.refs_0_, ...), custom_call_target="tpu_custom_call", output_to_operand_aliasing={{0}: (5, {}), {1}: (6, {}), {2}: (7, {})} | custom-call | tf_op jit(solution)/shard_map/final_far/pallas_call | solution.py:516
  (1 shorter events, 0.0 us)
Async XLA Ops:
  8.9 4.2 %collective-permute-start = (f32[128,128]{1,0:T(8,128)S(1)}, f32[128,128]{1,0:T(8,128)S(1)}, u32[]{:S(2)}, u32[]{:S(2)}) collective-permute-start(f32[128,128]{1,0:T(8,128)S(1)} %get-tuple-element.40), channel_id=1, source_target_pairs={{0,2},{2,0},{1,3},{3,1},{4,6},{6,4},{5,7},{7,5},{8,10},{10,8},{9,1... | collective-permute-start | bytes 196616 | tf_op jit(solution)/shard_map/ppermute | solution.py:536
  13.8 24.3 %all-to-all-start = ((f32[128,1,128]{2,1,0:T(1,128)}), f32[128,1,128]{2,1,0:T(1,128)S(1)}, u32[]{:S(2)}, u32[]{:S(2)}) async-start(f32[128,1,128]{2,1,0:T(1,128)} %bitcast.6), calls=%async_computation | async-start | bytes 131072 | tf_op jit(solution)/shard_map/all_to_all | solution.py:532
  45.4 3.8 %collective-permute-start.1 = (bf16[16,48,512]{2,1,0:T(8,128)(2,1)S(1)}, bf16[16,48,512]{2,1,0:T(8,128)(2,1)S(1)}, u32[]{:S(2)}, u32[]{:S(2)}) collective-permute-start(bf16[16,48,512]{2,1,0:T(8,128)(2,1)S(1)} %slice_bitcast_fusion), channel_id=1, source_target_pairs={{0,2},{2,0},{1,3},{3,1},{4,6},{6,4},{5,7},{7,5},{8,10},{10,8},{9,1... | collective-permute-start | bytes 2359304 | tf_op jit(solution)/shard_map/ppermute | solution.py:536
  50.3 17.1 %all-to-all-start.1 = ((bf16[16,48,512]{2,1,0:T(8,128)(2,1)}), bf16[16,48,512]{2,1,0:T(8,128)(2,1)}, u32[]{:S(2)}, u32[]{:S(2)}) async-start(bf16[16,48,512]{2,1,0:T(8,128)(2,1)} %fusion), calls=%async_computation.1 | async-start | bytes 1572864 | tf_op jit(solution)/shard_map/all_to_all | solution.py:532
  100.9 6.7 %collective-permute-start.2 = (bf16[16,48,512]{2,1,0:T(8,128)(2,1)S(1)}, bf16[16,48,512]{2,1,0:T(8,128)(2,1)S(1)}, u32[]{:S(2)}, u32[]{:S(2)}) collective-permute-start(bf16[16,48,512]{2,1,0:T(8,128)(2,1)S(1)} %all_to_all.27.blocks_ref), channel_id=1, source_target_pairs={{0,2},{2,0},{1,3},{3,1},{4,6},{6,4},{5,7},{7,5},{8,10},{10,8},{9,1... | collective-permute-start | bytes 2359304 | tf_op jit(solution)/shard_map/ppermute | solution.py:536

commit v4 on v3

--- a/solution.py
+++ b/solution.py
@@ -9,7 +9,6 @@
 from jax.sharding import PartitionSpec as P
 
 ALL = ("x", "z", "yh", "core", "yl")
-CHIPS = ("x", "z", "yh", "yl")
 PLANE = ("x", "yh", "yl")
 ROWS = 24
 ROW_STEP = 512
@@ -278,10 +277,9 @@
     w_copies = [
         copy(w_hbm.at[pl.ds(k * width, width)], w_ref.at[pl.ds(k * width, width)], w_sem.at[k]) for k in range(3)
     ]
-    kept = [
-        copy(m_hbm, mh_ref, keep_sem.at[0]),
-        copy(v_hbm, vh_ref, keep_sem.at[1]),
-    ]
+    side_rows = mh_ref.shape[0]
+    near = pl.ds(pl.multiple_of((me_ref[0] // 2) % 2 * side_rows, side_rows), side_rows)
+    kept = [copy(m_hbm.at[near], mh_ref, keep_sem.at[0]), copy(v_hbm.at[near], vh_ref, keep_sem.at[1])]
     d_copies = [copy(d_hbm.at[f], d_ref.at[f], d_sem.at[f]) for f in range(frames)]
     for i in range(frames):
         d_copies[frames - 1 - i].start()
@@ -308,11 +306,12 @@
         one.wait()
 
 
-def updated(weight, first, second, grad):
-    first_out = 0.9 * first + 0.1 * grad
-    second_out = 0.99 * second + 0.01 * grad * grad
-    new = (weight - 0.001 * first_out / (jnp.sqrt(second_out) + 1e-08)).astype(BF16)
-    return new, first_out, second_out
+def moments(first, second, grad):
+    return 0.9 * first + 0.1 * grad, 0.99 * second + 0.01 * grad * grad
+
+
+def stepped(weight, first_out, second_out):
+    return (weight - 0.001 * first_out / (jnp.sqrt(second_out) + 1e-08)).astype(BF16)
 
 
 def block_kernel(me_ref, parts_ref, w_hbm, mh_ref, vh_ref, send_ref, w_ref, w_sem):
@@ -321,70 +320,90 @@
     core = (me // 2) % 2
     slot = (me // 64) * 2 + (me // 4) % 2
     block = parts_ref.shape[1]
-    start = core * 8 * block + slot * block
-    rows = pl.ds(pl.multiple_of(start, block), block)
-    arriving = copy(w_hbm.at[pl.ds(pl.multiple_of(half * mh_ref.shape[0] + start, block), block)], w_ref, w_sem)
+    side_rows = mh_ref.shape[0]
+    rows = pl.ds(pl.multiple_of(slot * block, block), block)
+    start = half * 2 * side_rows + core * side_rows + slot * block
+    arriving = copy(w_hbm.at[pl.ds(pl.multiple_of(start, block), block)], w_ref, w_sem)
     arriving.start()
     grad = jnp.sum(parts_ref[...].astype(F32), axis=0).astype(BF16)
+    first_out, second_out = moments(mh_ref[rows, :], vh_ref[rows, :], grad.astype(F32))
     arriving.wait()
-    new, _, _ = updated(w_ref[...].astype(F32), mh_ref[rows, :], vh_ref[rows, :], grad.astype(F32))
+    new = stepped(w_ref[...].astype(F32), first_out, second_out)
     for d in range(0, send_ref.shape[0], 2):
         send_ref[d + half] = grad
         send_ref[d + 1 - half] = new
 
 
-def final_kernel(side, me_ref, blocks_ref, *refs):
+def final_kernel(side, me_ref, blocks_ref, w_in, mh_ref, vh_ref, *refs):
     half = me_ref[0] % 2
     core = (me_ref[0] // 2) % 2
     owner = core if side == 0 else 1 - core
     slots, block, width = blocks_ref.shape
+    side_rows = mh_ref.shape[0]
+    owned = 2 * side_rows
+    start = pl.multiple_of(owner * side_rows, side_rows)
+    pending = []
     if side == 0:
-        w_hbm, mh_ref, vh_ref = refs[:3]
-        new_hbm, first_hbm, second_hbm, w_next, new_ref, first_ref, second_ref, w_ref, sem, other_sem, w_sem = refs[3:]
+        m_hbm, v_hbm, new_hbm, first_hbm, second_hbm, w_next, m_next, v_next = refs[:8]
+        new_ref, first_ref, second_ref, w_ref, sem, other_sem, w_sem = refs[8:]
+        other = pl.ds(pl.multiple_of((1 - owner) * side_rows, side_rows), side_rows)
+        other_w = pl.ds(pl.multiple_of(half * owned + (1 - owner) * side_rows, side_rows), side_rows)
+        own_w = pl.ds(pl.multiple_of(half * owned + start, side_rows), side_rows)
+        near_w = copy(w_in.at[own_w], w_ref, w_sem.at[0])
+        near_w.start()
+        pending = [
+            copy(w_in.at[other_w], w_next, w_sem.at[1]),
+            copy(m_hbm.at[other], m_next, w_sem.at[2]),
+            copy(v_hbm.at[other], v_next, w_sem.at[3]),
+        ]
+        for one in pending:
+            one.start()
     else:
-        w_ref, mh_ref, vh_ref = refs[:3]
-        new_hbm, first_hbm, second_hbm, new_ref, first_ref, second_ref, sem, other_sem = refs[6:]
-    owned = mh_ref.shape[0]
-    side_rows = owned // 2
-    start = pl.multiple_of(owner * side_rows, side_rows)
-    if side == 0:
-        next_start = pl.multiple_of(half * owned + (1 - owner) * side_rows, side_rows)
-        near_w = copy(w_hbm.at[pl.ds(pl.multiple_of(half * owned + start, side_rows), side_rows)], w_ref, w_sem.at[0])
-        far_w = copy(w_hbm.at[pl.ds(next_start, side_rows)], w_next, w_sem.at[1])
-        near_w.start()
-        far_w.start()
+        new_hbm, first_hbm, second_hbm, new_ref, first_ref, second_ref, sem, other_sem = refs[3:]
+        w_ref = w_in
     sent = []
     for slot in range(slots // 2):
         peer = pl.multiple_of((1 - half) * owned + start + slot * block, block)
         sent.append(copy(blocks_ref.at[slot * 2 + 1 - half], new_hbm.at[pl.ds(peer, block)], other_sem.at[slot]))
         sent[-1].start()
+    per = 2
+    rows = per * block
+    chunks = slots // 2 // per
+
+    def first_part(chunk):
+        for slot in range(chunk * per, (chunk + 1) * per):
+            here = slice(slot * block, (slot + 1) * block)
+            grad = blocks_ref[slot * 2 + half].astype(F32)
+            first_out, second_out = moments(mh_ref[here, :], vh_ref[here, :], grad)
+            first_ref[here, :] = first_out
+            second_ref[here, :] = second_out
+            if side == 1:
+                new_ref[here, :] = stepped(w_ref[here, :].astype(F32), first_out, second_out)
+        far = pl.ds(pl.multiple_of(start + chunk * rows, rows), rows)
+        for i, (source, target) in enumerate([(first_ref, first_hbm), (second_ref, second_hbm)]):
+            one = copy(source.at[pl.ds(chunk * rows, rows)], target.at[far], sem.at[chunk, i])
+            one.start()
+            sent.append(one)
+
+    def second_part(chunk):
+        for slot in range(chunk * per, (chunk + 1) * per) if side == 0 else ():
+            here = slice(slot * block, (slot + 1) * block)
+            new_ref[here, :] = stepped(w_ref[here, :].astype(F32), first_ref[here, :], second_ref[here, :])
+        mine = pl.ds(pl.multiple_of(half * owned + start + chunk * rows, rows), rows)
+        one = copy(new_ref.at[pl.ds(chunk * rows, rows)], new_hbm.at[mine], sem.at[chunk, 2])
+        one.start()
+        sent.append(one)
+
+    for chunk in range(chunks):
+        first_part(chunk)
+        if side == 1:
+            second_part(chunk)
     if side == 0:
         near_w.wait()
-    per = 2
-    rows = per * block
-    for chunk in range(slots // 2 // per):
-        for j in range(per):
-            slot = chunk * per + j
-            part = pl.ds(pl.multiple_of(start + slot * block, block), block)
-            here = pl.ds(slot * block, block)
-            grad = blocks_ref[slot * 2 + half].astype(F32)
-            new, first_out, second_out = updated(w_ref[here, :].astype(F32), mh_ref[part, :], vh_ref[part, :], grad)
-            new_ref[here, :] = new
-            first_ref[here, :] = first_out
-            second_ref[here, :] = second_out
-        local = pl.ds(chunk * rows, rows)
-        far = pl.ds(pl.multiple_of(start + chunk * rows, rows), rows)
-        mine = pl.ds(pl.multiple_of(half * owned + start + chunk * rows, rows), rows)
-        for i, (source, target, place) in enumerate(
-            [(new_ref, new_hbm, mine), (first_ref, first_hbm, far), (second_ref, second_hbm, far)]
-        ):
-            one = copy(source.at[local], target.at[place], sem.at[chunk, i])
-            one.start()
-            sent.append(one)
-    for one in sent:
+        for chunk in range(chunks):
+            second_part(chunk)
+    for one in sent + pending:
         one.wait()
-    if side == 0:
-        far_w.wait()
 
 
 SCALAR = pl.BlockSpec(memory_space=pltpu.SMEM)
@@ -471,7 +490,7 @@
 
 def run_input(me, d_conv, weight, first, second, shape):
     batch, frames = shape[:2]
-    owned = first.shape
+    owned = (first.shape[0] // 2, first.shape[1])
     return pl.pallas_call(
         input_kernel,
         in_specs=[SCALAR] + [FAR] * 4,
@@ -502,30 +521,40 @@
     )(me, local(parts), remote(weight), *[local(a) for a in kept])
 
 
-def run_final(side, me, blocks, weight, kept, carried):
-    owned, width = kept[0].shape
-    shapes = [((2 * owned, width), BF16), ((owned, width), F32), ((owned, width), F32)]
+def run_near(me, blocks, weight, first, second, kept):
+    owned, width = first.shape
     half = (owned // 2, width)
-    outs = [pltpu.HBM(s, t) for s, t in shapes]
-    scratch = [pltpu.VMEM(half, BF16), pltpu.VMEM(half, F32), pltpu.VMEM(half, F32)]
-    sems = [DMA((4, 3)), DMA((8,))]
-    if side == 0:
-        outs.append(pltpu.VMEM(half, BF16))
-        scratch.append(pltpu.VMEM(half, BF16))
-        sems.append(DMA((2,)))
     return pl.pallas_call(
-        functools.partial(final_kernel, side),
-        in_specs=[SCALAR, NEAR, FAR if side == 0 else NEAR, NEAR, NEAR] + [FAR] * len(carried),
-        out_specs=[FAR] * 3 + [NEAR] * (1 - side),
-        out_shape=outs,
-        scratch_shapes=scratch + sems,
-        input_output_aliases={5 + i: i for i in range(len(carried))},
+        functools.partial(final_kernel, 0),
+        in_specs=[SCALAR, NEAR, FAR, NEAR, NEAR, FAR, FAR],
+        out_specs=[FAR] * 3 + [NEAR] * 3,
+        out_shape=[
+            pltpu.HBM(weight.shape, BF16), pltpu.HBM(first.shape, F32), pltpu.HBM(first.shape, F32),
+            pltpu.VMEM(half, BF16), pltpu.VMEM(half, F32), pltpu.VMEM(half, F32),
+        ],
+        scratch_shapes=[
+            pltpu.VMEM(half, BF16), pltpu.VMEM(half, F32), pltpu.VMEM(half, F32), pltpu.VMEM(half, BF16),
+            DMA((4, 3)), DMA((8,)), DMA((4,)),
+        ],
         compiler_params=PARAMS,
-        name="final_near" if side == 0 else "final_far",
-    )(
-        me, local(blocks), (remote if side == 0 else local)(weight),
-        *[local(a) for a in kept], *[remote(a) for a in carried],
-    )
+        name="final_near",
+    )(me, local(blocks), remote(weight), *[local(a) for a in kept], remote(first), remote(second))
+
+
+def run_far(me, blocks, saved, carried):
+    half = saved[0].shape
+    return pl.pallas_call(
+        functools.partial(final_kernel, 1),
+        in_specs=[SCALAR] + [NEAR] * 4 + [FAR] * 3,
+        out_specs=[FAR] * 3,
+        out_shape=[pltpu.HBM(a.shape, a.dtype) for a in carried],
+        scratch_shapes=[
+            pltpu.VMEM(half, BF16), pltpu.VMEM(half, F32), pltpu.VMEM(half, F32), DMA((4, 3)), DMA((8,)),
+        ],
+        input_output_aliases={5 + i: i for i in range(3)},
+        compiler_params=PARAMS,
+        name="final_far",
+    )(me, *[local(a) for a in (blocks, *saved)], *[remote(a) for a in carried])
 
 
 def spread(value, axes):
@@ -545,9 +574,9 @@
     me = lax.axis_index(ALL).astype(jnp.int32).reshape(1)
     cotangent = code_grad.transpose(1, 3, 0, 2)
     hidden, raw, inv, bias, cot, ag, stats = run_forward(
-        me, clips, conv_weight, proj_weight.T, norm_gain[None, :], code_bias[None, :], rotation, cotangent, lax.axis_size(CHIPS)
+        me, clips, conv_weight, proj_weight.T, norm_gain[None, :], code_bias[None, :], rotation, cotangent, devices
     )
-    parts = spread(stats + swapped(stats), CHIPS)
+    parts = spread(stats, ALL)
     saved = run_window(clips, hidden, raw, inv, bias, cot)
     d_conv, both, loss = run_backward(
         bits, clip_count, token_count, me, saved, ag, parts, conv_weight.shape[0]
@@ -560,8 +589,8 @@
     tower = spread(jnp.broadcast_to(column, (lax.axis_size("z"), *column.shape)), "z")
     near = spread(run_block(me, tower, conv_weight, kept), PLANE)
     far = swapped(near)
-    *carried, w_far = run_final(0, me, near, conv_weight, kept, [])
-    new_weight, first_out, second_out = run_final(1, me, far, w_far, kept, carried)
+    outs = run_near(me, near, conv_weight, first_moment, second_moment, kept)
+    new_weight, first_out, second_out = run_far(me, far, outs[3:], outs[:3])
     return new_weight, first_out, second_out, input_grad, loss[0, 0]
 
 

time: 110 us -> 107 us (0.973)
  starting transfers between devices: 27.4 us -> 24.2 us
  other arithmetic: 3.01 us -> 1.24 us
  waiting for transfers between devices: 14.1 us -> 15.6 us
  Pallas kernels: 32.6 us -> 34 us
    ppermute x3 -> x2, starting transfers between devices: 9.09 us -> 4.72 us  [swapped(): return lax.ppermute(value, 'core', [(0, 1), (1, 0)])]
    all_to_all x2, waiting for transfers between devices: 11.3 us -> 13.7 us  [spread(): return lax.all_to_all(value, axes, 0, 0, tiled=True)]
    all_to_all x2, starting transfers between devices: 18.3 us -> 19.4 us  [spread(): return lax.all_to_all(value, axes, 0, 0, tiled=True)]
    reduce_sum x1, other arithmetic: 1.25 us -> 0.11 us  [on_device(): column = jnp.sum(plane.astype(F32), axis=0).astype(BF16)]
    ppermute x3 -> x2, waiting for transfers between devices: 2.82 us -> 1.91 us  [swapped(): return lax.ppermute(value, 'core', [(0, 1), (1, 0)])]
  transfers between devices with their start and end apart: 5 -> 4, of which waited for: 4 -> 3; matrix products, arithmetic and copies ran while one was open for 0% -> 0% of each run, Pallas kernels for 13% -> 13%
where the time goes in v4:
time: 107 us
  Pallas kernels  34 us (32%)
  blocking collectives  31 us (29%)
  starting transfers between devices  24.2 us (23%)
  waiting for transfers between devices  15.6 us (15%)
  other arithmetic  1.24 us (1%)
    all_to_all x2, blocking collectives, spread(): return lax.all_to_all(value, axes, 0, 0, tiled=True)  31 us
    all_to_all x2, starting transfers between devices, spread(): return lax.all_to_all(value, axes, 0, 0, tiled=True)  19.4 us
    all_to_all x2, waiting for transfers between devices, spread(): return lax.all_to_all(value, axes, 0, 0, tiled=True)  13.7 us
    pallas_call x1, Pallas kernels, run_forward(): pl.pallas_call(forward_kernel, in_specs=[SCALAR] + [FAR] * 7, out_specs=[...  8.95 us
    pallas_call x1, Pallas kernels, run_backward(): pl.pallas_call(functools.partial(backward_kernel, bits, clip_count, token...  8.15 us
    pallas_call x1, Pallas kernels, run_input(): pl.pallas_call(input_kernel, in_specs=[SCALAR] + [FAR] * 4, out_specs=[FA...  6.58 us
    pallas_call x1, Pallas kernels, run_window(): pl.pallas_call(window_kernel, in_specs=[FAR] + [NEAR] * 5, out_specs=[FAR...  5.23 us
    ppermute x2, starting transfers between devices, swapped(): return lax.ppermute(value, 'core', [(0, 1), (1, 0)])  4.72 us
  transfers between devices with their start and end apart: 4, of which 3 were waited for; matrix products, arithmetic and copies ran while one was open for 0% of the time, Pallas kernels for 13%

profile of v4, /device:TPU:1, one launch (start us, length us, event | category | flops | bytes accessed | tf_op | source)
XLA Modules:
  0.0 107.1 jit_solution(11762813019250058909)
XLA Ops:
  0.6 8.9 %forward.1 = (bf16[5,512,512]{2,1,0:T(8,128)(2,1)S(1)}, f32[5,24,512]{2,1,0:T(8,128)S(1)}, f32[5,8,512]{2,1,0:T(8,128)S(1)}, f32[24,128]{1,0:T(8,128)S(1)}, f32[...) custom-call(s32[1]{0:T(128)} %bitcast._.me_ref, bf16[2,5,256,512]{3,2,1,0:T(8,128)(2,1)} %x_hbm.3, ...), custom_call_target="tpu_custom_call" | custom-call | tf_op jit(solution)/shard_map/forward/pallas_call | solution.py:433
  9.6 15.7 %all-to-all-start = ((f32[256,1,128]{2,1,0:T(1,128)}), f32[256,1,128]{2,1,0:T(1,128)S(1)}, u32[]{:S(2)}, u32[]{:S(2)}) async-start(f32[256,1,128]{2,1,0:T(1,128)} %bitcast.6), calls=%async_computation | async-start | bytes 262144 | tf_op jit(solution)/shard_map/all_to_all | solution.py:561
  25.3 5.2 %window.1 = (bf16[5,512,512]{2,1,0:T(8,128)(2,1)}, bf16[512,2560]{1,0:T(8,128)(2,1)}, f32[5,3,24,512]{3,2,1,0:T(8,128)}) custom-call(bf16[2,5,256,512]{3,2,1,0:T(8,128)(2,1)} %x_hbm.3, bf16[5,512,512]{2,1,0:T(8,128)(2,1)S(1)} %get-tuple-element.33.h_ref, f32[5,24,512]{2,1,0:T(8,128)S(1)} %get-tuple-element.34.raw_ref, ...), custom_call_target="tpu_custom_call" | custom-call | tf_op jit(solution)/shard_map/window/pallas_call | solution.py:452
  30.5 7.7 %all-to-all-done = f32[256,1,128]{2,1,0:T(1,128)S(1)} async-done(((f32[256,1,128]{2,1,0:T(1,128)}), f32[256,1,128]{2,1,0:T(1,128)S(1)}, u32[]{:S(2)}, u32[]{:S(2)}) %all-to-all-start) | async-done | bytes 131104 | tf_op jit(solution)/shard_map/all_to_all | solution.py:561
  38.2 8.1 %backward.1 = (bf16[5,512,512]{2,1,0:T(8,128)(2,1)}, bf16[2,16,48,512]{3,2,1,0:T(8,128)(2,1)S(1)}, f32[1,1]{1,0:T(1,128)}) custom-call(s32[1]{0:T(128)} %bitcast._.me_ref, bf16[5,512,512]{2,1,0:T(8,128)(2,1)} %get-tuple-element.38.h_hbm, bf16[512,2560]{1,0:T(8,128)(2,1)} %get-tuple-element.39.xt_hbm, f32[5,3,24,512]{3,2,1,0:T(8,128)} %get-tuple-element.40.rows_hbm, ...), custom_call_target="tpu_custom_call" | custom-call | tf_op jit(solution)/shard_map/backward/pallas_call | solution.py:472
  46.4 0.1 slice_bitcast_fusion
  46.5 0.6 collective-permute-start
  47.1 1.9 %collective-permute-done = bf16[16,48,512]{2,1,0:T(8,128)(2,1)S(1)} collective-permute-done((bf16[16,48,512]{2,1,0:T(8,128)(2,1)S(1)}, bf16[16,48,512]{2,1,0:T(8,128)(2,1)S(1)}, u32[]{:S(2)}, u32[]{:S(2)}) %collective-permute-start) | collective-permute-done | bytes 786464 | tf_op jit(solution)/shard_map/ppermute | solution.py:565
  49.0 1.1 %fusion = bf16[16,48,512]{2,1,0:T(8,128)(2,1)} fusion(bf16[16,48,512]{2,1,0:T(8,128)(2,1)S(1)} %collective-permute-done, bf16[2,16,48,512]{3,2,1,0:T(8,128)(2,1)S(1)} %get-tuple-element.43), kind=kLoop, calls=%fused_computation.1 | loop fusion | flops 1572864 | bytes 2359296 | tf_op jit(solution)/shard_map/convert_element_type | solution.py:584
  50.1 3.8 %all-to-all-start.1 = ((bf16[16,48,512]{2,1,0:T(8,128)(2,1)}), bf16[16,48,512]{2,1,0:T(8,128)(2,1)S(1)}, u32[]{:S(2)}, u32[]{:S(2)}) async-start(bf16[16,48,512]{2,1,0:T(8,128)(2,1)} %fusion), calls=%async_computation.1 | async-start | bytes 1572864 | tf_op jit(solution)/shard_map/all_to_all | solution.py:561
  53.9 6.6 %input_grad.1 = (bf16[2,5,256,512]{3,2,1,0:T(8,128)(2,1)}, f32[384,512]{1,0:T(8,128)S(1)}, f32[384,512]{1,0:T(8,128)S(1)}) custom-call(s32[1]{0:T(128)} %bitcast._.me_ref, bf16[5,512,512]{2,1,0:T(8,128)(2,1)} %get-tuple-element.44.d_hbm, bf16[1536,512]{1,0:T(8,128)(2,1)} %w_in.1, f32[768,512]{1,0:T(8,128)} %refs_0_.1, f32[768,512]{1,0:T(8,128)} %refs_1_.1), custom_call_target="tpu_custom_call" | custom-call | tf_op jit(solution)/shard_map/input_grad/pallas_call | solution.py:494
  60.5 6.0 %all-to-all-done.1 = bf16[16,48,512]{2,1,0:T(8,128)(2,1)S(1)} async-done(((bf16[16,48,512]{2,1,0:T(8,128)(2,1)}), bf16[16,48,512]{2,1,0:T(8,128)(2,1)S(1)}, u32[]{:S(2)}, u32[]{:S(2)}) %all-to-all-start.1) | async-done | bytes 786464 | tf_op jit(solution)/shard_map/all_to_all | solution.py:561
  66.5 0.1 reduce_sum.12
  66.6 13.8 %all_to_all.26.parts_ref = bf16[8,48,512]{2,1,0:T(8,128)(2,1)S(1)} all-to-all(bf16[8,48,512]{2,1,0:T(8,128)(2,1)S(1)} %broadcast_in_dim.11), channel_id=1, replica_groups=mesh['x'=4,'z'=8,'yh'=2,'core'=2,'yl'=2] {'z'}, dimensions={0} | all-to-all | bytes 786432 | tf_op jit(solution)/shard_map/all_to_all | solution.py:561
  80.5 0.9 owner_step.1
  81.4 17.2 %all_to_all.27.blocks_ref = bf16[16,48,512]{2,1,0:T(8,128)(2,1)S(1)} all-to-all(bf16[16,48,512]{2,1,0:T(8,128)(2,1)S(1)} %owner_step.1), channel_id=1, replica_groups=mesh['x'=4,'z'=8,'yh'=2,'core'=2,'yl'=2] {'x','yh','yl'}, dimensions={0} | all-to-all | bytes 1572864 | tf_op jit(solution)/shard_map/all_to_all | solution.py:561
  98.6 4.1 %collective-permute-start.1 = (bf16[16,48,512]{2,1,0:T(8,128)(2,1)S(1)}, bf16[16,48,512]{2,1,0:T(8,128)(2,1)S(1)}, u32[]{:S(2)}, u32[]{:S(2)}) collective-permute-start(bf16[16,48,512]{2,1,0:T(8,128)(2,1)S(1)} %all_to_all.27.blocks_ref), channel_id=1, source_target_pairs={{0,2},{2,0},{1,3},{3,1},{4,6},{6,4},{5,7},{7,5},{8,10},{10,8},{9,1... | collective-permute-start | bytes 2359304 | tf_op jit(solution)/shard_map/ppermute | solution.py:565
  102.7 2.6 %final_near.1 = (bf16[1536,512]{1,0:T(8,128)(2,1)}, f32[768,512]{1,0:T(8,128)}, f32[768,512]{1,0:T(8,128)}, bf16[384,512]{1,0:T(8,128)(2,1)S(1)}, f32[384,512]{1,0:T(8,128)S(1)}, /*index=5*/f32[384,512]{1,0:T(8,128)S(1)}) custom-call(s32[1]{0:T(128)} %bitcast._.me_ref, bf16[16,48,512]{2,1,0:T(8,128)(2,1)S(1)} %all_to_all.27.blocks_ref, ...), custom_call_target="tpu_custom_call" | custom-call | tf_op jit(solution)/shard_map/final_near/pallas_call | solution.py:527
  105.3 0.0 collective-permute-done.1.blocks_ref
  105.3 1.6 %final_far.1 = (bf16[1536,512]{1,0:T(8,128)(2,1)}, f32[768,512]{1,0:T(8,128)}, f32[768,512]{1,0:T(8,128)}) custom-call(s32[1]{0:T(128)} %bitcast._.me_ref, bf16[16,48,512]{2,1,0:T(8,128)(2,1)S(1)} %collective-permute-done.1.blocks_ref, bf16[384,512]{1,0:T(8,128)(2,1)S(1)} %get-tuple-element.50.w_in, ...), custom_call_target="tpu_custom_call", output_to_operand_aliasing={{0}: (5, {}), {1}: (6, {}), {2}: (7, {})} | custom-call | tf_op jit(solution)/shard_map/final_far/pallas_call | solution.py:546
  (1 shorter events, 0.0 us)
Async XLA Ops:
  9.6 28.6 %all-to-all-start = ((f32[256,1,128]{2,1,0:T(1,128)}), f32[256,1,128]{2,1,0:T(1,128)S(1)}, u32[]{:S(2)}, u32[]{:S(2)}) async-start(f32[256,1,128]{2,1,0:T(1,128)} %bitcast.6), calls=%async_computation | async-start | bytes 262144 | tf_op jit(solution)/shard_map/all_to_all | solution.py:561
  46.5 2.5 %collective-permute-start = (bf16[16,48,512]{2,1,0:T(8,128)(2,1)S(1)}, bf16[16,48,512]{2,1,0:T(8,128)(2,1)S(1)}, u32[]{:S(2)}, u32[]{:S(2)}) collective-permute-start(bf16[16,48,512]{2,1,0:T(8,128)(2,1)S(1)} %slice_bitcast_fusion), channel_id=1, source_target_pairs={{0,2},{2,0},{1,3},{3,1},{4,6},{6,4},{5,7},{7,5},{8,10},{10,8},{9,1... | collective-permute-start | bytes 2359304 | tf_op jit(solution)/shard_map/ppermute | solution.py:565
  50.1 16.4 %all-to-all-start.1 = ((bf16[16,48,512]{2,1,0:T(8,128)(2,1)}), bf16[16,48,512]{2,1,0:T(8,128)(2,1)S(1)}, u32[]{:S(2)}, u32[]{:S(2)}) async-start(bf16[16,48,512]{2,1,0:T(8,128)(2,1)} %fusion), calls=%async_computation.1 | async-start | bytes 1572864 | tf_op jit(solution)/shard_map/all_to_all | solution.py:561
  98.6 6.8 %collective-permute-start.1 = (bf16[16,48,512]{2,1,0:T(8,128)(2,1)S(1)}, bf16[16,48,512]{2,1,0:T(8,128)(2,1)S(1)}, u32[]{:S(2)}, u32[]{:S(2)}) collective-permute-start(bf16[16,48,512]{2,1,0:T(8,128)(2,1)S(1)} %all_to_all.27.blocks_ref), channel_id=1, source_target_pairs={{0,2},{2,0},{1,3},{3,1},{4,6},{6,4},{5,7},{7,5},{8,10},{10,8},{9,1... | collective-permute-start | bytes 2359304 | tf_op jit(solution)/shard_map/ppermute | solution.py:565

commit v5 on v4

--- a/solution.py
+++ b/solution.py
@@ -8,8 +8,8 @@
 from jax.sharding import Mesh
 from jax.sharding import PartitionSpec as P
 
-ALL = ("x", "z", "yh", "core", "yl")
-PLANE = ("x", "yh", "yl")
+ALL = ("x", "zh", "zl", "yh", "core", "yl")
+PLANE = ("x", "zl", "yh", "yl")
 ROWS = 24
 ROW_STEP = 512
 COL_STEP = 512
@@ -261,7 +261,10 @@
             owner, inside = divmod(within, group)
             slot, offset = divmod(inside, block)
             where = core if owner == 0 else 1 - core
-            both_ref[where, slot * 2 + half, offset : offset + stop - row, :] = grad_ref[row:stop, :]
+            for z in range(2):
+                index = (slot // 2) * 8 + z * 4 + (slot % 2) * 2 + half
+                cols = slice(z * width // 2, (z + 1) * width // 2)
+                both_ref[where, index, offset : offset + stop - row, :] = grad_ref[row:stop, cols]
             row = stop
     for one in leaving:
         one.wait()
@@ -319,14 +322,17 @@
     half = me % 2
     core = (me // 2) % 2
     slot = (me // 64) * 2 + (me // 4) % 2
-    block = parts_ref.shape[1]
+    z_low = (me // 8) % 2
+    _, block, width = parts_ref.shape
     side_rows = mh_ref.shape[0]
     rows = pl.ds(pl.multiple_of(slot * block, block), block)
-    start = half * 2 * side_rows + core * side_rows + slot * block
-    arriving = copy(w_hbm.at[pl.ds(pl.multiple_of(start, block), block)], w_ref, w_sem)
+    start = pl.multiple_of(half * 2 * side_rows + core * side_rows + slot * block, block)
+    arriving = copy(w_hbm.at[pl.ds(start, block), pl.ds(pl.multiple_of(z_low * width, width), width)], w_ref, w_sem)
     arriving.start()
     grad = jnp.sum(parts_ref[...].astype(F32), axis=0).astype(BF16)
-    first_out, second_out = moments(mh_ref[rows, :], vh_ref[rows, :], grad.astype(F32))
+    first = jnp.where(z_low == 0, mh_ref[rows, :width], mh_ref[rows, width:])
+    second = jnp.where(z_low == 0, vh_ref[rows, :width], vh_ref[rows, width:])
+    first_out, second_out = moments(first, second, grad.astype(F32))
     arriving.wait()
     new = stepped(w_ref[...].astype(F32), first_out, second_out)
     for d in range(0, send_ref.shape[0], 2):
@@ -338,7 +344,8 @@
     half = me_ref[0] % 2
     core = (me_ref[0] // 2) % 2
     owner = core if side == 0 else 1 - core
-    slots, block, width = blocks_ref.shape
+    count, block, part_width = blocks_ref.shape
+    slots = count // 2
     side_rows = mh_ref.shape[0]
     owned = 2 * side_rows
     start = pl.multiple_of(owner * side_rows, side_rows)
@@ -363,9 +370,12 @@
         w_ref = w_in
     sent = []
     for slot in range(slots // 2):
-        peer = pl.multiple_of((1 - half) * owned + start + slot * block, block)
-        sent.append(copy(blocks_ref.at[slot * 2 + 1 - half], new_hbm.at[pl.ds(peer, block)], other_sem.at[slot]))
-        sent[-1].start()
+        peer = pl.ds(pl.multiple_of((1 - half) * owned + start + slot * block, block), block)
+        for z in range(2):
+            source = blocks_ref.at[(slot // 2) * 8 + z * 4 + (slot % 2) * 2 + 1 - half]
+            cols = pl.ds(z * part_width, part_width)
+            sent.append(copy(source, new_hbm.at[peer, cols], other_sem.at[slot, z]))
+            sent[-1].start()
     per = 2
     rows = per * block
     chunks = slots // 2 // per
@@ -373,7 +383,8 @@
     def first_part(chunk):
         for slot in range(chunk * per, (chunk + 1) * per):
             here = slice(slot * block, (slot + 1) * block)
-            grad = blocks_ref[slot * 2 + half].astype(F32)
+            index = (slot // 2) * 8 + (slot % 2) * 2 + half
+            grad = jnp.concatenate([blocks_ref[index], blocks_ref[index + 4]], axis=1).astype(F32)
             first_out, second_out = moments(mh_ref[here, :], vh_ref[here, :], grad)
             first_ref[here, :] = first_out
             second_ref[here, :] = second_out
@@ -468,7 +479,7 @@
 
 def run_backward(bits, clip_count, token_count, me, saved, ag, parts, row_count):
     width = saved[0].shape[2]
-    both = (2, 16, row_count // 32, width)
+    both = (2, 32, row_count // 32, width // 2)
     return pl.pallas_call(
         functools.partial(backward_kernel, bits, clip_count, token_count),
         in_specs=[SCALAR] + [FAR] * 3 + [NEAR] * 2,
@@ -509,7 +520,7 @@
 
 
 def run_block(me, parts, weight, kept):
-    send = (16, *parts.shape[1:])
+    send = (32, *parts.shape[1:])
     return pl.pallas_call(
         block_kernel,
         in_specs=[SCALAR, NEAR, FAR, NEAR, NEAR],
@@ -534,7 +545,7 @@
         ],
         scratch_shapes=[
             pltpu.VMEM(half, BF16), pltpu.VMEM(half, F32), pltpu.VMEM(half, F32), pltpu.VMEM(half, BF16),
-            DMA((4, 3)), DMA((8,)), DMA((4,)),
+            DMA((4, 3)), DMA((8, 2)), DMA((4,)),
         ],
         compiler_params=PARAMS,
         name="final_near",
@@ -549,7 +560,7 @@
         out_specs=[FAR] * 3,
         out_shape=[pltpu.HBM(a.shape, a.dtype) for a in carried],
         scratch_shapes=[
-            pltpu.VMEM(half, BF16), pltpu.VMEM(half, F32), pltpu.VMEM(half, F32), DMA((4, 3)), DMA((8,)),
+            pltpu.VMEM(half, BF16), pltpu.VMEM(half, F32), pltpu.VMEM(half, F32), DMA((4, 3)), DMA((8, 2)),
         ],
         input_output_aliases={5 + i: i for i in range(3)},
         compiler_params=PARAMS,
@@ -586,7 +597,7 @@
     input_grad, *kept = run_input(me, d_conv, conv_weight, first_moment, second_moment, clips.shape)
     plane, kept = lax.optimization_barrier((plane, kept))
     column = jnp.sum(plane.astype(F32), axis=0).astype(BF16)
-    tower = spread(jnp.broadcast_to(column, (lax.axis_size("z"), *column.shape)), "z")
+    tower = spread(jnp.broadcast_to(column, (lax.axis_size("zh"), *column.shape)), "zh")
     near = spread(run_block(me, tower, conv_weight, kept), PLANE)
     far = swapped(near)
     outs = run_near(me, near, conv_weight, first_moment, second_moment, kept)
@@ -595,7 +606,7 @@
 
 
 def solution(mesh):
-    finer = Mesh(mesh.devices.reshape(4, 8, 2, 2, mesh.shape["shard"]), ALL)
+    finer = Mesh(mesh.devices.reshape(4, 4, 2, 2, 2, mesh.shape["shard"]), ALL)
     split = P(ALL, None, None, None)
     in_specs = (split, split, P(), P(), P(), P(), P(), P("yl", None), P("yl", None))
     out_specs = (P(), P("yl", None), P("yl", None), split, P())

time: 107 us -> 102 us (0.953)
  blocking collectives: 31 us -> 24.2 us
    all_to_all x2, blocking collectives: 31 us -> 24.2 us  [spread(): return lax.all_to_all(value, axes, 0, 0, tiled=True)]
  transfers between devices with their start and end apart: 4 -> 4, of which waited for: 3 -> 3; matrix products, arithmetic and copies ran while one was open for 0% -> 0% of each run, Pallas kernels for 13% -> 14%
where the time goes in v5:
time: 102 us
  Pallas kernels  34.1 us (33%)
  starting transfers between devices  25.2 us (25%)
  blocking collectives  24.2 us (24%)
  waiting for transfers between devices  15.9 us (16%)
  other arithmetic  1.23 us (1%)
    all_to_all x2, blocking collectives, spread(): return lax.all_to_all(value, axes, 0, 0, tiled=True)  24.2 us
    all_to_all x2, starting transfers between devices, spread(): return lax.all_to_all(value, axes, 0, 0, tiled=True)  20 us
    all_to_all x2, waiting for transfers between devices, spread(): return lax.all_to_all(value, axes, 0, 0, tiled=True)  14 us
    pallas_call x1, Pallas kernels, run_forward(): pl.pallas_call(forward_kernel, in_specs=[SCALAR] + [FAR] * 7, out_specs=[...  8.94 us
    pallas_call x1, Pallas kernels, run_backward(): pl.pallas_call(functools.partial(backward_kernel, bits, clip_count, token...  8.15 us
    pallas_call x1, Pallas kernels, run_input(): pl.pallas_call(input_kernel, in_specs=[SCALAR] + [FAR] * 4, out_specs=[FA...  6.58 us
    ppermute x2, starting transfers between devices, swapped(): return lax.ppermute(value, 'core', [(0, 1), (1, 0)])  5.25 us
    pallas_call x1, Pallas kernels, run_window(): pl.pallas_call(window_kernel, in_specs=[FAR] + [NEAR] * 5, out_specs=[FAR...  5.23 us
  transfers between devices with their start and end apart: 4, of which 3 were waited for; matrix products, arithmetic and copies ran while one was open for 0% of the time, Pallas kernels for 14%

profile of v5, /device:TPU:1, one launch (start us, length us, event | category | flops | bytes accessed | tf_op | source)
XLA Modules:
  0.0 101.6 jit_solution(17398232067238687097)
XLA Ops:
  0.6 8.9 %forward.1 = (bf16[5,512,512]{2,1,0:T(8,128)(2,1)S(1)}, f32[5,24,512]{2,1,0:T(8,128)S(1)}, f32[5,8,512]{2,1,0:T(8,128)S(1)}, f32[24,128]{1,0:T(8,128)S(1)}, f32[...) custom-call(s32[1]{0:T(128)} %bitcast._.me_ref, bf16[2,5,256,512]{3,2,1,0:T(8,128)(2,1)} %x_hbm.3, ...), custom_call_target="tpu_custom_call" | custom-call | tf_op jit(solution)/shard_map/forward/pallas_call | solution.py:444
  9.6 15.7 %all-to-all-start = ((f32[256,1,128]{2,1,0:T(1,128)}), f32[256,1,128]{2,1,0:T(1,128)S(1)}, u32[]{:S(2)}, u32[]{:S(2)}) async-start(f32[256,1,128]{2,1,0:T(1,128)} %bitcast.6), calls=%async_computation | async-start | bytes 262144 | tf_op jit(solution)/shard_map/all_to_all | solution.py:572
  25.3 5.2 %window.1 = (bf16[5,512,512]{2,1,0:T(8,128)(2,1)}, bf16[512,2560]{1,0:T(8,128)(2,1)}, f32[5,3,24,512]{3,2,1,0:T(8,128)}) custom-call(bf16[2,5,256,512]{3,2,1,0:T(8,128)(2,1)} %x_hbm.3, bf16[5,512,512]{2,1,0:T(8,128)(2,1)S(1)} %get-tuple-element.33.h_ref, f32[5,24,512]{2,1,0:T(8,128)S(1)} %get-tuple-element.34.raw_ref, ...), custom_call_target="tpu_custom_call" | custom-call | tf_op jit(solution)/shard_map/window/pallas_call | solution.py:463
  30.5 7.7 %all-to-all-done = f32[256,1,128]{2,1,0:T(1,128)S(1)} async-done(((f32[256,1,128]{2,1,0:T(1,128)}), f32[256,1,128]{2,1,0:T(1,128)S(1)}, u32[]{:S(2)}, u32[]{:S(2)}) %all-to-all-start) | async-done | bytes 131104 | tf_op jit(solution)/shard_map/all_to_all | solution.py:572
  38.2 8.2 %backward.1 = (bf16[5,512,512]{2,1,0:T(8,128)(2,1)}, bf16[2,32,48,256]{3,2,1,0:T(8,128)(2,1)S(1)}, f32[1,1]{1,0:T(1,128)}) custom-call(s32[1]{0:T(128)} %bitcast._.me_ref, bf16[5,512,512]{2,1,0:T(8,128)(2,1)} %get-tuple-element.38.h_hbm, bf16[512,2560]{1,0:T(8,128)(2,1)} %get-tuple-element.39.xt_hbm, f32[5,3,24,512]{3,2,1,0:T(8,128)} %get-tuple-element.40.rows_hbm, ...), custom_call_target="tpu_custom_call" | custom-call | tf_op jit(solution)/shard_map/backward/pallas_call | solution.py:483
  46.4 0.1 slice_bitcast_fusion
  46.5 0.6 collective-permute-start
  47.1 1.9 %collective-permute-done = bf16[32,48,256]{2,1,0:T(8,128)(2,1)S(1)} collective-permute-done((bf16[32,48,256]{2,1,0:T(8,128)(2,1)S(1)}, bf16[32,48,256]{2,1,0:T(8,128)(2,1)S(1)}, u32[]{:S(2)}, u32[]{:S(2)}) %collective-permute-start) | collective-permute-done | bytes 786464 | tf_op jit(solution)/shard_map/ppermute | solution.py:576
  49.0 1.1 %fusion = bf16[32,48,256]{2,1,0:T(8,128)(2,1)} fusion(bf16[32,48,256]{2,1,0:T(8,128)(2,1)S(1)} %collective-permute-done, bf16[2,32,48,256]{3,2,1,0:T(8,128)(2,1)S(1)} %get-tuple-element.43), kind=kLoop, calls=%fused_computation.1 | loop fusion | flops 1572864 | bytes 2359296 | tf_op jit(solution)/shard_map/convert_element_type | solution.py:595
  50.1 4.3 %all-to-all-start.1 = ((bf16[32,48,256]{2,1,0:T(8,128)(2,1)}), bf16[32,48,256]{2,1,0:T(8,128)(2,1)S(1)}, u32[]{:S(2)}, u32[]{:S(2)}) async-start(bf16[32,48,256]{2,1,0:T(8,128)(2,1)} %fusion), calls=%async_computation.1 | async-start | bytes 1572864 | tf_op jit(solution)/shard_map/all_to_all | solution.py:572
  54.4 6.6 %input_grad.1 = (bf16[2,5,256,512]{3,2,1,0:T(8,128)(2,1)}, f32[384,512]{1,0:T(8,128)S(1)}, f32[384,512]{1,0:T(8,128)S(1)}) custom-call(s32[1]{0:T(128)} %bitcast._.me_ref, bf16[5,512,512]{2,1,0:T(8,128)(2,1)} %get-tuple-element.44.d_hbm, bf16[1536,512]{1,0:T(8,128)(2,1)} %w_in.1, f32[768,512]{1,0:T(8,128)} %refs_0_.1, f32[768,512]{1,0:T(8,128)} %refs_1_.1), custom_call_target="tpu_custom_call" | custom-call | tf_op jit(solution)/shard_map/input_grad/pallas_call | solution.py:505
  61.0 6.2 %all-to-all-done.1 = bf16[32,48,256]{2,1,0:T(8,128)(2,1)S(1)} async-done(((bf16[32,48,256]{2,1,0:T(8,128)(2,1)}), bf16[32,48,256]{2,1,0:T(8,128)(2,1)S(1)}, u32[]{:S(2)}, u32[]{:S(2)}) %all-to-all-start.1) | async-done | bytes 786464 | tf_op jit(solution)/shard_map/all_to_all | solution.py:572
  67.2 0.1 reduce_sum.12
  67.3 9.6 %all_to_all.26.parts_ref = bf16[4,48,256]{2,1,0:T(8,128)(2,1)S(1)} all-to-all(bf16[4,48,256]{2,1,0:T(8,128)(2,1)S(1)} %broadcast_in_dim.11), channel_id=1, replica_groups=mesh['x'=4,'zh'=4,'zl'=2,'yh'=2,'core'=2,'yl'=2] {'zh'}, dimensions={0} | all-to-all | bytes 196608 | tf_op jit(solution)/shard_map/all_to_all | solution.py:572
  76.9 0.9 owner_step.1
  77.8 14.6 %all_to_all.27.blocks_ref = bf16[32,48,256]{2,1,0:T(8,128)(2,1)S(1)} all-to-all(bf16[32,48,256]{2,1,0:T(8,128)(2,1)S(1)} %owner_step.1), channel_id=1, replica_groups=mesh['x'=4,'zh'=4,'zl'=2,'yh'=2,'core'=2,'yl'=2] {'x','zl','yh','yl'}, dimensions={0} | all-to-all | bytes 1572864 | tf_op jit(solution)/shard_map/all_to_all | solution.py:572
  92.4 4.7 %collective-permute-start.1 = (bf16[32,48,256]{2,1,0:T(8,128)(2,1)S(1)}, bf16[32,48,256]{2,1,0:T(8,128)(2,1)S(1)}, u32[]{:S(2)}, u32[]{:S(2)}) collective-permute-start(bf16[32,48,256]{2,1,0:T(8,128)(2,1)S(1)} %all_to_all.27.blocks_ref), channel_id=1, source_target_pairs={{0,2},{2,0},{1,3},{3,1},{4,6},{6,4},{5,7},{7,5},{8,10},{10,8},{9,1... | collective-permute-start | bytes 2359304 | tf_op jit(solution)/shard_map/ppermute | solution.py:576
  97.0 2.7 %final_near.1 = (bf16[1536,512]{1,0:T(8,128)(2,1)}, f32[768,512]{1,0:T(8,128)}, f32[768,512]{1,0:T(8,128)}, bf16[384,512]{1,0:T(8,128)(2,1)S(1)}, f32[384,512]{1,0:T(8,128)S(1)}, /*index=5*/f32[384,512]{1,0:T(8,128)S(1)}) custom-call(s32[1]{0:T(128)} %bitcast._.me_ref, bf16[32,48,256]{2,1,0:T(8,128)(2,1)S(1)} %all_to_all.27.blocks_ref, ...), custom_call_target="tpu_custom_call" | custom-call | tf_op jit(solution)/shard_map/final_near/pallas_call | solution.py:538
  99.8 0.0 collective-permute-done.1.blocks_ref
  99.8 1.6 %final_far.1 = (bf16[1536,512]{1,0:T(8,128)(2,1)}, f32[768,512]{1,0:T(8,128)}, f32[768,512]{1,0:T(8,128)}) custom-call(s32[1]{0:T(128)} %bitcast._.me_ref, bf16[32,48,256]{2,1,0:T(8,128)(2,1)S(1)} %collective-permute-done.1.blocks_ref, bf16[384,512]{1,0:T(8,128)(2,1)S(1)} %get-tuple-element.50.w_in, ...), custom_call_target="tpu_custom_call", output_to_operand_aliasing={{0}: (5, {}), {1}: (6, {}), {2}: (7, {})} | custom-call | tf_op jit(solution)/shard_map/final_far/pallas_call | solution.py:557
  (1 shorter events, 0.0 us)
Async XLA Ops:
  9.6 28.6 %all-to-all-start = ((f32[256,1,128]{2,1,0:T(1,128)}), f32[256,1,128]{2,1,0:T(1,128)S(1)}, u32[]{:S(2)}, u32[]{:S(2)}) async-start(f32[256,1,128]{2,1,0:T(1,128)} %bitcast.6), calls=%async_computation | async-start | bytes 262144 | tf_op jit(solution)/shard_map/all_to_all | solution.py:572
  46.5 2.5 %collective-permute-start = (bf16[32,48,256]{2,1,0:T(8,128)(2,1)S(1)}, bf16[32,48,256]{2,1,0:T(8,128)(2,1)S(1)}, u32[]{:S(2)}, u32[]{:S(2)}) collective-permute-start(bf16[32,48,256]{2,1,0:T(8,128)(2,1)S(1)} %slice_bitcast_fusion), channel_id=1, source_target_pairs={{0,2},{2,0},{1,3},{3,1},{4,6},{6,4},{5,7},{7,5},{8,10},{10,8},{9,1... | collective-permute-start | bytes 2359304 | tf_op jit(solution)/shard_map/ppermute | solution.py:576
  50.1 17.1 %all-to-all-start.1 = ((bf16[32,48,256]{2,1,0:T(8,128)(2,1)}), bf16[32,48,256]{2,1,0:T(8,128)(2,1)S(1)}, u32[]{:S(2)}, u32[]{:S(2)}) async-start(bf16[32,48,256]{2,1,0:T(8,128)(2,1)} %fusion), calls=%async_computation.1 | async-start | bytes 1572864 | tf_op jit(solution)/shard_map/all_to_all | solution.py:572
  92.4 7.4 %collective-permute-start.1 = (bf16[32,48,256]{2,1,0:T(8,128)(2,1)S(1)}, bf16[32,48,256]{2,1,0:T(8,128)(2,1)S(1)}, u32[]{:S(2)}, u32[]{:S(2)}) collective-permute-start(bf16[32,48,256]{2,1,0:T(8,128)(2,1)S(1)} %all_to_all.27.blocks_ref), channel_id=1, source_target_pairs={{0,2},{2,0},{1,3},{3,1},{4,6},{6,4},{5,7},{7,5},{8,10},{10,8},{9,1... | collective-permute-start | bytes 2359304 | tf_op jit(solution)/shard_map/ppermute | solution.py:576

commit v6 on v5

--- a/solution.py
+++ b/solution.py
@@ -272,7 +272,7 @@
 
 def input_kernel(
     me_ref, d_hbm, w_hbm, m_hbm, v_hbm,
-    out_hbm, mh_ref, vh_ref,
+    out_hbm, mh_ref, vh_ref, wh_ref,
     w_ref, out_ref, d_ref, w_sem, keep_sem, out_sem, d_sem,
 ):
     frames, tokens, width = d_hbm.shape
@@ -282,7 +282,13 @@
     ]
     side_rows = mh_ref.shape[0]
     near = pl.ds(pl.multiple_of((me_ref[0] // 2) % 2 * side_rows, side_rows), side_rows)
-    kept = [copy(m_hbm.at[near], mh_ref, keep_sem.at[0]), copy(v_hbm.at[near], vh_ref, keep_sem.at[1])]
+    near_w = me_ref[0] % 2 * 2 * side_rows + (me_ref[0] // 2) % 2 * side_rows
+    near_w = pl.ds(pl.multiple_of(near_w, side_rows), side_rows)
+    kept = [
+        copy(m_hbm.at[near], mh_ref, keep_sem.at[0]),
+        copy(v_hbm.at[near], vh_ref, keep_sem.at[1]),
+        copy(w_hbm.at[near_w], wh_ref, keep_sem.at[2]),
+    ]
     d_copies = [copy(d_hbm.at[f], d_ref.at[f], d_sem.at[f]) for f in range(frames)]
     for i in range(frames):
         d_copies[frames - 1 - i].start()
@@ -317,30 +323,25 @@
     return (weight - 0.001 * first_out / (jnp.sqrt(second_out) + 1e-08)).astype(BF16)
 
 
-def block_kernel(me_ref, parts_ref, w_hbm, mh_ref, vh_ref, send_ref, w_ref, w_sem):
+def block_kernel(me_ref, parts_ref, mh_ref, vh_ref, wh_ref, send_ref):
     me = me_ref[0]
     half = me % 2
-    core = (me // 2) % 2
     slot = (me // 64) * 2 + (me // 4) % 2
     z_low = (me // 8) % 2
     _, block, width = parts_ref.shape
-    side_rows = mh_ref.shape[0]
     rows = pl.ds(pl.multiple_of(slot * block, block), block)
-    start = pl.multiple_of(half * 2 * side_rows + core * side_rows + slot * block, block)
-    arriving = copy(w_hbm.at[pl.ds(start, block), pl.ds(pl.multiple_of(z_low * width, width), width)], w_ref, w_sem)
-    arriving.start()
     grad = jnp.sum(parts_ref[...].astype(F32), axis=0).astype(BF16)
     first = jnp.where(z_low == 0, mh_ref[rows, :width], mh_ref[rows, width:])
     second = jnp.where(z_low == 0, vh_ref[rows, :width], vh_ref[rows, width:])
     first_out, second_out = moments(first, second, grad.astype(F32))
-    arriving.wait()
-    new = stepped(w_ref[...].astype(F32), first_out, second_out)
+    weight = jnp.where(z_low == 0, wh_ref[rows, :width].astype(F32), wh_ref[rows, width:].astype(F32))
+    new = stepped(weight, first_out, second_out)
     for d in range(0, send_ref.shape[0], 2):
         send_ref[d + half] = grad
         send_ref[d + 1 - half] = new
 
 
-def final_kernel(side, me_ref, blocks_ref, w_in, mh_ref, vh_ref, *refs):
+def final_kernel(side, me_ref, blocks_ref, mh_ref, vh_ref, w_ref, *refs):
     half = me_ref[0] % 2
     core = (me_ref[0] // 2) % 2
     owner = core if side == 0 else 1 - core
@@ -351,23 +352,19 @@
     start = pl.multiple_of(owner * side_rows, side_rows)
     pending = []
     if side == 0:
-        m_hbm, v_hbm, new_hbm, first_hbm, second_hbm, w_next, m_next, v_next = refs[:8]
-        new_ref, first_ref, second_ref, w_ref, sem, other_sem, w_sem = refs[8:]
+        m_hbm, v_hbm, w_hbm, new_hbm, first_hbm, second_hbm, m_next, v_next, w_next = refs[:9]
+        new_ref, first_ref, second_ref, sem, other_sem, w_sem = refs[9:]
         other = pl.ds(pl.multiple_of((1 - owner) * side_rows, side_rows), side_rows)
         other_w = pl.ds(pl.multiple_of(half * owned + (1 - owner) * side_rows, side_rows), side_rows)
-        own_w = pl.ds(pl.multiple_of(half * owned + start, side_rows), side_rows)
-        near_w = copy(w_in.at[own_w], w_ref, w_sem.at[0])
-        near_w.start()
         pending = [
-            copy(w_in.at[other_w], w_next, w_sem.at[1]),
-            copy(m_hbm.at[other], m_next, w_sem.at[2]),
-            copy(v_hbm.at[other], v_next, w_sem.at[3]),
+            copy(m_hbm.at[other], m_next, w_sem.at[0]),
+            copy(v_hbm.at[other], v_next, w_sem.at[1]),
+            copy(w_hbm.at[other_w], w_next, w_sem.at[2]),
         ]
         for one in pending:
             one.start()
     else:
         new_hbm, first_hbm, second_hbm, new_ref, first_ref, second_ref, sem, other_sem = refs[3:]
-        w_ref = w_in
     sent = []
     for slot in range(slots // 2):
         peer = pl.ds(pl.multiple_of((1 - half) * owned + start + slot * block, block), block)
@@ -388,8 +385,7 @@
             first_out, second_out = moments(mh_ref[here, :], vh_ref[here, :], grad)
             first_ref[here, :] = first_out
             second_ref[here, :] = second_out
-            if side == 1:
-                new_ref[here, :] = stepped(w_ref[here, :].astype(F32), first_out, second_out)
+            new_ref[here, :] = stepped(w_ref[here, :].astype(F32), first_out, second_out)
         far = pl.ds(pl.multiple_of(start + chunk * rows, rows), rows)
         for i, (source, target) in enumerate([(first_ref, first_hbm), (second_ref, second_hbm)]):
             one = copy(source.at[pl.ds(chunk * rows, rows)], target.at[far], sem.at[chunk, i])
@@ -397,9 +393,6 @@
             sent.append(one)
 
     def second_part(chunk):
-        for slot in range(chunk * per, (chunk + 1) * per) if side == 0 else ():
-            here = slice(slot * block, (slot + 1) * block)
-            new_ref[here, :] = stepped(w_ref[here, :].astype(F32), first_ref[here, :], second_ref[here, :])
         mine = pl.ds(pl.multiple_of(half * owned + start + chunk * rows, rows), rows)
         one = copy(new_ref.at[pl.ds(chunk * rows, rows)], new_hbm.at[mine], sem.at[chunk, 2])
         one.start()
@@ -407,12 +400,7 @@
 
     for chunk in range(chunks):
         first_part(chunk)
-        if side == 1:
-            second_part(chunk)
-    if side == 0:
-        near_w.wait()
-        for chunk in range(chunks):
-            second_part(chunk)
+        second_part(chunk)
     for one in sent + pending:
         one.wait()
 
@@ -505,31 +493,30 @@
     return pl.pallas_call(
         input_kernel,
         in_specs=[SCALAR] + [FAR] * 4,
-        out_specs=[FAR, NEAR, NEAR],
+        out_specs=[FAR, NEAR, NEAR, NEAR],
         out_shape=[
             pltpu.HBM(shape, BF16),
-            pltpu.VMEM(owned, F32), pltpu.VMEM(owned, F32),
+            pltpu.VMEM(owned, F32), pltpu.VMEM(owned, F32), pltpu.VMEM(owned, BF16),
         ],
         scratch_shapes=[
             pltpu.VMEM(weight.shape, BF16), pltpu.VMEM(d_conv.shape, BF16), pltpu.VMEM(d_conv.shape, BF16),
-            DMA((3,)), DMA((2,)), DMA((frames, batch)), DMA((frames,)),
+            DMA((3,)), DMA((3,)), DMA((frames, batch)), DMA((frames,)),
         ],
         compiler_params=PARAMS,
         name="input_grad",
     )(me, *[remote(a) for a in (d_conv, weight, first, second)])
 
 
-def run_block(me, parts, weight, kept):
+def run_block(me, parts, kept):
     send = (32, *parts.shape[1:])
     return pl.pallas_call(
         block_kernel,
-        in_specs=[SCALAR, NEAR, FAR, NEAR, NEAR],
+        in_specs=[SCALAR] + [NEAR] * 4,
         out_specs=NEAR,
         out_shape=pltpu.VMEM(send, BF16),
-        scratch_shapes=[pltpu.VMEM(parts.shape[1:], BF16), DMA(())],
         compiler_params=PARAMS,
         name="owner_step",
-    )(me, local(parts), remote(weight), *[local(a) for a in kept])
+    )(me, local(parts), *[local(a) for a in kept])
 
 
 def run_near(me, blocks, weight, first, second, kept):
@@ -537,19 +524,19 @@
     half = (owned // 2, width)
     return pl.pallas_call(
         functools.partial(final_kernel, 0),
-        in_specs=[SCALAR, NEAR, FAR, NEAR, NEAR, FAR, FAR],
+        in_specs=[SCALAR] + [NEAR] * 4 + [FAR] * 3,
         out_specs=[FAR] * 3 + [NEAR] * 3,
         out_shape=[
             pltpu.HBM(weight.shape, BF16), pltpu.HBM(first.shape, F32), pltpu.HBM(first.shape, F32),
+            pltpu.VMEM(half, F32), pltpu.VMEM(half, F32), pltpu.VMEM(half, BF16),
+        ],
+        scratch_shapes=[
             pltpu.VMEM(half, BF16), pltpu.VMEM(half, F32), pltpu.VMEM(half, F32),
-        ],
-        scratch_shapes=[
-            pltpu.VMEM(half, BF16), pltpu.VMEM(half, F32), pltpu.VMEM(half, F32), pltpu.VMEM(half, BF16),
-            DMA((4, 3)), DMA((8, 2)), DMA((4,)),
+            DMA((4, 3)), DMA((8, 2)), DMA((3,)),
         ],
         compiler_params=PARAMS,
         name="final_near",
-    )(me, local(blocks), remote(weight), *[local(a) for a in kept], remote(first), remote(second))
+    )(me, *[local(a) for a in (blocks, *kept)], *[remote(a) for a in (first, second, weight)])
 
 
 def run_far(me, blocks, saved, carried):
@@ -598,7 +585,7 @@
     plane, kept = lax.optimization_barrier((plane, kept))
     column = jnp.sum(plane.astype(F32), axis=0).astype(BF16)
     tower = spread(jnp.broadcast_to(column, (lax.axis_size("zh"), *column.shape)), "zh")
-    near = spread(run_block(me, tower, conv_weight, kept), PLANE)
+    near = spread(run_block(me, tower, kept), PLANE)
     far = swapped(near)
     outs = run_near(me, near, conv_weight, first_moment, second_moment, kept)
     new_weight, first_out, second_out = run_far(me, far, outs[3:], outs[:3])

time: 102 us -> 101 us (level)
  no operation moved by 1% of the time
where the time goes in v6:
time: 101 us
  Pallas kernels  33.3 us (33%)
  starting transfers between devices  25.2 us (25%)
  blocking collectives  24.2 us (24%)
  waiting for transfers between devices  15.9 us (16%)
  other arithmetic  1.23 us (1%)
    all_to_all x2, blocking collectives, spread(): return lax.all_to_all(value, axes, 0, 0, tiled=True)  24.2 us
    all_to_all x2, starting transfers between devices, spread(): return lax.all_to_all(value, axes, 0, 0, tiled=True)  20 us
    all_to_all x2, waiting for transfers between devices, spread(): return lax.all_to_all(value, axes, 0, 0, tiled=True)  13.9 us
    pallas_call x1, Pallas kernels, run_forward(): pl.pallas_call(forward_kernel, in_specs=[SCALAR] + [FAR] * 7, out_specs=[...  8.94 us
    pallas_call x1, Pallas kernels, run_backward(): pl.pallas_call(functools.partial(backward_kernel, bits, clip_count, token...  8.15 us
    pallas_call x1, Pallas kernels, run_input(): pl.pallas_call(input_kernel, in_specs=[SCALAR] + [FAR] * 4, out_specs=[FA...  6.59 us
    ppermute x2, starting transfers between devices, swapped(): return lax.ppermute(value, 'core', [(0, 1), (1, 0)])  5.25 us
    pallas_call x1, Pallas kernels, run_window(): pl.pallas_call(window_kernel, in_specs=[FAR] + [NEAR] * 5, out_specs=[FAR...  5.23 us
  transfers between devices with their start and end apart: 4, of which 3 were waited for; matrix products, arithmetic and copies ran while one was open for 0% of the time, Pallas kernels for 14%

profile of v6, /device:TPU:1, one launch (start us, length us, event | category | flops | bytes accessed | tf_op | source)
XLA Modules:
  0.0 100.7 jit_solution(5391602513508852551)
XLA Ops:
  0.6 8.9 %forward.1 = (bf16[5,512,512]{2,1,0:T(8,128)(2,1)S(1)}, f32[5,24,512]{2,1,0:T(8,128)S(1)}, f32[5,8,512]{2,1,0:T(8,128)S(1)}, f32[24,128]{1,0:T(8,128)S(1)}, f32[...) custom-call(s32[1]{0:T(128)} %bitcast._.me_ref, bf16[2,5,256,512]{3,2,1,0:T(8,128)(2,1)} %x_hbm.3, ...), custom_call_target="tpu_custom_call" | custom-call | tf_op jit(solution)/shard_map/forward/pallas_call | solution.py:432
  9.6 15.7 %all-to-all-start = ((f32[256,1,128]{2,1,0:T(1,128)}), f32[256,1,128]{2,1,0:T(1,128)S(1)}, u32[]{:S(2)}, u32[]{:S(2)}) async-start(f32[256,1,128]{2,1,0:T(1,128)} %bitcast.6), calls=%async_computation | async-start | bytes 262144 | tf_op jit(solution)/shard_map/all_to_all | solution.py:559
  25.3 5.2 %window.1 = (bf16[5,512,512]{2,1,0:T(8,128)(2,1)}, bf16[512,2560]{1,0:T(8,128)(2,1)}, f32[5,3,24,512]{3,2,1,0:T(8,128)}) custom-call(bf16[2,5,256,512]{3,2,1,0:T(8,128)(2,1)} %x_hbm.3, bf16[5,512,512]{2,1,0:T(8,128)(2,1)S(1)} %get-tuple-element.35.h_ref, f32[5,24,512]{2,1,0:T(8,128)S(1)} %get-tuple-element.36.raw_ref, ...), custom_call_target="tpu_custom_call" | custom-call | tf_op jit(solution)/shard_map/window/pallas_call | solution.py:451
  30.5 7.7 %all-to-all-done = f32[256,1,128]{2,1,0:T(1,128)S(1)} async-done(((f32[256,1,128]{2,1,0:T(1,128)}), f32[256,1,128]{2,1,0:T(1,128)S(1)}, u32[]{:S(2)}, u32[]{:S(2)}) %all-to-all-start) | async-done | bytes 131104 | tf_op jit(solution)/shard_map/all_to_all | solution.py:559
  38.2 8.2 %backward.1 = (bf16[5,512,512]{2,1,0:T(8,128)(2,1)}, bf16[2,32,48,256]{3,2,1,0:T(8,128)(2,1)S(1)}, f32[1,1]{1,0:T(1,128)}) custom-call(s32[1]{0:T(128)} %bitcast._.me_ref, bf16[5,512,512]{2,1,0:T(8,128)(2,1)} %get-tuple-element.40.h_hbm, bf16[512,2560]{1,0:T(8,128)(2,1)} %get-tuple-element.41.xt_hbm, f32[5,3,24,512]{3,2,1,0:T(8,128)} %get-tuple-element.42.rows_hbm, ...), custom_call_target="tpu_custom_call" | custom-call | tf_op jit(solution)/shard_map/backward/pallas_call | solution.py:471
  46.4 0.1 slice_bitcast_fusion
  46.5 0.6 collective-permute-start
  47.1 1.9 %collective-permute-done = bf16[32,48,256]{2,1,0:T(8,128)(2,1)S(1)} collective-permute-done((bf16[32,48,256]{2,1,0:T(8,128)(2,1)S(1)}, bf16[32,48,256]{2,1,0:T(8,128)(2,1)S(1)}, u32[]{:S(2)}, u32[]{:S(2)}) %collective-permute-start) | collective-permute-done | bytes 786464 | tf_op jit(solution)/shard_map/ppermute | solution.py:563
  49.0 1.1 %fusion = bf16[32,48,256]{2,1,0:T(8,128)(2,1)} fusion(bf16[32,48,256]{2,1,0:T(8,128)(2,1)S(1)} %collective-permute-done, bf16[2,32,48,256]{3,2,1,0:T(8,128)(2,1)S(1)} %get-tuple-element.45), kind=kLoop, calls=%fused_computation.1 | loop fusion | flops 1572864 | bytes 2359296 | tf_op jit(solution)/shard_map/convert_element_type | solution.py:582
  50.1 4.3 %all-to-all-start.1 = ((bf16[32,48,256]{2,1,0:T(8,128)(2,1)}), bf16[32,48,256]{2,1,0:T(8,128)(2,1)S(1)}, u32[]{:S(2)}, u32[]{:S(2)}) async-start(bf16[32,48,256]{2,1,0:T(8,128)(2,1)} %fusion), calls=%async_computation.1 | async-start | bytes 1572864 | tf_op jit(solution)/shard_map/all_to_all | solution.py:559
  54.4 6.6 %input_grad.1 = (bf16[2,5,256,512]{3,2,1,0:T(8,128)(2,1)}, f32[384,512]{1,0:T(8,128)S(1)}, f32[384,512]{1,0:T(8,128)S(1)}, bf16[384,512]{1,0:T(8,128)(2,1)S(1)}) custom-call(s32[1]{0:T(128)} %bitcast._.me_ref, bf16[5,512,512]{2,1,0:T(8,128)(2,1)} %get-tuple-element.46.d_hbm, bf16[1536,512]{1,0:T(8,128)(2,1)} %refs_2_.1, f32[768,512]{1,0:T(8,128)} %refs_0_.1, ...), custom_call_target="tpu_custom_call" | custom-call | tf_op jit(solution)/shard_map/input_grad/pallas_call | solution.py:493
  61.0 6.2 %all-to-all-done.1 = bf16[32,48,256]{2,1,0:T(8,128)(2,1)S(1)} async-done(((bf16[32,48,256]{2,1,0:T(8,128)(2,1)}), bf16[32,48,256]{2,1,0:T(8,128)(2,1)S(1)}, u32[]{:S(2)}, u32[]{:S(2)}) %all-to-all-start.1) | async-done | bytes 786464 | tf_op jit(solution)/shard_map/all_to_all | solution.py:559
  67.2 0.1 reduce_sum.12
  67.3 9.6 %all_to_all.26.parts_ref = bf16[4,48,256]{2,1,0:T(8,128)(2,1)S(1)} all-to-all(bf16[4,48,256]{2,1,0:T(8,128)(2,1)S(1)} %broadcast_in_dim.11), channel_id=1, replica_groups=mesh['x'=4,'zh'=4,'zl'=2,'yh'=2,'core'=2,'yl'=2] {'zh'}, dimensions={0} | all-to-all | bytes 196608 | tf_op jit(solution)/shard_map/all_to_all | solution.py:559
  76.9 0.1 owner_step.1
  77.0 14.6 %all_to_all.27.blocks_ref = bf16[32,48,256]{2,1,0:T(8,128)(2,1)S(1)} all-to-all(bf16[32,48,256]{2,1,0:T(8,128)(2,1)S(1)} %owner_step.1), channel_id=1, replica_groups=mesh['x'=4,'zh'=4,'zl'=2,'yh'=2,'core'=2,'yl'=2] {'x','zl','yh','yl'}, dimensions={0} | all-to-all | bytes 1572864 | tf_op jit(solution)/shard_map/all_to_all | solution.py:559
  91.6 4.7 %collective-permute-start.1 = (bf16[32,48,256]{2,1,0:T(8,128)(2,1)S(1)}, bf16[32,48,256]{2,1,0:T(8,128)(2,1)S(1)}, u32[]{:S(2)}, u32[]{:S(2)}) collective-permute-start(bf16[32,48,256]{2,1,0:T(8,128)(2,1)S(1)} %all_to_all.27.blocks_ref), channel_id=1, source_target_pairs={{0,2},{2,0},{1,3},{3,1},{4,6},{6,4},{5,7},{7,5},{8,10},{10,8},{9,1... | collective-permute-start | bytes 2359304 | tf_op jit(solution)/shard_map/ppermute | solution.py:563
  96.3 2.6 %final_near.1 = (bf16[1536,512]{1,0:T(8,128)(2,1)}, f32[768,512]{1,0:T(8,128)}, f32[768,512]{1,0:T(8,128)}, f32[384,512]{1,0:T(8,128)S(1)}, f32[384,512]{1,0:T(8,128)S(1)}, /*index=5*/bf16[384,512]{1,0:T(8,128)(2,1)S(1)}) custom-call(s32[1]{0:T(128)} %bitcast._.me_ref, bf16[32,48,256]{2,1,0:T(8,128)(2,1)S(1)} %all_to_all.27.blocks_ref, ...), custom_call_target="tpu_custom_call" | custom-call | tf_op jit(solution)/shard_map/final_near/pallas_call | solution.py:525
  98.9 0.0 collective-permute-done.1.blocks_ref
  98.9 1.6 %final_far.1 = (bf16[1536,512]{1,0:T(8,128)(2,1)}, f32[768,512]{1,0:T(8,128)}, f32[768,512]{1,0:T(8,128)}) custom-call(s32[1]{0:T(128)} %bitcast._.me_ref, bf16[32,48,256]{2,1,0:T(8,128)(2,1)S(1)} %collective-permute-done.1.blocks_ref, f32[384,512]{1,0:T(8,128)S(1)} %get-tuple-element.54.mh_ref, ...), custom_call_target="tpu_custom_call", output_to_operand_aliasing={{0}: (5, {}), {1}: (6, {}), {2}: (7, {})} | custom-call | tf_op jit(solution)/shard_map/final_far/pallas_call | solution.py:544
  (1 shorter events, 0.0 us)
Async XLA Ops:
  9.6 28.6 %all-to-all-start = ((f32[256,1,128]{2,1,0:T(1,128)}), f32[256,1,128]{2,1,0:T(1,128)S(1)}, u32[]{:S(2)}, u32[]{:S(2)}) async-start(f32[256,1,128]{2,1,0:T(1,128)} %bitcast.6), calls=%async_computation | async-start | bytes 262144 | tf_op jit(solution)/shard_map/all_to_all | solution.py:559
  46.5 2.5 %collective-permute-start = (bf16[32,48,256]{2,1,0:T(8,128)(2,1)S(1)}, bf16[32,48,256]{2,1,0:T(8,128)(2,1)S(1)}, u32[]{:S(2)}, u32[]{:S(2)}) collective-permute-start(bf16[32,48,256]{2,1,0:T(8,128)(2,1)S(1)} %slice_bitcast_fusion), channel_id=1, source_target_pairs={{0,2},{2,0},{1,3},{3,1},{4,6},{6,4},{5,7},{7,5},{8,10},{10,8},{9,1... | collective-permute-start | bytes 2359304 | tf_op jit(solution)/shard_map/ppermute | solution.py:563
  50.1 17.1 %all-to-all-start.1 = ((bf16[32,48,256]{2,1,0:T(8,128)(2,1)}), bf16[32,48,256]{2,1,0:T(8,128)(2,1)S(1)}, u32[]{:S(2)}, u32[]{:S(2)}) async-start(bf16[32,48,256]{2,1,0:T(8,128)(2,1)} %fusion), calls=%async_computation.1 | async-start | bytes 1572864 | tf_op jit(solution)/shard_map/all_to_all | solution.py:559
  91.6 7.3 %collective-permute-start.1 = (bf16[32,48,256]{2,1,0:T(8,128)(2,1)S(1)}, bf16[32,48,256]{2,1,0:T(8,128)(2,1)S(1)}, u32[]{:S(2)}, u32[]{:S(2)}) collective-permute-start(bf16[32,48,256]{2,1,0:T(8,128)(2,1)S(1)} %all_to_all.27.blocks_ref), channel_id=1, source_target_pairs={{0,2},{2,0},{1,3},{3,1},{4,6},{6,4},{5,7},{7,5},{8,10},{10,8},{9,1... | collective-permute-start | bytes 2359304 | tf_op jit(solution)/shard_map/ppermute | solution.py:563
